TPU v7x, 32 devices: a whole 2x2x4 slice. The times are simulated.
32 devices in a mesh: fsdp: 4 (over y, x), expert: 8 (over z, core).
Axes of the slice: x: 2, y: 2, z: 4, core: 2. Of those that a mesh axis runs over, the one named last changes fastest.
Arguments:
- inputs: bfloat16 [8, 512, 2048], P('expert', 'fsdp'), may hold values from -6 to 6
- teacher: bfloat16 [8, 512, 2048], P('expert', 'fsdp'), may hold values from -6 to 6
- lengths: int32 [16], replicated, may hold values from 1 to 448, as said below
- deal_order: int32 [16], replicated, may hold values from 0 to 15, as said below
- routes: int32 [8, 512, 4], P('expert', 'fsdp'), may hold values from 0 to 7, all different within a row; in each aligned block of 128 rows (0 to 127, 128 to 255, ..., all dimensions but the last counted through in order) at most 96 rows name the same one
- route_weights: float32 [8, 512, 4], P('expert', 'fsdp'), may hold values from 0.4 to 1.2
- norm_gains: bfloat16 [2, 2048], P(None, ('fsdp', 'expert')), may hold values from 0.5 to 1.5
- mixer_weights: bfloat16 [2048, 4, 2048], P('expert', None, 'fsdp')
- shared_weights: bfloat16 [2048, 3, 5632], P('expert', None, 'fsdp')
- shared_gate: bfloat16 [2048], P(('fsdp', 'expert')), may hold values from -0.125 to 0.125
- expert_gate: bfloat16 [8, 2048, 1408], P('expert', 'fsdp'), may hold values from -0.125 to 0.125
- expert_up: bfloat16 [8, 2048, 1408], P('expert', 'fsdp'), may hold values from -0.125 to 0.125
- expert_down: bfloat16 [8, 1408, 2048], P('expert', 'fsdp'), may hold values from -0.15625 to 0.15625
Outputs:
- out_block: bfloat16 [8, 512, 2048], P('expert', 'fsdp')
- grad_input: float32 [8, 512, 2048], P('expert', 'fsdp')
- grad_gains: float32 [2, 2048], P(None, ('fsdp', 'expert'))
- grad_mixer: float32 [2048, 4, 2048], P('expert', None, 'fsdp')
- grad_shared: float32 [2048, 3, 5632], P('expert', None, 'fsdp')
- grad_shared_gate: float32 [2048], P(('fsdp', 'expert'))
- grad_expert_gate: float32 [8, 2048, 1408], P('expert', 'fsdp')
- grad_expert_up: float32 [8, 2048, 1408], P('expert', 'fsdp')
- grad_expert_down: float32 [8, 1408, 2048], P('expert', 'fsdp')
Inputs may be any that keep to these rules, and one draw needn't show every extreme that they name: `routes`: A token's 4 experts differ; the 128 tokens of one device name each expert at most 96 times, and some device names some expert exactly 96 times. `lengths`: the two sequences that one row holds have at most 512 tokens together; some sequence has exactly 448 tokens. A permutation of the 16 sequences: row g holds sequence deal_order[2g] and then deal_order[2g+1], packed from its start; the rest of the row is padding.
All inputs are finite; a program needn't handle non-finite values.
Results may differ from a plain program's by a relative error of at most 0.02.
Values may be sent and summed in bfloat16 or wider, within the bound.
A program may use at most 256 MiB of HBM per device.

v0:
```python
import jax
import jax.numpy as jnp
from jax import lax
from jax.sharding import PartitionSpec as P

HD = 128
EFF = 1408
TOP = 4


THETA = 1000000.0
EPSILON = 1e-06
NEG_LARGE = -1e30


def rope_tables(positions, head_size):
    half_size = head_size // 2
    inverse = THETA ** (-(jnp.arange(half_size, dtype=jnp.float32) * 2.0) / head_size)
    angles = positions.astype(jnp.float32)[:, None] * inverse[None, :]
    cosine_table = jnp.concatenate([jnp.cos(angles), jnp.cos(angles)], axis=1)[:, None, :]
    sine_table = jnp.concatenate([jnp.sin(angles), jnp.sin(angles)], axis=1)[:, None, :]
    return (cosine_table, sine_table)


def rotary(values, cosine_table, sine_table):
    half_size = values.shape[-1] // 2
    turned = jnp.concatenate([-values[..., half_size:], values[..., :half_size]], axis=-1)
    return values * cosine_table + turned * sine_table


def rotate_back(incoming, cosine_table, sine_table):
    half_size = incoming.shape[-1] // 2
    scaled = incoming * sine_table
    turned = jnp.concatenate([scaled[..., half_size:], -scaled[..., :half_size]], axis=-1)
    return incoming * cosine_table + turned


def norm_back(incoming, values, scale_rows, gain_row):
    unit_rows = values * scale_rows[:, None]
    gain_grad = jnp.sum(incoming * unit_rows, axis=0)
    dunit = incoming * gain_row[None, :]
    back_rows = scale_rows[:, None] * (
        dunit - unit_rows * jnp.mean(dunit * unit_rows, axis=1, keepdims=True)
    )
    return (back_rows, gain_grad)


def score_block(queries, key_heads, allowed):
    raw_scores = jnp.einsum("qhd,khd->hqk", queries, key_heads, preferred_element_type=jnp.float32)
    return jnp.where(allowed[None], raw_scores * queries.shape[2] ** (-0.5), NEG_LARGE)


def row_tokens(values):
    return lax.all_gather(values, "fsdp", axis=0, tiled=True)


def sliced_product(form, left, right):
    return lax.psum_scatter(
        jnp.einsum(form, left, right, preferred_element_type=jnp.float32).astype(jnp.bfloat16),
        "fsdp",
        scatter_dimension=0,
        tiled=True,
    ).astype(jnp.float32)


def on_device(
    inputs,
    teacher,
    lengths,
    deal_order,
    routes,
    route_weights,
    norm_gains,
    mixer_weights,
    shared_weights,
    shared_gate,
    expert_gate,
    expert_up,
    expert_down,
):
    tokens_dev = inputs.shape[1]
    model_width = inputs.shape[2]
    groups = lax.axis_size("expert")
    row_len = tokens_dev * lax.axis_size("fsdp")
    capacity = 3 * tokens_dev * TOP // (2 * groups)
    total_tokens = row_len * groups
    heads_local = mixer_weights.shape[2] // HD
    columns = mixer_weights.shape[2]
    fsdp_index = lax.axis_index("fsdp")
    group_index = lax.axis_index("expert")
    first_len = lengths[deal_order[2 * group_index]]
    second_len = lengths[deal_order[2 * group_index + 1]]
    row_places = jnp.arange(row_len, dtype=jnp.int32)
    row_segment = (row_places >= first_len).astype(jnp.int32) + (
        row_places >= first_len + second_len
    ).astype(jnp.int32)
    row_position = (
        row_places
        - first_len * (row_segment >= 1).astype(jnp.int32)
        - second_len * (row_segment >= 2).astype(jnp.int32)
    )
    own_segment = lax.dynamic_slice_in_dim(row_segment, fsdp_index * tokens_dev, tokens_dev)
    allowed = (row_segment[:, None] == row_segment[None, :]) & (
        row_places[None, :] <= row_places[:, None]
    )
    cosine_table, sine_table = rope_tables(row_position, HD)
    gains_full, vector_full = (
        lax.all_gather(norm_gains, ("fsdp", "expert"), axis=1, tiled=True),
        lax.all_gather(shared_gate, ("fsdp", "expert"), axis=0, tiled=True),
    )
    mixer_local, shared_local = (
        lax.all_gather(mixer_weights, "expert", axis=0, tiled=True),
        lax.all_gather(shared_weights, "expert", axis=0, tiled=True),
    )
    gate_full, up_full, down_full = (
        lax.all_gather(expert_gate, "fsdp", axis=1, tiled=True),
        lax.all_gather(expert_up, "fsdp", axis=1, tiled=True),
        lax.all_gather(expert_down, "fsdp", axis=1, tiled=True),
    )
    gate_rows = gate_full[0]
    up_rows = up_full[0]
    down_rows = down_full[0]
    flat_inputs = inputs[0].astype(jnp.float32)
    first_gain = gains_full[0].astype(jnp.float32)
    second_gain = gains_full[1].astype(jnp.float32)
    first_scale = lax.rsqrt(jnp.mean(flat_inputs * flat_inputs, axis=1) + EPSILON)
    normed = (flat_inputs * first_scale[:, None] * first_gain[None, :]).astype(jnp.bfloat16)
    row_normed = row_tokens(normed)
    projected = jnp.einsum(
        "td,dke->tke", row_normed, mixer_local[:, :3], preferred_element_type=jnp.float32
    )
    queries = rotary(
        projected[:, 0].reshape(row_len, heads_local, HD), cosine_table, sine_table
    ).astype(jnp.bfloat16)
    key_heads = rotary(
        projected[:, 1].reshape(row_len, heads_local, HD), cosine_table, sine_table
    ).astype(jnp.bfloat16)
    value_heads = projected[:, 2].astype(jnp.bfloat16).reshape(row_len, heads_local, HD)
    scores = score_block(queries, key_heads, allowed)
    top_score = jnp.max(scores, axis=2, keepdims=True)
    shifted = jnp.exp(scores - top_score)
    row_total = jnp.sum(shifted, axis=2, keepdims=True)
    probabilities = shifted / row_total
    log_total = top_score + jnp.log(row_total)
    context = jnp.einsum(
        "hqk,khd->qhd",
        probabilities.astype(jnp.bfloat16),
        value_heads,
        preferred_element_type=jnp.float32,
    )
    context = context.reshape(row_len, columns).astype(jnp.bfloat16)
    attn_out = sliced_product("tc,dc->td", context, mixer_local[:, 3])
    residual = flat_inputs + attn_out
    second_scale = lax.rsqrt(jnp.mean(residual * residual, axis=1) + EPSILON)
    mixed_in = (residual * second_scale[:, None] * second_gain[None, :]).astype(jnp.bfloat16)
    row_mixed = row_tokens(mixed_in)
    shared_pre = jnp.einsum(
        "td,dkf->tkf", row_mixed, shared_local[:, :2], preferred_element_type=jnp.float32
    )
    shared_hidden = (jax.nn.silu(shared_pre[:, 0]) * shared_pre[:, 1]).astype(jnp.bfloat16)
    shared_out = sliced_product("tf,df->td", shared_hidden, shared_local[:, 2])
    gate_value = jax.nn.sigmoid(jnp.dot(mixed_in, vector_full, preferred_element_type=jnp.float32))
    chosen = routes[0].reshape(tokens_dev * TOP)
    one_hot = (chosen[:, None] == jnp.arange(groups, dtype=jnp.int32)[None, :]).astype(jnp.int32)
    before = jnp.cumsum(one_hot, axis=0) - one_hot
    slots = chosen * capacity + jnp.sum(before * one_hot, axis=1)
    outgoing = (
        jnp.zeros((groups * capacity, model_width), jnp.bfloat16)
        .at[slots]
        .set(jnp.repeat(mixed_in, TOP, axis=0))
    )
    outgoing = outgoing.reshape(groups, capacity, model_width)
    arrived_block = lax.all_to_all(outgoing, "expert", split_axis=0, concat_axis=0, tiled=True)
    sources = arrived_block.shape[0]
    slot_count = arrived_block.shape[1]
    flat_rows = arrived_block.reshape(sources * slot_count, model_width)
    gate_pre = jnp.dot(flat_rows, gate_rows, preferred_element_type=jnp.float32)
    up_pre = jnp.dot(flat_rows, up_rows, preferred_element_type=jnp.float32)
    hidden = (jax.nn.silu(gate_pre) * up_pre).astype(jnp.bfloat16)
    result = jnp.dot(hidden, down_rows, preferred_element_type=jnp.float32).astype(jnp.bfloat16)
    returned_rows = lax.all_to_all(
        result.reshape(sources, slot_count, model_width),
        "expert",
        split_axis=0,
        concat_axis=0,
        tiled=True,
    )
    gate_kept = gate_pre.reshape(sources, slot_count, EFF)
    up_kept = up_pre.reshape(sources, slot_count, EFF)
    weights_route = route_weights[0]
    expert_back = returned_rows.reshape(groups * capacity, model_width)[slots].reshape(
        tokens_dev, TOP, model_width
    )
    routed_sum = jnp.sum(weights_route[:, :, None] * expert_back.astype(jnp.float32), axis=1)
    block_total = residual + gate_value[:, None] * shared_out + routed_sum
    out_block = block_total.astype(jnp.bfloat16)[None]
    valid_mask = (own_segment < 2).astype(jnp.float32)
    valid_count = jnp.sum(lengths).astype(jnp.float32)
    dtotal = (
        total_tokens
        / valid_count
        * valid_mask[:, None]
        * (block_total - teacher[0].astype(jnp.float32))
    )
    mixer_back, shared_back = (
        lax.all_gather(mixer_weights, "expert", axis=0, tiled=True),
        lax.all_gather(shared_weights, "expert", axis=0, tiled=True),
    )
    dexpert = (
        (weights_route[:, :, None] * dtotal[:, None, :])
        .astype(jnp.bfloat16)
        .reshape(tokens_dev * TOP, model_width)
    )
    dsend = jnp.zeros((groups * capacity, model_width), jnp.bfloat16).at[slots].set(dexpert)
    dreceived = lax.all_to_all(
        dsend.reshape(groups, capacity, model_width),
        "expert",
        split_axis=0,
        concat_axis=0,
        tiled=True,
    )
    dreceived = dreceived.reshape(groups * capacity, model_width)
    gate_flat = gate_kept.reshape(groups * capacity, EFF)
    up_flat = up_kept.reshape(groups * capacity, EFF)
    gate_sigmoid = jax.nn.sigmoid(gate_flat)
    activated = gate_flat * gate_sigmoid
    hidden_again = (activated * up_flat).astype(jnp.bfloat16)
    dhidden = jnp.einsum("rd,fd->rf", dreceived, down_rows, preferred_element_type=jnp.float32)
    dgate = (dhidden * up_flat * gate_sigmoid * (1.0 + gate_flat * (1.0 - gate_sigmoid))).astype(
        jnp.bfloat16
    )
    dup_rows = (dhidden * activated).astype(jnp.bfloat16)
    dreturn = (
        jnp.einsum("rf,df->rd", dgate, gate_rows, preferred_element_type=jnp.float32)
        + jnp.einsum("rf,df->rd", dup_rows, up_rows, preferred_element_type=jnp.float32)
    ).astype(jnp.bfloat16)
    dx_back = lax.all_to_all(
        dreturn.reshape(groups, capacity, model_width),
        "expert",
        split_axis=0,
        concat_axis=0,
        tiled=True,
    )
    arrived_rows = arrived_block.reshape(groups * capacity, model_width)
    gate_term = jnp.einsum("rd,rf->df", arrived_rows, dgate, preferred_element_type=jnp.float32)
    up_term = jnp.einsum("rd,rf->df", arrived_rows, dup_rows, preferred_element_type=jnp.float32)
    down_term = jnp.einsum("rf,rd->fd", hidden_again, dreceived, preferred_element_type=jnp.float32)
    grad_expert_gate, grad_expert_up, grad_expert_down = (
        lax.psum_scatter(
            gate_term[None].astype(jnp.bfloat16), "fsdp", scatter_dimension=1, tiled=True
        ).astype(jnp.float32),
        lax.psum_scatter(
            up_term[None].astype(jnp.bfloat16), "fsdp", scatter_dimension=1, tiled=True
        ).astype(jnp.float32),
        lax.psum_scatter(
            down_term[None].astype(jnp.bfloat16), "fsdp", scatter_dimension=1, tiled=True
        ).astype(jnp.float32),
    )
    from_experts = dx_back.reshape(groups * capacity, model_width)[slots].reshape(
        tokens_dev, TOP, model_width
    )
    from_experts = jnp.sum(from_experts.astype(jnp.float32), axis=1)
    dshared_out = (gate_value[:, None] * dtotal).astype(jnp.bfloat16)
    dlogit = jnp.sum(dtotal * shared_out, axis=1) * gate_value * (1.0 - gate_value)
    row_dout = row_tokens(dshared_out)
    shared_gate_pre = shared_pre[:, 0]
    shared_up_pre = shared_pre[:, 1]
    shared_sigmoid = jax.nn.sigmoid(shared_gate_pre)
    dshared_hidden = jnp.einsum(
        "td,df->tf", row_dout, shared_back[:, 2], preferred_element_type=jnp.float32
    )
    dshared_pre = jnp.stack(
        [
            dshared_hidden
            * shared_up_pre
            * shared_sigmoid
            * (1.0 + shared_gate_pre * (1.0 - shared_sigmoid)),
            dshared_hidden * shared_gate_pre * shared_sigmoid,
        ],
        axis=1,
    ).astype(jnp.bfloat16)
    dmixed = (
        sliced_product("tkf,dkf->td", dshared_pre, shared_back[:, :2])
        + dlogit[:, None] * vector_full.astype(jnp.float32)[None, :]
        + from_experts
    )
    shared_term = jnp.concatenate(
        [
            jnp.einsum("td,tkf->dkf", row_mixed, dshared_pre, preferred_element_type=jnp.float32),
            jnp.einsum("td,tf->df", row_dout, shared_hidden, preferred_element_type=jnp.float32)[
                :, None, :
            ],
        ],
        axis=1,
    )
    vector_term = jnp.dot(dlogit, mixed_in.astype(jnp.float32), precision=lax.Precision.HIGHEST)
    dresidual_norm, second_gain_grad = norm_back(dmixed, residual, second_scale, second_gain)
    dresidual = dtotal + dresidual_norm
    dattn = dresidual.astype(jnp.bfloat16)
    row_dattn = row_tokens(dattn)
    dcontext = jnp.einsum(
        "td,dc->tc", row_dattn, mixer_back[:, 3], preferred_element_type=jnp.float32
    )
    dcontext = dcontext.astype(jnp.bfloat16).reshape(row_len, heads_local, HD)
    scores_again = score_block(queries, key_heads, allowed)
    probabilities_again = jnp.exp(scores_again - log_total)
    dprobs = jnp.einsum("qhd,khd->hqk", dcontext, value_heads, preferred_element_type=jnp.float32)
    delta_rows = jnp.sum(probabilities_again * dprobs, axis=2, keepdims=True)
    dscores = (probabilities_again * (dprobs - delta_rows)).astype(jnp.bfloat16)
    score_factor = HD ** (-0.5)
    dqueries = (
        jnp.einsum("hqk,khd->qhd", dscores, key_heads, preferred_element_type=jnp.float32)
        * score_factor
    )
    dkeys = (
        jnp.einsum("hqk,qhd->khd", dscores, queries, preferred_element_type=jnp.float32)
        * score_factor
    )
    dvalues = jnp.einsum(
        "hqk,qhd->khd",
        probabilities_again.astype(jnp.bfloat16),
        dcontext,
        preferred_element_type=jnp.float32,
    )
    dprojected = jnp.stack(
        [
            rotate_back(dqueries, cosine_table, sine_table).reshape(row_len, columns),
            rotate_back(dkeys, cosine_table, sine_table).reshape(row_len, columns),
            dvalues.reshape(row_len, columns),
        ],
        axis=1,
    ).astype(jnp.bfloat16)
    dnormed = sliced_product("tke,dke->td", dprojected, mixer_back[:, :3])
    dflat, first_gain_grad = norm_back(dnormed, flat_inputs, first_scale, first_gain)
    grad_input = (dresidual + dflat)[None]
    mixer_term = jnp.concatenate(
        [
            jnp.einsum("td,tke->dke", row_normed, dprojected, preferred_element_type=jnp.float32),
            jnp.einsum("td,tc->dc", row_dattn, context, preferred_element_type=jnp.float32)[
                :, None, :
            ],
        ],
        axis=1,
    )
    grad_mixer, grad_shared = (
        lax.psum_scatter(
            mixer_term.astype(jnp.bfloat16), "expert", scatter_dimension=0, tiled=True
        ).astype(jnp.float32),
        lax.psum_scatter(
            shared_term.astype(jnp.bfloat16), "expert", scatter_dimension=0, tiled=True
        ).astype(jnp.float32),
    )
    gains_term = jnp.stack([first_gain_grad, second_gain_grad], axis=0)
    grad_gains, grad_shared_gate = (
        lax.psum_scatter(gains_term, ("fsdp", "expert"), scatter_dimension=1, tiled=True),
        lax.psum_scatter(vector_term, ("fsdp", "expert"), scatter_dimension=0, tiled=True),
    )
    return (
        out_block,
        grad_input,
        grad_gains,
        grad_mixer,
        grad_shared,
        grad_shared_gate,
        grad_expert_gate,
        grad_expert_up,
        grad_expert_down,
    )


def solution(mesh):
    in_specs = (
        P("expert", "fsdp", None),
        P("expert", "fsdp", None),
        P(),
        P(),
        P("expert", "fsdp", None),
        P("expert", "fsdp", None),
        P(None, ("fsdp", "expert")),
        P("expert", None, "fsdp"),
        P("expert", None, "fsdp"),
        P(("fsdp", "expert")),
        P("expert", "fsdp", None),
        P("expert", "fsdp", None),
        P("expert", "fsdp", None),
    )
    out_specs = (
        P("expert", "fsdp", None),
        P("expert", "fsdp", None),
        P(None, ("fsdp", "expert")),
        P("expert", None, "fsdp"),
        P("expert", None, "fsdp"),
        P(("fsdp", "expert")),
        P("expert", "fsdp", None),
        P("expert", "fsdp", None),
        P("expert", "fsdp", None),
    )
    return jax.shard_map(
        on_device, mesh=mesh, in_specs=in_specs, out_specs=out_specs, check_vma=False
    )
```

profile of v0, /device:TPU:0, one launch (start us, length us, event | category | flops | bytes accessed | tf_op | source)
XLA Modules:
  0.0 1652.0 jit_solution(13765754366420022365)
XLA Ops:
  7.2 43.5 %all-gather = bf16[32,64,2]{1,2,0:T(2,128)(2,1)S(1)} all-gather(bf16[1,64,2]{1,2,0:T(2,128)(2,1)} %bitcast.277), channel_id=1, replica_groups=mesh['fsdp'=4,'expert'=8] {'fsdp','expert'}, dimensions={0}, use_global_device_ids=true | all-gather | bytes 8448 | tf_op jit(solution)/shard_map/all_gather | solution.py:108
  67.2 19.0 %all-gather.11.cloned.1.call-done = bf16[512,2048]{1,0:T(8,128)(2,1)} async-done(((bf16[128,2048]{1,0:T(8,128)(2,1)}), bf16[512,2048]{1,0:T(8,128)(2,1)}) %all-gather.11.cloned.1.call-update) | async-done | bytes 2097168 | tf_op jit(solution)/shard_map/all_gather | solution.py:54
  86.2 84.7 %all-gather.13.cloned.1.call-done = bf16[2048,4,512]{0,2,1:T(8,128)(2,1)} async-done(((bf16[256,4,512]{0,2,1:T(8,128)(2,1)}), bf16[2048,4,512]{0,2,1:T(8,128)(2,1)}) %all-gather.13.cloned.1.call-update) | async-done | bytes 8388624 | tf_op jit(solution)/shard_map/all_gather | solution.py:112
  170.9 6.2 fusion.22
  182.2 4.2 convolution_convert_fusion.7
  188.2 31.7 %reduce-scatter.13.cloned.1.call-done = bf16[128,2048]{1,0:T(8,128)(2,1)} async-done(((bf16[512,2048]{1,0:T(8,128)(2,1)}), bf16[128,2048]{1,0:T(8,128)(2,1)}) %reduce-scatter.13.cloned.1.call-update) | async-done | bytes 524304 | tf_op jit(solution)/shard_map/reduce_scatter | solution.py:58
  229.3 6.9 scatter_custom_fusion
  236.2 4.7 all-to-all-start
  240.9 46.5 %all-gather.19.cloned.1.call-done = bf16[1,2048,1408]{2,1,0:T(8,128)(2,1)} async-done(((bf16[1,512,1408]{2,1,0:T(8,128)(2,1)}), bf16[1,2048,1408]{2,1,0:T(8,128)(2,1)}) %all-gather.19.cloned.1.call-update) | async-done | bytes 5767184 | tf_op jit(solution)/shard_map/all_gather | solution.py:116
  287.4 25.0 %all-to-all-done = bf16[8,96,2048]{2,1,0:T(8,128)(2,1)S(1)} async-done(((bf16[8,96,2048]{2,1,0:T(8,128)(2,1)}), bf16[8,96,2048]{2,1,0:T(8,128)(2,1)S(1)}, u32[]{:S(2)}, u32[]{:S(2)}) %all-to-all-start) | async-done | bytes 3145760 | tf_op jit(solution)/shard_map/all_to_all | solution.py:173
  312.4 10.4 fusion.18
  322.7 32.0 %all-gather.21.cloned.1.call-done = bf16[1,2048,1408]{2,1,0:T(8,128)(2,1)} async-done(((bf16[1,512,1408]{2,1,0:T(8,128)(2,1)}), bf16[1,2048,1408]{2,1,0:T(8,128)(2,1)}) %all-gather.21.cloned.1.call-update) | async-done | bytes 5767184 | tf_op jit(solution)/shard_map/all_gather | solution.py:117
  354.7 10.3 multiply_convert_fusion.2
  365.0 57.1 %all-gather.23.cloned.1.call-done = bf16[1,1408,2048]{2,1,0:T(8,128)(2,1)} async-done(((bf16[1,352,2048]{2,1,0:T(8,128)(2,1)}), bf16[1,1408,2048]{2,1,0:T(8,128)(2,1)}) %all-gather.23.cloned.1.call-update) | async-done | bytes 5767184 | tf_op jit(solution)/shard_map/all_gather | solution.py:118
  422.1 8.9 fusion.28
  431.0 4.6 all-to-all-start.1
  435.7 23.5 %all-gather.15.cloned.1.call-done = bf16[512,2048]{1,0:T(8,128)(2,1)} async-done(((bf16[128,2048]{1,0:T(8,128)(2,1)}), bf16[512,2048]{1,0:T(8,128)(2,1)}) %all-gather.15.cloned.1.call-update) | async-done | bytes 2097168 | tf_op jit(solution)/shard_map/all_gather | solution.py:54
  459.2 189.1 %all-gather.17.cloned.1.call-done = bf16[2048,3,1408]{2,0,1:T(8,128)(2,1)} async-done(((bf16[256,3,1408]{2,0,1:T(8,128)(2,1)}), bf16[2048,3,1408]{2,0,1:T(8,128)(2,1)}) %all-gather.17.cloned.1.call-update) | async-done | bytes 17301520 | tf_op jit(solution)/shard_map/all_gather | solution.py:113
  648.3 10.1 fusion.2
  661.0 7.3 fusion.38
  669.1 37.5 %all-reduce = bf16[2048]{0:T(1024)(128)(2,1)S(1)} all-reduce(bf16[2048]{0:T(1024)(128)(2,1)S(1)} %dynamic-update-slice), channel_id=1, replica_groups=mesh['fsdp'=4,'expert'=8] {'fsdp','expert'}, use_global_device_ids=true, to_apply=%add | all-reduce | flops 2048 | bytes 8192
  709.0 3.3 gather_fusion
  712.3 4.8 reshape.246
  717.1 5.5 multiply_reduce_fusion.1
  726.1 3.2 mul.438
  729.3 5.3 mul.439
  734.6 7.4 scatter_custom_fusion.1
  742.0 4.2 all-to-all-start.2
  746.8 70.9 %all-to-all-done.2 = bf16[8,96,2048]{2,1,0:T(8,128)(2,1)S(1)} async-done(((bf16[8,96,2048]{2,1,0:T(8,128)(2,1)}), bf16[8,96,2048]{2,1,0:T(8,128)(2,1)S(1)}, u32[]{:S(2)}, u32[]{:S(2)}) %all-to-all-start.2) | async-done | bytes 3145760 | tf_op jit(solution)/shard_map/all_to_all | solution.py:215
  817.8 11.3 multiply_convert_fusion.1
  829.1 8.7 fusion.12
  837.8 9.2 add_convert_fusion
  847.0 3.7 all-to-all-start.3
  850.8 9.0 fusion.73
  861.3 10.0 bitcast_convert_fusion.1
  873.2 48.9 %all-to-all-done.3 = bf16[8,96,2048]{2,1,0:T(8,128)(2,1)S(1)} async-done(((bf16[8,96,2048]{2,1,0:T(8,128)(2,1)}), bf16[8,96,2048]{2,1,0:T(8,128)(2,1)S(1)}, u32[]{:S(2)}, u32[]{:S(2)}) %all-to-all-start.3) | async-done | bytes 3145760 | tf_op jit(solution)/shard_map/all_to_all | solution.py:237
  922.1 3.3 gather_fusion.1
  925.4 4.7 reshape.248
  930.1 5.0 reduce_sum.127
  939.7 34.9 %all-gather.27.cloned.1.call-done = bf16[512,2048]{1,0:T(8,128)(2,1)} async-done(((bf16[128,2048]{1,0:T(8,128)(2,1)}), bf16[512,2048]{1,0:T(8,128)(2,1)}) %all-gather.27.cloned.1.call-update) | async-done | bytes 2097168 | tf_op jit(solution)/shard_map/all_gather | solution.py:54
  974.6 3.6 fusion.74
  979.3 2.9 multiply_reduce_fusion
  982.5 4.7 multiply_convert_fusion.3
  990.8 7.5 bitcast_convert_fusion
  998.4 9.0 fusion.5
  1008.0 9.0 fusion.6
  1017.0 9.8 fusion.7
  1026.9 3.1 fusion.50
  1030.1 5.5 convolution_convert_fusion.5
  1038.5 7.2 pad_maximum_fusion.1
  1046.0 7.0 fusion.4
  1053.1 6.5 convolution_convert_fusion
  1059.5 7.2 pad_maximum_fusion
  1068.0 39.6 %all-reduce.1 = f32[2048]{0:T(1024)S(1)} all-reduce(f32[2048]{0:T(1024)S(1)} %bitcast.268), channel_id=9, replica_groups=mesh['fsdp'=4,'expert'=8] {'fsdp','expert'}, use_global_device_ids=true, to_apply=%region_25.26.clone | all-reduce | flops 2048 | bytes 16384
  1108.2 3.1 convert_element_type.269
  1111.3 60.2 %reduce-scatter.27.cloned.1.call-done = bf16[1,512,1408]{2,1,0:T(8,128)(2,1)} async-done(((bf16[1,2048,1408]{2,1,0:T(8,128)(2,1)}), bf16[1,512,1408]{2,1,0:T(8,128)(2,1)}) %reduce-scatter.27.cloned.1.call-update) | async-done | bytes 1441808 | tf_op jit(solution)/shard_map/reduce_scatter | solution.py:252
  1171.5 3.1 convert_element_type.272
  1174.7 65.4 %reduce-scatter.29.cloned.1.call-done = bf16[1,352,2048]{2,1,0:T(8,128)(2,1)} async-done(((bf16[1,1408,2048]{2,1,0:T(8,128)(2,1)}), bf16[1,352,2048]{2,1,0:T(8,128)(2,1)}) %reduce-scatter.29.cloned.1.call-update) | async-done | bytes 1441808 | tf_op jit(solution)/shard_map/reduce_scatter | solution.py:255
  1240.1 3.3 convert_element_type.275
  1244.7 134.7 %reduce-scatter.31.cloned.1.call-done = f32[64,2]{1,0:T(8,128)} async-done(((f32[2048,2]{1,0:T(8,128)}), f32[64,2]{1,0:T(8,128)}) %reduce-scatter.31.cloned.1.call-update) | async-done | bytes 528
  1380.8 86.5 %reduce-scatter.21.cloned.1.call-done = bf16[256,4,512]{2,0,1:T(8,128)(2,1)} async-done(((bf16[2048,4,512]{2,0,1:T(8,128)(2,1)}), bf16[256,4,512]{2,0,1:T(8,128)(2,1)}) %reduce-scatter.21.cloned.1.call-update) | async-done | bytes 1048592 | tf_op jit(solution)/shard_map/reduce_scatter | solution.py:346
  1467.3 3.4 copy.82
  1470.7 170.6 %reduce-scatter.23.cloned.1.call-done = bf16[256,3,1408]{2,0,1:T(8,128)(2,1)} async-done(((bf16[2048,3,1408]{2,0,1:T(8,128)(2,1)}), bf16[256,3,1408]{2,0,1:T(8,128)(2,1)}) %reduce-scatter.23.cloned.1.call-update) | async-done | bytes 2162704 | tf_op jit(solution)/shard_map/reduce_scatter | solution.py:349
  1641.3 3.9 convert_element_type.266
  (221 shorter events, 57.7 us)
Async XLA Ops:
  7.2 50.0 %copy-start.38 = (s32[16]{0:T(128)S(1)}, s32[16]{0:T(128)}, u32[]{:S(2)}) copy-start(s32[16]{0:T(128)} %param.16) | copy-start | bytes 196
  7.2 54.5 %copy-start.39 = (s32[16]{0:T(128)S(1)}, s32[16]{0:T(128)}, u32[]{:S(2)}) copy-start(s32[16]{0:T(128)} %param.15) | copy-start | bytes 196
  7.2 79.0 %all-gather.11.cloned.1.call-start = ((), (), s32[]{:S(2)}) async-start(), calls=%async_computation.14 | async-start | bytes 2621440 | tf_op jit(solution)/shard_map/all_gather | solution.py:54
  54.6 116.3 %all-gather.13.cloned.1.call-start = ((), (), s32[]{:S(2)}) async-start(), calls=%async_computation.15 | async-start | bytes 9437184 | tf_op jit(solution)/shard_map/all_gather | solution.py:112
  57.1 162.8 %reduce-scatter.13.cloned.1.call-start = ((), (), s32[]{:S(2)}) async-start(), calls=%async_computation.16 | async-start | bytes 2621440 | tf_op jit(solution)/shard_map/reduce_scatter | solution.py:58
  177.2 2.8 copy-start.18
  178.4 1.6 copy-start.11
  178.4 1.6 copy-start.13
  179.4 2.0 copy-start
  179.4 2.0 copy-start.30
  180.0 1.4 copy-start.32
  186.4 33.6 %copy-start.2 = (bf16[1,128,2048]{2,1,0:T(8,128)(2,1)S(1)}, bf16[1,128,2048]{2,1,0:T(8,128)(2,1)}, u32[]{:S(2)}) copy-start(bf16[1,128,2048]{2,1,0:T(8,128)(2,1)} %param.13) | copy-start | bytes 1572868
  186.4 100.9 %all-gather.19.cloned.1.call-start = ((), (), s32[]{:S(2)}) async-start(), calls=%async_computation.20 | async-start | bytes 7208960 | tf_op jit(solution)/shard_map/all_gather | solution.py:116
  187.0 167.7 %all-gather.21.cloned.1.call-start = ((), (), s32[]{:S(2)}) async-start(), calls=%async_computation.21 | async-start | bytes 7208960 | tf_op jit(solution)/shard_map/all_gather | solution.py:117
  187.6 36.6 %copy-start.35 = (s32[1,128,4]{1,2,0:T(4,128)S(1)}, s32[1,128,4]{1,2,0:T(4,128)}, u32[]{:S(2)}) copy-start(s32[1,128,4]{1,2,0:T(4,128)} %param.17) | copy-start | bytes 6148
  187.6 234.5 %all-gather.23.cloned.1.call-start = ((), (), s32[]{:S(2)}) async-start(), calls=%async_computation.22 | async-start | bytes 7208960 | tf_op jit(solution)/shard_map/all_gather | solution.py:118
  188.2 271.0 %all-gather.15.cloned.1.call-start = ((), (), s32[]{:S(2)}) async-start(), calls=%async_computation.17 | async-start | bytes 2621440 | tf_op jit(solution)/shard_map/all_gather | solution.py:54
  223.4 2.9 copy-start.7
  223.4 424.9 %all-gather.17.cloned.1.call-start = ((), (), s32[]{:S(2)}) async-start(), calls=%async_computation.18 | async-start | bytes 19464192 | tf_op jit(solution)/shard_map/all_gather | solution.py:113
  236.2 76.2 %all-to-all-start = ((bf16[8,96,2048]{2,1,0:T(8,128)(2,1)}), bf16[8,96,2048]{2,1,0:T(8,128)(2,1)S(1)}, u32[]{:S(2)}, u32[]{:S(2)}) async-start(bf16[8,96,2048]{2,1,0:T(8,128)(2,1)} %bitcast.27), calls=%async_computation.2 | async-start | bytes 6291456 | tf_op jit(solution)/shard_map/all_to_all | solution.py:173
  312.4 42.4 %copy-start.16 = (bf16[8,96,2048]{2,1,0:T(8,128)(2,1)}, bf16[8,96,2048]{2,1,0:T(8,128)(2,1)S(1)}, u32[]{:S(2)}) copy-start(bf16[8,96,2048]{2,1,0:T(8,128)(2,1)S(1)} %all-to-all-done) | copy-start | bytes 9437188
  431.0 278.0 %all-to-all-start.1 = ((bf16[8,96,2048]{2,1,0:T(8,128)(2,1)}), bf16[8,96,2048]{2,1,0:T(8,128)(2,1)S(1)}, u32[]{:S(2)}, u32[]{:S(2)}) async-start(bf16[8,96,2048]{2,1,0:T(8,128)(2,1)} %bitcast.252), calls=%async_computation.3 | async-start | bytes 6291456 | tf_op jit(solution)/shard_map/all_to_all | solution.py:181
  435.6 287.0 %reduce-scatter.15.cloned.1.call-start = ((), (), s32[]{:S(2)}) async-start(), calls=%async_computation.19 | async-start | bytes 2621440 | tf_op jit(solution)/shard_map/reduce_scatter | solution.py:58
  658.4 2.5 copy-start.44
  660.9 8.0 copy-start.42
  660.9 45.7 %copy-start.34 = (f32[1,128,4]{1,2,0:T(4,128)S(1)}, f32[1,128,4]{1,2,0:T(4,128)}, u32[]{:S(2)}) copy-start(f32[1,128,4]{1,2,0:T(4,128)} %param.18) | copy-start | bytes 6148
  717.1 5.5 copy-start.3
  717.1 5.5 copy-start.9
  717.1 5.5 copy-start.27
  742.0 75.7 %all-to-all-start.2 = ((bf16[8,96,2048]{2,1,0:T(8,128)(2,1)}), bf16[8,96,2048]{2,1,0:T(8,128)(2,1)S(1)}, u32[]{:S(2)}, u32[]{:S(2)}) async-start(bf16[8,96,2048]{2,1,0:T(8,128)(2,1)} %bitcast.41), calls=%async_computation.5 | async-start | bytes 6291456 | tf_op jit(solution)/shard_map/all_to_all | solution.py:215
  746.3 104.5 %all-gather.25.cloned.1.call-start = ((), (), s32[]{:S(2)}) async-start(), calls=%async_computation.23 | async-start | bytes 2621440 | tf_op jit(solution)/shard_map/all_gather | solution.py:54
  817.8 11.3 copy-start.17
  829.1 8.7 copy-start.46
  829.1 8.7 copy-start.45
  847.0 75.1 %all-to-all-start.3 = ((bf16[8,96,2048]{2,1,0:T(8,128)(2,1)}), bf16[8,96,2048]{2,1,0:T(8,128)(2,1)S(1)}, u32[]{:S(2)}, u32[]{:S(2)}) async-start(bf16[8,96,2048]{2,1,0:T(8,128)(2,1)} %bitcast.253), calls=%async_computation.6 | async-start | bytes 6291456 | tf_op jit(solution)/shard_map/all_to_all | solution.py:237
  850.7 84.4 %reduce-scatter.17.cloned.1.call-start = ((), (), s32[]{:S(2)}) async-start(), calls=%async_computation.24 | async-start | bytes 2621440 | tf_op jit(solution)/shard_map/reduce_scatter | solution.py:58
  859.8 1.6 copy-start.49
  871.4 103.2 %all-gather.27.cloned.1.call-start = ((), (), s32[]{:S(2)}) async-start(), calls=%async_computation.25 | async-start | bytes 2621440 | tf_op jit(solution)/shard_map/all_gather | solution.py:54
  930.1 5.0 copy-start.4
  930.1 5.0 copy-start.10
  930.1 6.7 copy-start.6
  936.8 2.9 copy-start.31
  936.8 2.9 copy-start.33
  939.6 96.0 %reduce-scatter.19.cloned.1.call-start = ((), (), s32[]{:S(2)}) async-start(), calls=%async_computation.26 | async-start | bytes 2621440 | tf_op jit(solution)/shard_map/reduce_scatter | solution.py:58
  974.6 3.7 copy-start.1
  982.4 4.7 copy-start.14
  990.6 7.8 copy-start.23
  990.8 7.6 copy-start.25
  998.4 109.8 %reduce-scatter.25.cloned.1.call-start = ((), (), s32[]{:S(2)}) async-start(), calls=%async_computation.29 | async-start | bytes 7208960 | tf_op jit(solution)/shard_map/reduce_scatter | solution.py:249
  1007.5 164.0 %reduce-scatter.27.cloned.1.call-start = ((), (), s32[]{:S(2)}) async-start(), calls=%async_computation.30 | async-start | bytes 7208960 | tf_op jit(solution)/shard_map/reduce_scatter | solution.py:252
  1017.0 223.1 %reduce-scatter.29.cloned.1.call-start = ((), (), s32[]{:S(2)}) async-start(), calls=%async_computation.31 | async-start | bytes 7208960 | tf_op jit(solution)/shard_map/reduce_scatter | solution.py:255
  1026.8 352.6 %reduce-scatter.31.cloned.1.call-start = ((), (), s32[]{:S(2)}) async-start(), calls=%async_computation.32 | async-start | bytes 1081344
  1026.9 3.2 copy-start.24
  1026.9 3.2 copy-start.26
  1026.9 3.2 copy-start.40
  1030.1 5.5 copy-start.29
  1030.1 5.5 copy-start.37
  1038.4 428.9 %reduce-scatter.21.cloned.1.call-start = ((), (), s32[]{:S(2)}) async-start(), calls=%async_computation.27 | async-start | bytes 9437184 | tf_op jit(solution)/shard_map/reduce_scatter | solution.py:346
  1045.7 7.3 copy-start.41
  1045.7 595.5 %reduce-scatter.23.cloned.1.call-start = ((), (), s32[]{:S(2)}) async-start(), calls=%async_computation.28 | async-start | bytes 19464192 | tf_op jit(solution)/shard_map/reduce_scatter | solution.py:349
  1046.0 7.1 copy-start.48
  1046.0 7.1 copy-start.50
  1174.6 68.7 %copy-start.15 = (f32[128,2048]{1,0:T(8,128)S(1)}, f32[128,2048]{1,0:T(8,128)}, u32[]{:S(2)}) copy-start(f32[128,2048]{1,0:T(8,128)} %get-tuple-element.41) | copy-start | bytes 3145732
  1174.7 68.7 %copy-start.20 = (bf16[128,2048]{1,0:T(8,128)(2,1)S(1)}, bf16[128,2048]{1,0:T(8,128)(2,1)}, u32[]{:S(2)}) copy-start(bf16[128,2048]{1,0:T(8,128)(2,1)} %reduce-scatter.19.cloned.1.call-done) | copy-start | bytes 1572868
  (10 other events, 9.8 us)
Sparse Core Ops, SparseCore 0:
  54.7 31.4 all-gather.10
  88.4 82.4 all-gather.12
  186.5 33.3 reduce-scatter.12
  221.7 65.6 all-gather.18
  289.0 65.6 all-gather.20
  356.4 65.6 all-gather.22
  424.0 35.1 all-gather.14
  460.8 187.4 all-gather.16
  668.4 33.5 reduce-scatter.14
  749.2 37.3 all-gather.24
  871.5 37.2 reduce-scatter.16
  939.7 34.8 all-gather.26
  998.5 35.1 reduce-scatter.18
  1036.6 66.2 reduce-scatter.24
  1105.8 65.7 reduce-scatter.26
  1174.4 65.6 reduce-scatter.28
  1242.7 136.6 reduce-scatter.30
  1381.6 85.7 reduce-scatter.20
  1469.7 171.5 reduce-scatter.22
where the time goes:
time: 1660 us; the launch traced here: 1650 us
  waiting for transfers between devices  1180 us (71%)
  matrix products  175 us (11%)
  blocking collectives  121 us (7%)
  other arithmetic  76.4 us (5%)
  local copies, waits for them, and re-layouts  56.2 us (3%)
  between operations  21 us (1%)
  starting transfers between devices  19.5 us (1%)
    all_gather x1, waiting for transfers between devices, on_device(): lax.all_gather(shared_weights, 'expert', axis=0, tiled=True)  189 us
    reduce_scatter x1, waiting for transfers between devices, on_device(): lax.psum_scatter(shared_term.astype(jnp.bfloat16), 'expert', scatter_dime...  171 us
    unnamed x20, waiting for transfers between devices  137 us
    reduce_scatter x1, waiting for transfers between devices, on_device(): lax.psum_scatter(mixer_term.astype(jnp.bfloat16), 'expert', scatter_dimen...  86.5 us
    all_gather x1, waiting for transfers between devices, on_device(): lax.all_gather(mixer_weights, 'expert', axis=0, tiled=True)  84.7 us
    all_gather x4, waiting for transfers between devices, row_tokens(): return lax.all_gather(values, 'fsdp', axis=0, tiled=True)  77.4 us
    unnamed x2, blocking collectives  77.1 us
    all_to_all x1, waiting for transfers between devices, on_device(): lax.all_to_all(dsend.reshape(groups, capacity, model_width), 'expert', sp...  70.9 us
  transfers between devices with their start and end apart: 23, of which 17 were waited for; matrix products, arithmetic and copies ran while one was open for 14% of the time, Pallas kernels for 0%

commit v1 on v0

v1 whole, which is shorter than its diff:
```python
import functools

import jax
import jax.numpy as jnp
from jax import lax
from jax.experimental import pallas as pl
from jax.experimental.pallas import tpu as pltpu
from jax.sharding import PartitionSpec as P

HD = 128
TOP = 4
THETA = 1000000.0
EPSILON = 1e-06
NEG_LARGE = -1e30
MESH = pl.DeviceIdType.MESH
F32 = jnp.float32
BF16 = jnp.bfloat16


def turn(values):
    half = values.shape[-1] // 2
    return jnp.concatenate([-values[..., half:], values[..., :half]], axis=-1)


def turn_back(values):
    half = values.shape[-1] // 2
    return jnp.concatenate([values[..., half:], -values[..., :half]], axis=-1)


def norm_back(incoming, values, scale_rows, gain_row):
    unit_rows = values * scale_rows[:, None]
    gain_grad = jnp.sum(incoming * unit_rows, axis=0)
    dunit = incoming * gain_row[None, :]
    back_rows = scale_rows[:, None] * (
        dunit - unit_rows * jnp.mean(dunit * unit_rows, axis=1, keepdims=True)
    )
    return (back_rows, gain_grad)


def dot(form, left, right):
    return jnp.einsum(form, left, right, preferred_element_type=F32)


def swap_x(values):
    return lax.ppermute(values, "fsdp", [(0, 1), (1, 0), (2, 3), (3, 2)])


def swap_y(values):
    return lax.ppermute(values, "fsdp", [(0, 2), (2, 0), (1, 3), (3, 1)])


def square_gather(block):
    half = block.shape[0] // 2
    from_x = swap_x(block)
    from_y = swap_y(block)
    low = swap_y(from_x[:half])
    high = swap_x(from_y[half:])
    return [block, from_x, from_y, low, high]


def square_scatter(parts):
    half = parts[0].shape[0] // 2
    low_send = parts[3][:half].astype(BF16)
    high_send = parts[3][half:].astype(BF16)
    low = swap_x(low_send)
    high = swap_y(high_send)
    to_y = jnp.concatenate(
        [(parts[2][:half].astype(F32) + low.astype(F32)).astype(BF16), parts[2][half:].astype(BF16)]
    )
    to_x = jnp.concatenate(
        [parts[1][:half].astype(BF16), (parts[1][half:].astype(F32) + high.astype(F32)).astype(BF16)]
    )
    from_x = swap_x(to_x)
    from_y = swap_y(to_y)
    return parts[0].astype(F32) + from_x.astype(F32) + from_y.astype(F32)


def row_tokens(block):
    return jnp.concatenate(square_gather(block), axis=0)


def row_scatter(product):
    quarter = product.shape[0] // 4
    return square_scatter([product[j * quarter : (j + 1) * quarter] for j in range(4)])


def gather_shards(shard, index):
    rows = shard.shape[0]
    half = rows // 2
    own, from_x, from_y, low, high = square_gather(shard)
    whole = jnp.zeros((4 * rows,) + shard.shape[1:], shard.dtype)
    for piece, start in (
        (own, index * rows),
        (from_x, (index ^ 1) * rows),
        (from_y, (index ^ 2) * rows),
        (low, (index ^ 3) * rows),
        (high, (index ^ 3) * rows + half),
    ):
        whole = lax.dynamic_update_slice(whole, piece, (start, 0))
    return whole


def scatter_shards(whole, index):
    rows = whole.shape[0] // 4
    return square_scatter(
        [lax.dynamic_slice_in_dim(whole, (index ^ j) * rows, rows) for j in range(4)]
    )


def opening_kernel(
    chips,
    x_ref, vector_ref, routed_ref, mixer_ref, gate_ref,
    gains_ref, tables_ref, row_ref, mixers_ref, gates_ref,
    vectors, send_v, receive_v, send_t, receive_t,
    send_n, receive_n, send_g, receive_g,
    up_sem, down_sem, in_low, in_high, to_partner, in_partner, local,
):
    nf, ne = lax.axis_size("fsdp"), lax.axis_size("expert")
    total = nf * ne
    f, e = lax.axis_index("fsdp"), lax.axis_index("expert")
    me = f * ne + e
    z, c = e // 2, lax.rem(e, 2)
    xn, yn = f ^ 1, f ^ 2
    up = (f, jnp.minimum(z + 1, chips - 1) * 2 + c)
    down = (f, jnp.maximum(z - 1, 0) * 2 + c)
    partner = (f, z * 2 + 1 - c)
    own_mixer = pltpu.make_async_copy(mixer_ref, mixers_ref.at[:, e], local.at[0])
    own_gate = pltpu.make_async_copy(gate_ref, gates_ref.at[f], local.at[1])
    own_mixer.start()
    own_gate.start()
    barrier = pltpu.get_barrier_semaphore()

    def greet(step, carry):
        peer = lax.rem(me + step, total)
        pl.semaphore_signal(
            barrier, inc=1, device_id=(peer // ne, lax.rem(peer, ne)), device_id_type=MESH
        )
        return carry

    lax.fori_loop(1, total, greet, 0)
    pl.semaphore_wait(barrier, total - 1)

    def remote(source, target, send, receive, device):
        return pltpu.make_async_remote_copy(
            src_ref=source,
            dst_ref=target,
            send_sem=send,
            recv_sem=receive,
            device_id=device,
            device_id_type=MESH,
        )

    def vector_copy(slot, peer):
        return remote(
            vector_ref, vectors.at[slot], send_v.at[peer], receive_v.at[slot],
            (peer // ne, lax.rem(peer, ne)),
        )

    def table_copy(slot, peer):
        return remote(routed_ref, tables_ref.at[slot], send_t.at[peer], receive_t.at[slot], (f, peer))

    def start_vector(step, carry):
        vector_copy(me, lax.rem(me + step, total)).start()
        return carry

    def start_table(step, carry):
        table_copy(e, lax.rem(e + step, ne)).start()
        return carry

    lax.fori_loop(1, total, start_vector, 0)
    lax.fori_loop(1, ne, start_table, 0)
    vectors[me] = vector_ref[...]
    tables_ref[e] = routed_ref[...]

    def shard(origin, target, send, receive, own):
        place = mixers_ref.at[:, origin * 2 + c]
        return remote(mixer_ref if own else place, place, send, receive, target)

    def upward(origin, r, own=False):
        return shard(origin, up, up_sem.at[r], in_low.at[r], own)

    def downward(origin, r, own=False):
        return shard(origin, down, down_sem.at[r], in_high.at[r], own)

    def across(origin, own=False):
        return shard(origin, partner, to_partner.at[origin], in_partner.at[origin], own)

    @pl.when(z < chips - 1)
    def _():
        upward(z, 0, True).start()

    @pl.when(z > 0)
    def _():
        downward(z, 0, True).start()

    across(z, True).start()

    def end_vector(step, carry):
        peer = lax.rem(me + step, total)
        vector_copy(peer, peer).wait_recv()
        return carry

    lax.fori_loop(1, total, end_vector, 0)
    blocks = gains_ref.shape[1] // 128
    per = total // blocks
    for block in range(blocks):
        gains_ref[:, block * 128 : (block + 1) * 128] = jnp.sum(
            vectors[block * per : (block + 1) * per], axis=0
        )
    half = x_ref.shape[0] // 2
    low, high = pl.ds(0, half), pl.ds(half, half)

    def piece(index, ref, origin, rows, device, slot):
        place = ref.at[origin, rows]
        send, receive = (send_n, receive_n) if index == 0 else (send_g, receive_g)
        return remote(place, place, send.at[slot], receive.at[slot], (device, e))

    def outgoing(index, ref, first, second):
        return [
            piece(index, ref, f, first, xn, 0),
            piece(index, ref, f, second, yn, 1),
            piece(index, ref, f, second, xn, 2),
            piece(index, ref, f, first, yn, 3),
        ]

    def relays(index, ref, first, second):
        return [piece(index, ref, xn, first, yn, 4), piece(index, ref, yn, second, xn, 5)]

    for rows in (low, high):
        values = x_ref[rows].astype(F32)
        scale = lax.rsqrt(jnp.mean(values * values, axis=1, keepdims=True) + EPSILON)
        row_ref[f, rows] = (values * scale * gains_ref[0:1]).astype(BF16)
    own_gate.wait()
    row_out = outgoing(0, row_ref, low, high)
    row_relay = relays(0, row_ref, low, high)
    depth = gate_ref.shape[0] // 2
    first, second = pl.ds(0, depth), pl.ds(depth, depth)
    gate_out = outgoing(1, gates_ref, first, second)
    gate_relay = relays(1, gates_ref, first, second)
    for copy in row_out + gate_out:
        copy.start()
    piece(0, row_ref, xn, low, xn, 0).wait_recv()
    row_relay[0].start()
    piece(0, row_ref, yn, high, yn, 1).wait_recv()
    row_relay[1].start()

    def hop(r, carry):
        before, after = z - r, z + r

        @pl.when(before >= 0)
        def _():
            upward(before, r - 1).wait_recv()

            @pl.when(z < chips - 1)
            def _():
                upward(before, r).start()

            across(before).start()

        @pl.when(after < chips)
        def _():
            downward(after, r - 1).wait_recv()

            @pl.when(z > 0)
            def _():
                downward(after, r).start()

            across(after).start()

        return carry

    lax.fori_loop(1, 3, hop, 0)
    piece(1, gates_ref, xn, first, xn, 0).wait_recv()
    gate_relay[0].start()
    piece(1, gates_ref, yn, second, yn, 1).wait_recv()
    gate_relay[1].start()
    lax.fori_loop(3, chips, hop, 0)

    for index, ref, (one, two) in ((0, row_ref, (low, high)), (1, gates_ref, (first, second))):
        piece(index, ref, xn, two, xn, 2).wait_recv()
        piece(index, ref, yn, one, yn, 3).wait_recv()
        piece(index, ref, f ^ 3, one, yn, 4).wait_recv()
        piece(index, ref, f ^ 3, two, xn, 5).wait_recv()
    for copy in row_out + gate_out + row_relay + gate_relay:
        copy.wait_send()
    own_mixer.wait()

    @pl.when(z < chips - 1)
    def _():
        upward(z, 0, True).wait_send()

    @pl.when(z > 0)
    def _():
        downward(z, 0, True).wait_send()

    def finish(r, carry):
        before, after = z - r, z + r

        @pl.when((before >= 0) & (z < chips - 1))
        def _():
            upward(before, r).wait_send()

        @pl.when((after < chips) & (z > 0))
        def _():
            downward(after, r).wait_send()

        return carry

    lax.fori_loop(1, chips, finish, 0)

    def shared(origin, carry):
        across(origin).wait_send()
        across(origin).wait_recv()
        return carry

    lax.fori_loop(0, chips, shared, 0)

    def sent_vector(step, carry):
        peer = lax.rem(me + step, total)
        vector_copy(peer, peer).wait_send()
        return carry

    def end_table(step, carry):
        peer = lax.rem(e + step, ne)
        copy = table_copy(peer, peer)
        copy.wait_recv()
        copy.wait_send()
        return carry

    lax.fori_loop(1, total, sent_vector, 0)
    lax.fori_loop(1, ne, end_table, 0)


def opening(x, vector, routed, mixer, gate, nf):
    ne = routed.shape[0]
    chips, devices = ne // 2, nf * ne
    whole = pl.BlockSpec(memory_space=pltpu.VMEM)
    far = pl.BlockSpec(memory_space=pl.ANY)
    dma = pltpu.SemaphoreType.DMA
    return pl.pallas_call(
        functools.partial(opening_kernel, chips),
        out_shape=[
            jax.ShapeDtypeStruct((8, x.shape[1]), F32),
            jax.ShapeDtypeStruct((ne,) + routed.shape, F32),
            jax.ShapeDtypeStruct((nf,) + x.shape, BF16),
            jax.ShapeDtypeStruct((mixer.shape[0], ne) + mixer.shape[1:], BF16),
            jax.ShapeDtypeStruct((nf,) + gate.shape, BF16),
        ],
        in_specs=[whole] * 5,
        out_specs=[whole, whole, whole, far, far],
        scratch_shapes=[pltpu.VMEM((devices,) + vector.shape, F32)]
        + [dma((devices,))] * 2
        + [dma((ne,))] * 2
        + [dma((6,))] * 4
        + [dma((chips,))] * 6
        + [dma((2,))],
        compiler_params=pltpu.CompilerParams(
            collective_id=1, has_side_effects=True, vmem_limit_bytes=24 * 1024 * 1024
        ),
        name="opening",
    )(x, vector, routed, mixer, gate)


def collect_kernel(terms_ref, sum_ref, arrived, send, receive):
    nf, ne = lax.axis_size("fsdp"), lax.axis_size("expert")
    total = nf * ne
    me = lax.axis_index("fsdp") * ne + lax.axis_index("expert")
    barrier = pltpu.get_barrier_semaphore()

    def greet(step, carry):
        peer = lax.rem(me + step, total)
        pl.semaphore_signal(
            barrier, inc=1, device_id=(peer // ne, lax.rem(peer, ne)), device_id_type=MESH
        )
        return carry

    lax.fori_loop(1, total, greet, 0)
    pl.semaphore_wait(barrier, total - 1)

    def copy_of(slot, peer):
        return pltpu.make_async_remote_copy(
            src_ref=terms_ref.at[peer],
            dst_ref=arrived.at[slot],
            send_sem=send.at[peer],
            recv_sem=receive.at[slot],
            device_id=(peer // ne, lax.rem(peer, ne)),
            device_id_type=MESH,
        )

    def begin(step, carry):
        copy_of(me, lax.rem(me + step, total)).start()
        return carry

    lax.fori_loop(1, total, begin, 0)
    arrived[me] = terms_ref[me]

    def end(step, carry):
        peer = lax.rem(me + step, total)
        copy = copy_of(peer, peer)
        copy.wait_recv()
        copy.wait_send()
        return carry

    lax.fori_loop(1, total, end, 0)
    sum_ref[...] = jnp.sum(arrived[...], axis=0)


def collect(terms):
    devices = terms.shape[0]
    return pl.pallas_call(
        collect_kernel,
        out_shape=jax.ShapeDtypeStruct(terms.shape[1:], terms.dtype),
        in_specs=[pl.BlockSpec(memory_space=pltpu.VMEM)],
        out_specs=pl.BlockSpec(memory_space=pltpu.VMEM),
        scratch_shapes=[pltpu.VMEM(terms.shape, terms.dtype)]
        + [pltpu.SemaphoreType.DMA((devices,))] * 2,
        compiler_params=pltpu.CompilerParams(collective_id=2, has_side_effects=True),
        name="collect",
    )(terms)


def line_entry(f, z, c, chips):
    up = (f, jnp.minimum(z + 1, chips - 1) * 2 + c)
    down = (f, jnp.maximum(z - 1, 0) * 2 + c)
    partner = (f, z * 2 + 1 - c)
    barrier = pltpu.get_barrier_semaphore()
    pl.semaphore_signal(barrier, inc=1, device_id=partner, device_id_type=MESH)

    @pl.when(z < chips - 1)
    def _():
        pl.semaphore_signal(barrier, inc=1, device_id=up, device_id_type=MESH)

    @pl.when(z > 0)
    def _():
        pl.semaphore_signal(barrier, inc=1, device_id=down, device_id_type=MESH)

    known = 1 + jnp.where(z < chips - 1, 1, 0) + jnp.where(z > 0, 1, 0)
    pl.semaphore_wait(barrier, known)
    return up, down, partner


def line_gather_kernel(chips, block_ref, all_ref, up_sem, down_sem, in_low, in_high, to_partner, in_partner, own_sem):
    f, e = lax.axis_index("fsdp"), lax.axis_index("expert")
    z, c = e // 2, lax.rem(e, 2)
    own = pltpu.make_async_copy(block_ref, all_ref.at[e], own_sem)
    own.start()
    up, down, partner = line_entry(f, z, c, chips)

    def copy(origin, target, send, receive):
        place = all_ref.at[origin * 2 + c]
        return pltpu.make_async_remote_copy(
            src_ref=place,
            dst_ref=place,
            send_sem=send,
            recv_sem=receive,
            device_id=target,
            device_id_type=MESH,
        )

    def upward(origin, r):
        return copy(origin, up, up_sem.at[r], in_low.at[r])

    def downward(origin, r):
        return copy(origin, down, down_sem.at[r], in_high.at[r])

    def across(origin):
        return copy(origin, partner, to_partner.at[origin], in_partner.at[origin])

    own.wait()

    @pl.when(z < chips - 1)
    def _():
        upward(z, 0).start()

    @pl.when(z > 0)
    def _():
        downward(z, 0).start()

    across(z).start()

    def hop(r, carry):
        low, high = z - r, z + r

        @pl.when(low >= 0)
        def _():
            upward(low, r - 1).wait_recv()

            @pl.when(z < chips - 1)
            def _():
                upward(low, r).start()

            across(low).start()

        @pl.when(high < chips)
        def _():
            downward(high, r - 1).wait_recv()

            @pl.when(z > 0)
            def _():
                downward(high, r).start()

            across(high).start()

        return carry

    lax.fori_loop(1, chips, hop, 0)

    def finish(r, carry):
        low, high = z - r, z + r

        @pl.when((low >= 0) & (z < chips - 1))
        def _():
            upward(low, r).wait_send()

        @pl.when((high < chips) & (z > 0))
        def _():
            downward(high, r).wait_send()

        return carry

    lax.fori_loop(0, chips, finish, 0)

    def shared(origin, carry):
        across(origin).wait_send()
        across(origin).wait_recv()
        return carry

    lax.fori_loop(0, chips, shared, 0)


def line_gather(block, ne, cid):
    chips = ne // 2
    return pl.pallas_call(
        functools.partial(line_gather_kernel, chips),
        out_shape=jax.ShapeDtypeStruct((ne,) + block.shape, block.dtype),
        in_specs=[pl.BlockSpec(memory_space=pltpu.VMEM)],
        out_specs=pl.BlockSpec(memory_space=pltpu.VMEM),
        scratch_shapes=[pltpu.SemaphoreType.DMA((chips,))] * 6 + [pltpu.SemaphoreType.DMA],
        compiler_params=pltpu.CompilerParams(collective_id=cid, has_side_effects=True),
        name=f"line_gather{cid}",
    )(block)


def line_scatter_kernel(
    chips, terms_ref, sum_ref, theirs, going_up, going_down, from_low, from_high,
    up_sem, down_sem, in_low, in_high, to_partner, in_partner,
):
    f, e = lax.axis_index("fsdp"), lax.axis_index("expert")
    z, c = e // 2, lax.rem(e, 2)
    up, down, partner = line_entry(f, z, c, chips)

    def across(target):
        return pltpu.make_async_remote_copy(
            src_ref=terms_ref.at[target * 2 + 1 - c],
            dst_ref=theirs.at[target],
            send_sem=to_partner.at[target],
            recv_sem=in_partner.at[target],
            device_id=partner,
            device_id_type=MESH,
        )

    def upward(target):
        return pltpu.make_async_remote_copy(
            src_ref=going_up.at[target],
            dst_ref=from_low.at[target],
            send_sem=up_sem.at[target],
            recv_sem=in_low.at[target],
            device_id=up,
            device_id_type=MESH,
        )

    def downward(target):
        return pltpu.make_async_remote_copy(
            src_ref=going_down.at[target],
            dst_ref=from_high.at[target],
            send_sem=down_sem.at[target],
            recv_sem=in_high.at[target],
            device_id=down,
            device_id_type=MESH,
        )

    def offer(r, carry):
        across(r).start()
        across(chips - 1 - r).start()
        return carry

    lax.fori_loop(0, chips // 2, offer, 0)

    def chip_term(target):
        return terms_ref[target * 2 + c].astype(F32) + theirs[target].astype(F32)

    def pass_on(r, carry):
        high, low = chips - 1 - r, r

        @pl.when(high > z)
        def _():
            across(high).wait_recv()

            @pl.when(z > 0)
            def _():
                upward(high).wait_recv()
                going_up[high] = (chip_term(high) + from_low[high].astype(F32)).astype(BF16)

            @pl.when(z == 0)
            def _():
                going_up[high] = chip_term(high).astype(BF16)

            upward(high).start()

        @pl.when(low < z)
        def _():
            across(low).wait_recv()

            @pl.when(z < chips - 1)
            def _():
                downward(low).wait_recv()
                going_down[low] = (chip_term(low) + from_high[low].astype(F32)).astype(BF16)

            @pl.when(z == chips - 1)
            def _():
                going_down[low] = chip_term(low).astype(BF16)

            downward(low).start()

        return carry

    lax.fori_loop(0, chips, pass_on, 0)
    across(z).wait_recv()
    sum_ref[...] = chip_term(z)

    @pl.when(z > 0)
    def _():
        upward(z).wait_recv()
        sum_ref[...] += from_low[z].astype(F32)

    @pl.when(z < chips - 1)
    def _():
        downward(z).wait_recv()
        sum_ref[...] += from_high[z].astype(F32)

    def finish(target, carry):
        across(target).wait_send()

        @pl.when(target > z)
        def _():
            upward(target).wait_send()

        @pl.when(target < z)
        def _():
            downward(target).wait_send()

        return carry

    lax.fori_loop(0, chips, finish, 0)


def line_scatter(terms, cid):
    ne = terms.shape[0]
    chips = ne // 2
    blocks = (chips,) + terms.shape[1:]
    return pl.pallas_call(
        functools.partial(line_scatter_kernel, chips),
        out_shape=jax.ShapeDtypeStruct(terms.shape[1:], F32),
        in_specs=[pl.BlockSpec(memory_space=pltpu.VMEM)],
        out_specs=pl.BlockSpec(memory_space=pltpu.VMEM),
        scratch_shapes=[pltpu.VMEM(blocks, terms.dtype)] * 5
        + [pltpu.SemaphoreType.DMA((chips,))] * 6,
        compiler_params=pltpu.CompilerParams(
            collective_id=cid, has_side_effects=True, vmem_limit_bytes=60 * 1024 * 1024
        ),
        name=f"line_scatter{cid}",
    )(terms)


def on_device(
    inputs,
    teacher,
    lengths,
    deal_order,
    routes,
    route_weights,
    norm_gains,
    mixer_weights,
    shared_weights,
    shared_gate,
    expert_gate,
    expert_up,
    expert_down,
):
    tokens_dev = inputs.shape[1]
    width = inputs.shape[2]
    nf = lax.axis_size("fsdp")
    ne = lax.axis_size("expert")
    devices = nf * ne
    row_len = tokens_dev * nf
    capacity = 3 * tokens_dev * TOP // (2 * ne)
    total_tokens = row_len * ne
    columns = mixer_weights.shape[2]
    heads_local = columns // HD
    f_index = lax.axis_index("fsdp")
    e_index = lax.axis_index("expert")

    piece = norm_gains.shape[1]
    slot = (f_index * ne + e_index) % (128 // piece)
    vector = jnp.concatenate([norm_gains, shared_gate[None]], axis=0).astype(F32)
    vector = lax.dynamic_update_slice(jnp.zeros((8, 128), F32), vector, (0, slot * piece))
    chosen = routes[0]
    weights_route = route_weights[0]
    expert_ids = jnp.arange(ne, dtype=jnp.int32)
    routed = jnp.sum(
        jnp.where(chosen.T[None] == expert_ids[:, None, None], weights_route.T[None], 0.0), axis=1
    )
    mixer_shard = jnp.transpose(mixer_weights, (1, 0, 2))
    gains, tables, row_blocks, mixers, gates = opening(
        inputs[0], vector, routed, mixer_shard, expert_gate[0], nf
    )
    first_gain, second_gain, gate_vector = gains[0], gains[1], gains[2]
    token_weight = lax.dynamic_index_in_dim(tables, e_index, axis=1, keepdims=False)
    mixers = mixers.reshape(4, width, columns)
    mixer_in, mixer_out = mixers[:3], mixers[3]
    gate_rows = gates.reshape(width, gates.shape[2])
    order_x = f_index ^ jnp.arange(nf, dtype=jnp.int32)
    row_normed = row_blocks[order_x].reshape(row_len, width)

    shared_shard, up_shard, down_shard, gains = lax.optimization_barrier(
        (shared_weights, expert_up[0], expert_down[0], gains)
    )
    shared_shard = jnp.transpose(shared_shard, (1, 0, 2))
    shared_in = lax.all_gather(shared_shard[:2], "expert", axis=1, tiled=True)
    shared_down = lax.all_gather(shared_shard[2], "expert", axis=0, tiled=True)
    up_rows = gather_shards(up_shard, f_index)
    down_rows = gather_shards(down_shard, f_index)

    first_len = lengths[deal_order[2 * e_index]]
    second_len = lengths[deal_order[2 * e_index + 1]]
    row_places = (
        (f_index ^ jnp.arange(nf, dtype=jnp.int32))[:, None] * tokens_dev
        + jnp.arange(tokens_dev, dtype=jnp.int32)[None]
    ).reshape(row_len)
    row_segment = (row_places >= first_len).astype(jnp.int32) + (
        row_places >= first_len + second_len
    ).astype(jnp.int32)
    row_position = (
        row_places
        - first_len * (row_segment >= 1).astype(jnp.int32)
        - second_len * (row_segment >= 2).astype(jnp.int32)
    )
    own_segment = row_segment[:tokens_dev]
    allowed = (row_segment[:, None] == row_segment[None, :]) & (
        row_places[None, :] <= row_places[:, None]
    )
    inverse = THETA ** (-(jnp.arange(HD // 2, dtype=F32) * 2.0) / HD)
    angles = row_position.astype(F32)[:, None] * inverse[None, :]
    cosine = jnp.concatenate([jnp.cos(angles)] * 2, axis=1)[:, None, :]
    sine = jnp.concatenate([jnp.sin(angles)] * 2, axis=1)[:, None, :]

    flat_inputs = inputs[0].astype(F32)
    first_scale = lax.rsqrt(jnp.mean(flat_inputs * flat_inputs, axis=1) + EPSILON)
    projected = dot("td,kde->kte", row_normed, mixer_in)

    def heads(values):
        return values.reshape(row_len, heads_local, HD)

    raw_query, raw_key = heads(projected[0]), heads(projected[1])
    queries = (raw_query * cosine + turn(raw_query) * sine).astype(BF16)
    keys = (raw_key * cosine + turn(raw_key) * sine).astype(BF16)
    values = heads(projected[2].astype(BF16))
    score_factor = HD ** (-0.5)

    def score():
        raw = dot("qhd,khd->hqk", queries, keys)
        return jnp.where(allowed[None], raw * score_factor, NEG_LARGE)

    scores = score()
    top_score = jnp.max(scores, axis=2, keepdims=True)
    shifted = jnp.exp(scores - top_score)
    row_total = jnp.sum(shifted, axis=2, keepdims=True)
    probabilities = shifted / row_total
    log_total = top_score + jnp.log(row_total)
    context = dot("hqk,khd->qhd", probabilities.astype(BF16), values)
    context = context.reshape(row_len, columns).astype(BF16)
    attn_out = row_scatter(dot("tc,dc->td", context, mixer_out))
    residual = flat_inputs + attn_out
    second_scale = lax.rsqrt(jnp.mean(residual * residual, axis=1) + EPSILON)
    mixed_in = (residual * second_scale[:, None] * second_gain[None, :]).astype(BF16)

    tokens_all = line_gather(mixed_in, ne, 3)
    routed_here = token_weight > 0.0
    marks = routed_here.astype(BF16)
    upper = (
        jnp.arange(tokens_dev, dtype=jnp.int32)[:, None]
        <= jnp.arange(tokens_dev, dtype=jnp.int32)[None, :]
    ).astype(BF16)
    order = dot("st,tu->su", marks, upper) - 1.0
    slots = jnp.arange(capacity, dtype=jnp.int32).astype(F32)
    hit = (order[:, None, :] == slots[None, :, None]) & routed_here[:, None, :]
    picker = hit.astype(BF16)
    slot_weight = jnp.sum(jnp.where(hit, token_weight[:, None, :], 0.0), axis=2).reshape(
        ne * capacity, 1
    )

    def pick(blocks):
        return dot("srt,std->srd", picker, blocks).reshape(ne * capacity, width)

    def unpick(rows):
        return dot("srt,srd->std", picker, rows.reshape(ne, capacity, width)).astype(BF16)

    rows_in = pick(tokens_all).astype(BF16)
    gate_pre = dot("rd,df->rf", rows_in, gate_rows)
    up_pre = dot("rd,df->rf", rows_in, up_rows)
    hidden = (jax.nn.silu(gate_pre) * up_pre).astype(BF16)
    result = (slot_weight * dot("rf,fd->rd", hidden, down_rows)).astype(BF16)
    routed_sum = line_scatter(unpick(result), 4)

    row_mixed = row_tokens(mixed_in)
    shared_pre = dot("td,kdf->ktf", row_mixed, shared_in)
    shared_hidden = (jax.nn.silu(shared_pre[0]) * shared_pre[1]).astype(BF16)
    shared_out = row_scatter(dot("tf,df->td", shared_hidden, shared_down))
    gate_value = jax.nn.sigmoid(
        jnp.sum(mixed_in.astype(F32) * gate_vector[None, :], axis=1)
    )

    block_total = residual + gate_value[:, None] * shared_out + routed_sum
    out_block = block_total.astype(BF16)[None]
    valid_mask = (own_segment < 2).astype(F32)
    valid_count = jnp.sum(lengths).astype(F32)
    dtotal = (
        total_tokens
        / valid_count
        * valid_mask[:, None]
        * (block_total - teacher[0].astype(F32))
    )

    dshared_out = (gate_value[:, None] * dtotal).astype(BF16)
    dlogit = jnp.sum(dtotal * shared_out, axis=1) * gate_value * (1.0 - gate_value)
    row_dout = row_tokens(dshared_out)
    shared_sigmoid = jax.nn.sigmoid(shared_pre[0])
    dshared_hidden = dot("td,df->tf", row_dout, shared_down)
    dshared_gate = (
        dshared_hidden * shared_pre[1] * shared_sigmoid * (1.0 + shared_pre[0] * (1.0 - shared_sigmoid))
    ).astype(BF16)
    dshared_up = (dshared_hidden * shared_pre[0] * shared_sigmoid).astype(BF16)
    dmixed_shared = row_scatter(
        dot("tf,df->td", dshared_gate, shared_in[0]) + dot("tf,df->td", dshared_up, shared_in[1])
    )

    def scatter_columns(term):
        return lax.psum_scatter(term.astype(BF16), "expert", scatter_dimension=0, tiled=True)

    grad_shared_down = scatter_columns(dot("td,tf->df", row_dout, shared_hidden))
    grad_shared_gates = scatter_columns(dot("td,tf->df", row_mixed, dshared_gate))
    grad_shared_ups = scatter_columns(dot("td,tf->df", row_mixed, dshared_up))

    dtotal_all = line_gather(dtotal.astype(BF16), ne, 5)
    dresult = (slot_weight * pick(dtotal_all)).astype(BF16)
    gate_sigmoid = jax.nn.sigmoid(gate_pre)
    activated = gate_pre * gate_sigmoid
    dhidden = dot("rd,fd->rf", dresult, down_rows)
    dgate = (dhidden * up_pre * gate_sigmoid * (1.0 + gate_pre * (1.0 - gate_sigmoid))).astype(BF16)
    dup = (dhidden * activated).astype(BF16)
    dreturn = (dot("rf,df->rd", dgate, gate_rows) + dot("rf,df->rd", dup, up_rows)).astype(BF16)
    grad_gate_term = dot("rd,rf->df", rows_in, dgate).astype(BF16)
    grad_up_term = dot("rd,rf->df", rows_in, dup).astype(BF16)
    grad_down_term = dot("rf,rd->fd", hidden, dresult).astype(BF16)
    dreturn, grad_gate_term, grad_up_term, grad_down_term = lax.optimization_barrier(
        (dreturn, grad_gate_term, grad_up_term, grad_down_term)
    )
    from_experts = line_scatter(unpick(dreturn), 6)
    grad_expert_down = scatter_shards(grad_down_term, f_index)[None]
    grad_expert_gate = scatter_shards(grad_gate_term, f_index)[None]
    grad_expert_up = scatter_shards(grad_up_term, f_index)[None]

    dmixed = dmixed_shared + dlogit[:, None] * gate_vector[None, :] + from_experts
    vector_term = jnp.sum(dlogit[:, None] * mixed_in.astype(F32), axis=0)
    dresidual_norm, second_gain_grad = norm_back(dmixed, residual, second_scale, second_gain)
    dresidual = dtotal + dresidual_norm
    dattn = dresidual.astype(BF16)
    row_dattn = row_tokens(dattn)

    dcontext = dot("td,dc->tc", row_dattn, mixer_out).astype(BF16)
    grad_mixer_out = scatter_columns(dot("td,tc->dc", row_dattn, context))
    dcontext = heads(dcontext)
    probabilities_again = jnp.exp(score() - log_total)
    dprobs = dot("qhd,khd->hqk", dcontext, values)
    delta_rows = jnp.sum(probabilities_again * dprobs, axis=2, keepdims=True)
    dscores = (probabilities_again * (dprobs - delta_rows)).astype(BF16)
    dqueries = dot("hqk,khd->qhd", dscores, keys) * score_factor
    dkeys = dot("hqk,qhd->khd", dscores, queries) * score_factor
    dvalues = dot("hqk,qhd->khd", probabilities_again.astype(BF16), dcontext)

    def back(incoming):
        return (incoming * cosine + turn_back(incoming * sine)).reshape(row_len, columns)

    dprojected = jnp.stack(
        [back(dqueries), back(dkeys), dvalues.reshape(row_len, columns)], axis=0
    ).astype(BF16)
    grad_mixer_in = lax.psum_scatter(
        dot("td,kte->kde", row_normed, dprojected).astype(BF16),
        "expert",
        scatter_dimension=1,
        tiled=True,
    )
    dnormed = row_scatter(dot("kte,kde->td", dprojected, mixer_in))
    dflat, first_gain_grad = norm_back(dnormed, flat_inputs, first_scale, first_gain)
    grad_input = (dresidual + dflat)[None]

    grad_mixer = jnp.concatenate([grad_mixer_in, grad_mixer_out[None]], axis=0)
    grad_mixer = jnp.transpose(grad_mixer, (1, 0, 2)).astype(F32)
    grad_shared = jnp.stack([grad_shared_gates, grad_shared_ups, grad_shared_down], axis=1)
    grad_shared = grad_shared.astype(F32)
    terms = jnp.stack([first_gain_grad, second_gain_grad, vector_term]).reshape(3, devices, piece)
    terms = jnp.pad(jnp.transpose(terms, (1, 0, 2)), ((0, 0), (0, 5), (0, 128 - piece)))
    sums = collect(terms)
    grad_gains = sums[:2, :piece]
    grad_shared_gate = sums[2, :piece]
    return (
        out_block,
        grad_input,
        grad_gains,
        grad_mixer,
        grad_shared,
        grad_shared_gate,
        grad_expert_gate,
        grad_expert_up,
        grad_expert_down,
    )


def solution(mesh):
    rows = P("expert", "fsdp", None)
    both = P(("fsdp", "expert"))
    gains = P(None, ("fsdp", "expert"))
    shared = P("expert", None, "fsdp")
    return jax.shard_map(
        on_device,
        mesh=mesh,
        in_specs=(rows, rows, P(), P(), rows, rows, gains, shared, shared, both, rows, rows, rows),
        out_specs=(rows, rows, gains, shared, shared, both, rows, rows, rows),
        check_vma=False,
    )
```

time: 1660 us -> 1000 us (0.60)
  waiting for transfers between devices: 1180 us -> 176 us
  Pallas kernels: 0 us -> 402 us
  blocking collectives: 121 us -> 0 us
  starting transfers between devices: 19.5 us -> 54 us
  local copies, waits for them, and re-layouts: 56.2 us -> 89.6 us
  other arithmetic: 76.4 us -> 58.3 us
    all_gather x9 -> x2, waiting for transfers between devices: 487 us -> 0.02 us  [the longest x1 0.02 us: on_device(): shared_down = lax.all_gather(shared_shard[2], 'expert', axis=0, tiled=True)]
    reduce_scatter x9 -> x5, waiting for transfers between devices: 415 us -> 0.01 us  [the longest x4 0.01 us: scatter_columns(): lax.psum_scatter(term.astype(BF16), 'expert', scatter_dimension=0, tiled=...]
    pallas_call x0 -> x6, Pallas kernels: none -> 402 us  [the longest x2 162 us: line_gather(): pl.pallas_call(functools.partial(line_gather_kernel, chips), out_shape=ja...]
    ppermute x0 -> x48, waiting for transfers between devices: none -> 176 us  [the longest x24 167 us: swap_y(): return lax.ppermute(values, 'fsdp', [(0, 2), (2, 0), (1, 3), (3, 1)])]
    all_to_all x4 -> x0, waiting for transfers between devices: 145 us -> none  [the longest x1 70.9 us: on_device(): lax.all_to_all(dsend.reshape(groups, capacity, model_width), 'expert', sp...]
    unnamed x20 -> x7, waiting for transfers between devices: 137 us -> 0.11 us
    unnamed x2 -> x0, blocking collectives: 77.1 us -> none
    ppermute x0 -> x48, starting transfers between devices: none -> 53.5 us  [the longest x24 28.4 us: swap_y(): return lax.ppermute(values, 'fsdp', [(0, 2), (2, 0), (1, 3), (3, 1)])]
  transfers between devices with their start and end apart: 23 -> 55, of which waited for: 17 -> 22; matrix products, arithmetic and copies ran while one was open for 14% -> 30% of each run, Pallas kernels for 0% -> 32%
where the time goes in v1:
time: 1000 us; the launch traced here: 990 us
  Pallas kernels  402 us (40%)
  matrix products  188 us (19%)
  waiting for transfers between devices  176 us (18%)
  local copies, waits for them, and re-layouts  89.6 us (9%)
  other arithmetic  58.3 us (6%)
  starting transfers between devices  54 us (5%)
  between operations  22 us (2%)
    dot_general x34, matrix products, dot(): return jnp.einsum(form, left, right, preferred_element_type=F32)  188 us
    ppermute x24, waiting for transfers between devices, swap_y(): return lax.ppermute(values, 'fsdp', [(0, 2), (2, 0), (1, 3), (3, 1)])  167 us
    pallas_call x2, Pallas kernels, line_gather(): pl.pallas_call(functools.partial(line_gather_kernel, chips), out_shape=ja...  162 us
    pallas_call x2, Pallas kernels, line_scatter(): pl.pallas_call(functools.partial(line_scatter_kernel, chips), out_shape=j...  144 us
    pallas_call x1, Pallas kernels, opening(): pl.pallas_call(functools.partial(opening_kernel, chips), out_shape=[jax.S...  86 us
    ppermute x24, starting transfers between devices, swap_y(): return lax.ppermute(values, 'fsdp', [(0, 2), (2, 0), (1, 3), (3, 1)])  28.4 us
    ppermute x24, starting transfers between devices, swap_x(): return lax.ppermute(values, 'fsdp', [(0, 1), (1, 0), (2, 3), (3, 2)])  25 us
    unnamed x172, local copies, waits for them, and re-layouts  24.4 us
  transfers between devices with their start and end apart: 55, of which 22 were waited for; matrix products, arithmetic and copies ran while one was open for 30% of the time, Pallas kernels for 32%

profile of v1, /device:TPU:0, one launch (start us, length us, event | category | flops | bytes accessed | tf_op | source)
XLA Modules:
  0.0 990.0 jit_solution(4920963305439443676)
XLA Ops:
  12.8 86.0 %opening.1 = (f32[8,2048]{1,0:T(8,128)S(1)}, f32[8,8,128]{2,1,0:T(8,128)S(1)}, bf16[4,128,2048]{2,1,0:T(8,128)(2,1)S(1)}, bf16[4,8,256,512]{3,2,1,0:T(8,128)(2,1)S(1)}, bf16[4,512,1408]{2,1,0:T(8,128)(2,1)S(1)}) custom-call(bf16[128,2048]{1,0:T(8,128)(2,1)S(1)} %bitcast.207, f32[8,128]{1,0:T(8,128)S(1)} %dynamic_update_slice.33.vector_ref, ...), custom_call_target="tpu_custom_call" | custom-call | tf_op jit(solution)/shard_map/opening/pallas_call | solution.py:340
  98.8 3.2 copy-done
  104.5 4.1 copy.65
  108.6 2.6 slice.402
  117.4 3.4 slice.313
  120.8 6.1 slice.304
  129.0 6.2 convolution_bitcast_fusion.2
  147.9 3.3 fusion.87
  155.9 2.9 broadcast_in_dim.65
  161.3 3.1 broadcast_in_dim.66
  165.6 16.3 %collective-permute-done = bf16[64,2048]{1,0:T(8,128)(2,1)S(1)} collective-permute-done((bf16[64,2048]{1,0:T(8,128)(2,1)S(1)}, bf16[64,2048]{1,0:T(8,128)(2,1)S(1)}, u32[]{:S(2)}, u32[]{:S(2)}) %collective-permute-start) | collective-permute-done | bytes 262176 | tf_op jit(solution)/shard_map/ppermute | solution.py:49
  186.8 10.0 %collective-permute-done.3 = bf16[128,2048]{1,0:T(8,128)(2,1)} collective-permute-done((bf16[128,2048]{1,0:T(8,128)(2,1)S(1)}, bf16[128,2048]{1,0:T(8,128)(2,1)}, u32[]{:S(2)}, u32[]{:S(2)}) %collective-permute-start.3) | collective-permute-done | bytes 524320 | tf_op jit(solution)/shard_map/ppermute | solution.py:49
  203.4 80.6 %line_gather3.1 = bf16[8,128,2048]{2,1,0:T(8,128)(2,1)} custom-call(bf16[128,2048]{1,0:T(8,128)(2,1)} %copy-done.12), custom_call_target="tpu_custom_call" | custom-call | tf_op jit(solution)/shard_map/line_gather3/pallas_call | solution.py:533
  284.0 3.4 convolution_convert_fusion.8
  287.5 8.5 fusion.91
  297.4 4.2 collective-permute-done.4
  313.0 2.6 constant_dynamic-update-slice_fusion.23
  315.6 2.6 constant_dynamic-update-slice_fusion.22
  319.8 2.6 constant_dynamic-update-slice_fusion.17
  325.5 3.8 collective-permute-done.14
  331.2 9.7 multiply_convert_fusion.3
  341.0 9.8 convolution_bitcast_fusion
  354.3 16.5 %fusion.88 = (bf16[512,2048]{1,0:T(8,128)(2,1)S(1)}, f32[512,2048]{1,0:T(8,128)S(1)}) fusion(bf16[512,1408]{0,1:T(8,128)(2,1)S(1)} %multiply_convert_fusion.7, bf16[1,2048,1408]{1,2,0:T(8,128)(2,1)} %all-gather.6.cloned.1.call-done), kind=kOutput, calls=%fused_computation.260 | convolution fusion | flops 2953838592 | bytes 13500416 | tf_op jit(solution)/shard_map/tf,df->td/dot_general | solution.py:41
  377.3 3.2 collective-permute-done.8
  381.3 7.9 multiply_convert_fusion
  389.2 3.3 convolution_convert_fusion.7.terms_ref
  392.5 54.8 %line_scatter4.1 = f32[128,2048]{1,0:T(8,128)} custom-call(bf16[8,128,2048]{2,1,0:T(8,128)(2,1)} %convolution_convert_fusion.7.terms_ref), custom_call_target="tpu_custom_call" | custom-call | tf_op jit(solution)/shard_map/line_scatter4/pallas_call | solution.py:661
  453.2 8.0 collective-permute-done.21
  465.5 4.3 collective-permute-done.22
  471.1 5.4 convolution_convert_fusion
  476.6 10.4 %multiply_convert_fusion.6 = (bf16[512,1408]{0,1:T(8,128)(2,1)S(1)}, bf16[512,1408]{0,1:T(8,128)(2,1)}) fusion(f32[2,512,1408]{1,2,0:T(8,128)} %copy-done.18, bf16[512,2048]{1,0:T(8,128)(2,1)} %copy-done.45, bf16[1,2048,1408]{1,2,0:T(8,128)(2,1)} %all-gather.6.cloned.1.call-done), kind=kOutput, calls=%fused_computation.46 | convolution fusion | flops 2962161664 | bytes 16515072 | tf_op jit(solution)/shard_map/td,df->tf/dot_general | solution.py:41
  488.0 5.3 convolution_convert_fusion.2
  494.5 81.5 %line_gather5.1 = bf16[8,128,2048]{2,1,0:T(8,128)(2,1)} custom-call(bf16[128,2048]{1,0:T(8,128)(2,1)} %get-tuple-element.130.block_ref), custom_call_target="tpu_custom_call" | custom-call | tf_op jit(solution)/shard_map/line_gather5/pallas_call | solution.py:533
  576.1 3.2 fusion.53
  579.7 12.8 %multiply_convert_fusion.1 = (bf16[768,1408]{1,0:T(8,128)(2,1)}, bf16[768,1408]{1,0:T(8,128)(2,1)}) fusion(f32[768,1408]{1,0:T(8,128)} %copy-done.68, f32[768,1408]{1,0:T(8,128)} %get-tuple-element.166, bf16[768,2048]{1,0:T(8,128)(2,1)S(1)} %fusion, bf16[1408,2048]{1,0:T(8,128)(2,1)} %constant_dynamic-update-slice_fusion.15), kind=kOutput, calls=%fused_computation.20 | convolution fusion | flops 4443242496 | bytes 21889024 | tf_op jit(solution)/shard_map/rd,fd->rf/dot_general | solution.py:41
  592.5 5.3 convolution_convert_fusion.1
  598.0 9.9 %convolution_convert_fusion.3 = bf16[1408,2048]{1,0:T(8,128)(2,1)} fusion(bf16[768,1408]{1,0:T(8,128)(2,1)} %get-tuple-element.165, bf16[768,2048]{1,0:T(8,128)(2,1)} %copy-done.26), kind=kOutput, calls=%fused_computation.4 | convolution fusion | flops 4432068608 | bytes 11075584 | tf_op jit(solution)/shard_map/rf,rd->fd/dot_general | solution.py:41
  607.9 7.3 convolution_convert_fusion.4
  615.2 5.1 fusion.92
  620.3 8.0 add_convert_fusion
  628.4 5.0 fusion.1
  633.4 5.5 fusion.89
  642.0 7.1 convolution_convert_fusion.5
  652.7 3.4 convolution_convert_fusion.6.terms_ref
  656.1 89.3 %line_scatter6.1 = f32[128,2048]{1,0:T(8,128)} custom-call(bf16[8,128,2048]{2,1,0:T(8,128)(2,1)} %convolution_convert_fusion.6.terms_ref), custom_call_target="tpu_custom_call" | custom-call | tf_op jit(solution)/shard_map/line_scatter6/pallas_call | solution.py:661
  745.5 3.0 multiply_reduce_fusion.1
  749.9 3.2 collective-permute-start.29
  754.5 9.7 collective-permute-done.29
  767.3 5.1 collective-permute-done.30
  776.5 3.0 convolution_convert_fusion.10
  781.5 3.3 multiply_reduce_fusion
  790.7 6.9 convert_bitcast_fusion
  808.0 10.9 %collective-permute-done.36 = bf16[256,1408]{1,0:T(8,128)(2,1)S(1)} collective-permute-done((bf16[256,1408]{1,0:T(8,128)(2,1)S(1)}, bf16[256,1408]{1,0:T(8,128)(2,1)S(1)}, u32[]{:S(2)}, u32[]{:S(2)}) %collective-permute-start.36) | collective-permute-done | bytes 720928 | tf_op jit(solution)/shard_map/ppermute | solution.py:49
  825.2 9.2 collective-permute-done.44
  840.9 8.9 collective-permute-done.40
  855.6 25.1 %collective-permute-done.39 = bf16[512,1408]{1,0:T(8,128)(2,1)S(1)} collective-permute-done((bf16[512,1408]{1,0:T(8,128)(2,1)}, bf16[512,1408]{1,0:T(8,128)(2,1)S(1)}, u32[]{:S(2)}, u32[]{:S(2)}) %collective-permute-start.39) | collective-permute-done | bytes 1441824 | tf_op jit(solution)/shard_map/ppermute | solution.py:49
  882.1 3.8 add_bitcast_fusion.2
  886.0 5.6 fusion.90
  892.6 47.2 %collective-permute-done.43 = bf16[512,1408]{1,0:T(8,128)(2,1)S(1)} collective-permute-done((bf16[512,1408]{1,0:T(8,128)(2,1)}, bf16[512,1408]{1,0:T(8,128)(2,1)S(1)}, u32[]{:S(2)}, u32[]{:S(2)}) %collective-permute-start.43) | collective-permute-done | bytes 1441824 | tf_op jit(solution)/shard_map/ppermute | solution.py:49
  942.2 3.4 add_bitcast_fusion.1
  950.4 4.6 add_bitcast_fusion
  960.3 10.1 %collect.1 = f32[8,128]{1,0:T(8,128)} custom-call(f32[32,8,128]{2,1,0:T(8,128)} %pad.4.terms_ref), custom_call_target="tpu_custom_call" | custom-call | tf_op jit(solution)/shard_map/collect/pallas_call | solution.py:410
  972.8 2.6 fusion.29
  975.5 3.9 maximum_convert_fusion
  (392 shorter events, 160.8 us)
Async XLA Ops:
  7.2 333.8 %all-gather.4.cloned.1.call-start = ((), (), s32[]{:S(2)}) async-start(), calls=%async_computation.5 | async-start | bytes 12976128 | tf_op jit(solution)/shard_map/all_gather | solution.py:729
  111.2 243.1 %all-gather.6.cloned.1.call-start = ((), (), s32[]{:S(2)}) async-start(), calls=%async_computation.11 | async-start | bytes 6488064 | tf_op jit(solution)/shard_map/all_gather | solution.py:730
  111.3 193.4 %collective-permute-start.13 = (bf16[512,1408]{1,0:T(8,128)(2,1)}, bf16[512,1408]{1,0:T(8,128)(2,1)}, u32[]{:S(2)}, u32[]{:S(2)}) collective-permute-start(bf16[512,1408]{1,0:T(8,128)(2,1)} %bitcast.241), channel_id=1, source_target_pairs={{0,16},{16,0},{8,24},{24,8},{1,17},{17,1},{9,25},{25,9},{2,18},{18... | collective-permute-start | bytes 4325384 | tf_op jit(solution)/shard_map/ppermute | solution.py:49
  112.2 194.4 %collective-permute-start.12 = (bf16[512,1408]{1,0:T(8,128)(2,1)}, bf16[512,1408]{1,0:T(8,128)(2,1)}, u32[]{:S(2)}, u32[]{:S(2)}) collective-permute-start(bf16[512,1408]{1,0:T(8,128)(2,1)} %bitcast.242), channel_id=1, source_target_pairs={{0,8},{8,0},{16,24},{24,16},{1,9},{9,1},{17,25},{25,17},{2,10},{10... | collective-permute-start | bytes 4325384 | tf_op jit(solution)/shard_map/ppermute | solution.py:45
  113.0 196.0 %collective-permute-start.17 = (bf16[352,2048]{1,0:T(8,128)(2,1)}, bf16[352,2048]{1,0:T(8,128)(2,1)}, u32[]{:S(2)}, u32[]{:S(2)}) collective-permute-start(bf16[352,2048]{1,0:T(8,128)(2,1)} %bitcast.244), channel_id=1, source_target_pairs={{0,16},{16,0},{8,24},{24,8},{1,17},{17,1},{9,25},{25,9},{2,18},{18... | collective-permute-start | bytes 4325384 | tf_op jit(solution)/shard_map/ppermute | solution.py:49
  151.3 14.3 %collective-permute-start.2 = (bf16[64,2048]{1,0:T(8,128)(2,1)S(1)}, bf16[64,2048]{1,0:T(8,128)(2,1)S(1)}, u32[]{:S(2)}, u32[]{:S(2)}) collective-permute-start(bf16[64,2048]{1,0:T(8,128)(2,1)S(1)} %get-tuple-element.124), channel_id=1, source_target_pairs={{0,8},{8,0},{16,24},{24,16},{1,9},{9,1},{17,25},{25,17},{2,10},{10... | collective-permute-start | bytes 786440 | tf_op jit(solution)/shard_map/ppermute | solution.py:45
  152.4 29.5 %collective-permute-start = (bf16[64,2048]{1,0:T(8,128)(2,1)S(1)}, bf16[64,2048]{1,0:T(8,128)(2,1)S(1)}, u32[]{:S(2)}, u32[]{:S(2)}) collective-permute-start(bf16[64,2048]{1,0:T(8,128)(2,1)S(1)} %get-tuple-element.125), channel_id=1, source_target_pairs={{0,16},{16,0},{8,24},{24,8},{1,17},{17,1},{9,25},{25,9},{2,18},{18... | collective-permute-start | bytes 786440 | tf_op jit(solution)/shard_map/ppermute | solution.py:49
  155.4 820.1 %reduce-scatter.14.cloned.1.call-start = ((), (), s32[]{:S(2)}) async-start(), calls=%async_computation.10 | async-start | bytes 6488064 | tf_op jit(solution)/shard_map/reduce_scatter | solution.py:848
  183.3 13.6 %collective-permute-start.3 = (bf16[128,2048]{1,0:T(8,128)(2,1)S(1)}, bf16[128,2048]{1,0:T(8,128)(2,1)}, u32[]{:S(2)}, u32[]{:S(2)}) collective-permute-start(bf16[128,2048]{1,0:T(8,128)(2,1)S(1)} %pad_maximum_fusion.10), channel_id=1, source_target_pairs={{0,16},{16,0},{8,24},{24,8},{1,17},{17,1},{9,25},{25,9},{2,18},{18... | collective-permute-start | bytes 1572872 | tf_op jit(solution)/shard_map/ppermute | solution.py:49
  185.1 13.5 %collective-permute-start.1 = (bf16[128,2048]{1,0:T(8,128)(2,1)}, bf16[128,2048]{1,0:T(8,128)(2,1)}, u32[]{:S(2)}, u32[]{:S(2)}) collective-permute-start(bf16[128,2048]{1,0:T(8,128)(2,1)} %pad_maximum_fusion.9), channel_id=1, source_target_pairs={{0,8},{8,0},{16,24},{24,16},{1,9},{9,1},{17,25},{25,17},{2,10},{10... | collective-permute-start | bytes 1572872 | tf_op jit(solution)/shard_map/ppermute | solution.py:45
  186.8 109.2 %copy-start.48 = (f32[1,2048]{1,0:T(1,128)}, f32[1,2048]{1,0:T(1,128)S(1)}, u32[]{:S(2)}) copy-start(f32[1,2048]{1,0:T(1,128)S(1)} %get-tuple-element.148) | copy-start | bytes 24580
  196.9 121.4 %collective-permute-start.16 = (bf16[352,2048]{1,0:T(8,128)(2,1)}, bf16[352,2048]{1,0:T(8,128)(2,1)S(1)}, u32[]{:S(2)}, u32[]{:S(2)}) collective-permute-start(bf16[352,2048]{1,0:T(8,128)(2,1)} %bitcast.245), channel_id=1, source_target_pairs={{0,8},{8,0},{16,24},{24,16},{1,9},{9,1},{17,25},{25,17},{2,10},{10... | collective-permute-start | bytes 4325384 | tf_op jit(solution)/shard_map/ppermute | solution.py:45
  202.0 85.4 %collective-permute-start.5 = (bf16[128,2048]{1,0:T(8,128)(2,1)S(1)}, bf16[128,2048]{1,0:T(8,128)(2,1)}, u32[]{:S(2)}, u32[]{:S(2)}) collective-permute-start(bf16[128,2048]{1,0:T(8,128)(2,1)S(1)} %get-tuple-element.73.block_ref), channel_id=1, source_target_pairs={{0,16},{16,0},{8,24},{24,8},{1,17},{17,1},{9,25},{25,9},{2,18},{18... | collective-permute-start | bytes 1572872 | tf_op jit(solution)/shard_map/ppermute | solution.py:49
  287.4 43.8 %copy-start.24 = (bf16[8,96,2048]{2,1,0:T(8,128)(2,1)}, bf16[8,96,2048]{2,1,0:T(8,128)(2,1)S(1)}, u32[]{:S(2)}) copy-start(bf16[8,96,2048]{2,1,0:T(8,128)(2,1)S(1)} %convolution_convert_fusion.8) | copy-start | bytes 9437188
  287.4 14.2 %collective-permute-start.4 = (bf16[128,2048]{1,0:T(8,128)(2,1)S(1)}, bf16[128,2048]{1,0:T(8,128)(2,1)S(1)}, u32[]{:S(2)}, u32[]{:S(2)}) collective-permute-start(bf16[128,2048]{1,0:T(8,128)(2,1)S(1)} %copy-done.13), channel_id=1, source_target_pairs={{0,8},{8,0},{16,24},{24,16},{1,9},{9,1},{17,25},{25,17},{2,10},{10... | collective-permute-start | bytes 1572872 | tf_op jit(solution)/shard_map/ppermute | solution.py:45
  301.6 23.1 %collective-permute-start.7 = (bf16[64,2048]{1,0:T(8,128)(2,1)S(1)}, bf16[64,2048]{1,0:T(8,128)(2,1)S(1)}, u32[]{:S(2)}, u32[]{:S(2)}) collective-permute-start(bf16[64,2048]{1,0:T(8,128)(2,1)S(1)} %slice.404), channel_id=1, source_target_pairs={{0,8},{8,0},{16,24},{24,16},{1,9},{9,1},{17,25},{25,17},{2,10},{10... | collective-permute-start | bytes 786440 | tf_op jit(solution)/shard_map/ppermute | solution.py:45
  304.7 18.6 %collective-permute-start.6 = (bf16[64,2048]{1,0:T(8,128)(2,1)S(1)}, bf16[64,2048]{1,0:T(8,128)(2,1)S(1)}, u32[]{:S(2)}, u32[]{:S(2)}) collective-permute-start(bf16[64,2048]{1,0:T(8,128)(2,1)S(1)} %slice.403), channel_id=1, source_target_pairs={{0,16},{16,0},{8,24},{24,8},{1,17},{17,1},{9,25},{25,9},{2,18},{18... | collective-permute-start | bytes 786440 | tf_op jit(solution)/shard_map/ppermute | solution.py:49
  306.7 23.5 %collective-permute-start.15 = (bf16[256,1408]{1,0:T(8,128)(2,1)S(1)}, bf16[256,1408]{1,0:T(8,128)(2,1)S(1)}, u32[]{:S(2)}, u32[]{:S(2)}) collective-permute-start(bf16[256,1408]{1,0:T(8,128)(2,1)S(1)} %slice.416), channel_id=1, source_target_pairs={{0,8},{8,0},{16,24},{24,16},{1,9},{9,1},{17,25},{25,17},{2,10},{10... | collective-permute-start | bytes 2162696 | tf_op jit(solution)/shard_map/ppermute | solution.py:45
  308.9 20.4 %collective-permute-start.14 = (bf16[256,1408]{1,0:T(8,128)(2,1)S(1)}, bf16[256,1408]{1,0:T(8,128)(2,1)S(1)}, u32[]{:S(2)}, u32[]{:S(2)}) collective-permute-start(bf16[256,1408]{1,0:T(8,128)(2,1)S(1)} %slice.415), channel_id=1, source_target_pairs={{0,16},{16,0},{8,24},{24,8},{1,17},{17,1},{9,25},{25,9},{2,18},{18... | collective-permute-start | bytes 2162696 | tf_op jit(solution)/shard_map/ppermute | solution.py:49
  318.2 56.5 %collective-permute-start.19 = (bf16[176,2048]{1,0:T(8,128)(2,1)}, bf16[176,2048]{1,0:T(8,128)(2,1)}, u32[]{:S(2)}, u32[]{:S(2)}) collective-permute-start(bf16[176,2048]{1,0:T(8,128)(2,1)} %slice.418), channel_id=1, source_target_pairs={{0,8},{8,0},{16,24},{24,16},{1,9},{9,1},{17,25},{25,17},{2,10},{10... | collective-permute-start | bytes 2162696 | tf_op jit(solution)/shard_map/ppermute | solution.py:45
  323.3 49.4 %collective-permute-start.18 = (bf16[176,2048]{1,0:T(8,128)(2,1)}, bf16[176,2048]{1,0:T(8,128)(2,1)}, u32[]{:S(2)}, u32[]{:S(2)}) collective-permute-start(bf16[176,2048]{1,0:T(8,128)(2,1)} %slice.417), channel_id=1, source_target_pairs={{0,16},{16,0},{8,24},{24,8},{1,17},{17,1},{9,25},{25,9},{2,18},{18... | collective-permute-start | bytes 2162696 | tf_op jit(solution)/shard_map/ppermute | solution.py:49
  370.9 6.4 collective-permute-start.10
  372.7 7.8 collective-permute-start.8
  380.7 66.6 %collective-permute-start.11 = (bf16[128,2048]{1,0:T(8,128)(2,1)S(1)}, bf16[128,2048]{1,0:T(8,128)(2,1)S(1)}, u32[]{:S(2)}, u32[]{:S(2)}) collective-permute-start(bf16[128,2048]{1,0:T(8,128)(2,1)S(1)} %pad_maximum_fusion.12), channel_id=1, source_target_pairs={{0,16},{16,0},{8,24},{24,8},{1,17},{17,1},{9,25},{25,9},{2,18},{18... | collective-permute-start | bytes 1572872 | tf_op jit(solution)/shard_map/ppermute | solution.py:49
  380.8 66.5 %collective-permute-start.9 = (bf16[128,2048]{1,0:T(8,128)(2,1)S(1)}, bf16[128,2048]{1,0:T(8,128)(2,1)S(1)}, u32[]{:S(2)}, u32[]{:S(2)}) collective-permute-start(bf16[128,2048]{1,0:T(8,128)(2,1)S(1)} %pad_maximum_fusion.11), channel_id=1, source_target_pairs={{0,8},{8,0},{16,24},{24,16},{1,9},{9,1},{17,25},{25,17},{2,10},{10... | collective-permute-start | bytes 1572872 | tf_op jit(solution)/shard_map/ppermute | solution.py:45
  392.5 54.8 %copy-start.15 = (bf16[1,128,2048]{2,1,0:T(8,128)(2,1)S(1)}, bf16[1,128,2048]{2,1,0:T(8,128)(2,1)}, u32[]{:S(2)}) copy-start(bf16[1,128,2048]{2,1,0:T(8,128)(2,1)} %param.14) | copy-start | bytes 1572868
  449.5 11.7 %collective-permute-start.21 = (bf16[128,2048]{1,0:T(8,128)(2,1)S(1)}, bf16[128,2048]{1,0:T(8,128)(2,1)S(1)}, u32[]{:S(2)}, u32[]{:S(2)}) collective-permute-start(bf16[128,2048]{1,0:T(8,128)(2,1)S(1)} %get-tuple-element.71), channel_id=1, source_target_pairs={{0,16},{16,0},{8,24},{24,8},{1,17},{17,1},{9,25},{25,9},{2,18},{18... | collective-permute-start | bytes 1572872 | tf_op jit(solution)/shard_map/ppermute | solution.py:49
  451.2 11.8 %collective-permute-start.20 = (bf16[128,2048]{1,0:T(8,128)(2,1)S(1)}, bf16[128,2048]{1,0:T(8,128)(2,1)S(1)}, u32[]{:S(2)}, u32[]{:S(2)}) collective-permute-start(bf16[128,2048]{1,0:T(8,128)(2,1)S(1)} %get-tuple-element.71), channel_id=1, source_target_pairs={{0,8},{8,0},{16,24},{24,16},{1,9},{9,1},{17,25},{25,17},{2,10},{10... | collective-permute-start | bytes 1572872 | tf_op jit(solution)/shard_map/ppermute | solution.py:45
  461.2 8.5 collective-permute-start.23
  463.1 6.6 collective-permute-start.22
  476.5 499.0 %reduce-scatter.10.cloned.1.call-start = ((), (), s32[]{:S(2)}) async-start(), calls=%async_computation.8 | async-start | bytes 6488064 | tf_op jit(solution)/shard_map/reduce_scatter | solution.py:848
  493.3 482.1 %reduce-scatter.12.cloned.1.call-start = ((), (), s32[]{:S(2)}) async-start(), calls=%async_computation.9 | async-start | bytes 6488064 | tf_op jit(solution)/shard_map/reduce_scatter | solution.py:848
  597.9 381.5 %reduce-scatter.8.cloned.1.call-start = ((), (), s32[]{:S(2)}) async-start(), calls=%async_computation.7 | async-start | bytes 2359296 | tf_op jit(solution)/shard_map/reduce_scatter | solution.py:848
  639.0 10.1 %collective-permute-start.26 = (bf16[64,2048]{1,0:T(8,128)(2,1)S(1)}, bf16[64,2048]{1,0:T(8,128)(2,1)S(1)}, u32[]{:S(2)}, u32[]{:S(2)}) collective-permute-start(bf16[64,2048]{1,0:T(8,128)(2,1)S(1)} %get-tuple-element.116), channel_id=1, source_target_pairs={{0,8},{8,0},{16,24},{24,16},{1,9},{9,1},{17,25},{25,17},{2,10},{10... | collective-permute-start | bytes 786440 | tf_op jit(solution)/shard_map/ppermute | solution.py:45
  640.6 8.5 collective-permute-start.24
  650.1 95.4 %collective-permute-start.27 = (bf16[128,2048]{1,0:T(8,128)(2,1)}, bf16[128,2048]{1,0:T(8,128)(2,1)S(1)}, u32[]{:S(2)}, u32[]{:S(2)}) collective-permute-start(bf16[128,2048]{1,0:T(8,128)(2,1)} %pad_maximum_fusion.14), channel_id=1, source_target_pairs={{0,16},{16,0},{8,24},{24,8},{1,17},{17,1},{9,25},{25,9},{2,18},{18... | collective-permute-start | bytes 1572872 | tf_op jit(solution)/shard_map/ppermute | solution.py:49
  651.9 93.5 %collective-permute-start.25 = (bf16[128,2048]{1,0:T(8,128)(2,1)}, bf16[128,2048]{1,0:T(8,128)(2,1)}, u32[]{:S(2)}, u32[]{:S(2)}) collective-permute-start(bf16[128,2048]{1,0:T(8,128)(2,1)} %pad_maximum_fusion.13), channel_id=1, source_target_pairs={{0,8},{8,0},{16,24},{24,16},{1,9},{9,1},{17,25},{25,17},{2,10},{10... | collective-permute-start | bytes 1572872 | tf_op jit(solution)/shard_map/ppermute | solution.py:45
  656.1 89.4 %copy-start.63 = (f32[128]{0:T(128)S(1)}, f32[128]{0:T(128)}, u32[]{:S(2)}) copy-start(f32[128]{0:T(128)} %copy-done.62) | copy-start | bytes 1540
  656.1 89.4 %copy-start.14 = (bf16[128,2048]{1,0:T(8,128)(2,1)S(1)}, bf16[128,2048]{1,0:T(8,128)(2,1)}, u32[]{:S(2)}) copy-start(bf16[128,2048]{1,0:T(8,128)(2,1)} %copy-done.12) | copy-start | bytes 1572868
  656.1 89.4 %copy-start.41 = (f32[1,2048]{1,0:T(1,128)S(1)}, f32[1,2048]{1,0:T(1,128)}, u32[]{:S(2)}) copy-start(f32[1,2048]{1,0:T(1,128)} %copy-done.40) | copy-start | bytes 24580
  656.1 89.4 %copy-start.49 = (f32[1,2048]{1,0:T(1,128)S(1)}, f32[1,2048]{1,0:T(1,128)}, u32[]{:S(2)}) copy-start(f32[1,2048]{1,0:T(1,128)} %copy-done.48) | copy-start | bytes 24580
  656.1 89.4 %copy-start.57 = (f32[128]{0:T(128)S(1)}, f32[128]{0:T(128)}, u32[]{:S(2)}) copy-start(f32[128]{0:T(128)} %copy-done.56) | copy-start | bytes 1540
  749.9 14.3 %collective-permute-start.29 = (bf16[128,2048]{1,0:T(8,128)(2,1)S(1)}, bf16[128,2048]{1,0:T(8,128)(2,1)S(1)}, u32[]{:S(2)}, u32[]{:S(2)}) collective-permute-start(bf16[128,2048]{1,0:T(8,128)(2,1)S(1)} %get-tuple-element.65), channel_id=1, source_target_pairs={{0,16},{16,0},{8,24},{24,8},{1,17},{17,1},{9,25},{25,9},{2,18},{18... | collective-permute-start | bytes 1572872 | tf_op jit(solution)/shard_map/ppermute | solution.py:49
  753.1 12.9 %collective-permute-start.28 = (bf16[128,2048]{1,0:T(8,128)(2,1)S(1)}, bf16[128,2048]{1,0:T(8,128)(2,1)S(1)}, u32[]{:S(2)}, u32[]{:S(2)}) collective-permute-start(bf16[128,2048]{1,0:T(8,128)(2,1)S(1)} %get-tuple-element.65), channel_id=1, source_target_pairs={{0,8},{8,0},{16,24},{24,16},{1,9},{9,1},{17,25},{25,17},{2,10},{10... | collective-permute-start | bytes 1572872 | tf_op jit(solution)/shard_map/ppermute | solution.py:45
  764.3 8.2 collective-permute-start.31
  766.0 6.4 collective-permute-start.30
  776.4 203.0 %reduce-scatter.6.cloned.1.call-start = ((), (), s32[]{:S(2)}) async-start(), calls=%async_computation.6 | async-start | bytes 7077888 | tf_op jit(solution)/shard_map/reduce_scatter | solution.py:897
  799.8 19.1 %collective-permute-start.36 = (bf16[256,1408]{1,0:T(8,128)(2,1)S(1)}, bf16[256,1408]{1,0:T(8,128)(2,1)S(1)}, u32[]{:S(2)}, u32[]{:S(2)}) collective-permute-start(bf16[256,1408]{1,0:T(8,128)(2,1)S(1)} %get-tuple-element.95), channel_id=1, source_target_pairs={{0,16},{16,0},{8,24},{24,8},{1,17},{17,1},{9,25},{25,9},{2,18},{18... | collective-permute-start | bytes 2162696 | tf_op jit(solution)/shard_map/ppermute | solution.py:49
  801.1 19.2 %collective-permute-start.38 = (bf16[256,1408]{1,0:T(8,128)(2,1)S(1)}, bf16[256,1408]{1,0:T(8,128)(2,1)S(1)}, u32[]{:S(2)}, u32[]{:S(2)}) collective-permute-start(bf16[256,1408]{1,0:T(8,128)(2,1)S(1)} %get-tuple-element.97), channel_id=1, source_target_pairs={{0,8},{8,0},{16,24},{24,16},{1,9},{9,1},{17,25},{25,17},{2,10},{10... | collective-permute-start | bytes 2162696 | tf_op jit(solution)/shard_map/ppermute | solution.py:45
  804.6 29.8 %collective-permute-start.44 = (bf16[176,2048]{1,0:T(8,128)(2,1)S(1)}, bf16[176,2048]{1,0:T(8,128)(2,1)S(1)}, u32[]{:S(2)}, u32[]{:S(2)}) collective-permute-start(bf16[176,2048]{1,0:T(8,128)(2,1)S(1)} %get-tuple-element.83), channel_id=1, source_target_pairs={{0,16},{16,0},{8,24},{24,8},{1,17},{17,1},{9,25},{25,9},{2,18},{18... | collective-permute-start | bytes 2162696 | tf_op jit(solution)/shard_map/ppermute | solution.py:49
  805.9 29.9 %collective-permute-start.46 = (bf16[176,2048]{1,0:T(8,128)(2,1)S(1)}, bf16[176,2048]{1,0:T(8,128)(2,1)S(1)}, u32[]{:S(2)}, u32[]{:S(2)}) collective-permute-start(bf16[176,2048]{1,0:T(8,128)(2,1)S(1)} %get-tuple-element.85), channel_id=1, source_target_pairs={{0,8},{8,0},{16,24},{24,16},{1,9},{9,1},{17,25},{25,17},{2,10},{10... | collective-permute-start | bytes 2162696 | tf_op jit(solution)/shard_map/ppermute | solution.py:45
  806.8 43.0 %collective-permute-start.40 = (bf16[256,1408]{1,0:T(8,128)(2,1)S(1)}, bf16[256,1408]{1,0:T(8,128)(2,1)S(1)}, u32[]{:S(2)}, u32[]{:S(2)}) collective-permute-start(bf16[256,1408]{1,0:T(8,128)(2,1)S(1)} %get-tuple-element.89), channel_id=1, source_target_pairs={{0,16},{16,0},{8,24},{24,8},{1,17},{17,1},{9,25},{25,9},{2,18},{18... | collective-permute-start | bytes 2162696 | tf_op jit(solution)/shard_map/ppermute | solution.py:49
  818.9 32.3 %collective-permute-start.42 = (bf16[256,1408]{1,0:T(8,128)(2,1)S(1)}, bf16[256,1408]{1,0:T(8,128)(2,1)S(1)}, u32[]{:S(2)}, u32[]{:S(2)}) collective-permute-start(bf16[256,1408]{1,0:T(8,128)(2,1)S(1)} %get-tuple-element.91), channel_id=1, source_target_pairs={{0,8},{8,0},{16,24},{24,16},{1,9},{9,1},{17,25},{25,17},{2,10},{10... | collective-permute-start | bytes 2162696 | tf_op jit(solution)/shard_map/ppermute | solution.py:45
  823.2 57.5 %collective-permute-start.39 = (bf16[512,1408]{1,0:T(8,128)(2,1)}, bf16[512,1408]{1,0:T(8,128)(2,1)S(1)}, u32[]{:S(2)}, u32[]{:S(2)}) collective-permute-start(bf16[512,1408]{1,0:T(8,128)(2,1)} %pad_maximum_fusion.2), channel_id=1, source_target_pairs={{0,16},{16,0},{8,24},{24,8},{1,17},{17,1},{9,25},{25,9},{2,18},{18... | collective-permute-start | bytes 4325384 | tf_op jit(solution)/shard_map/ppermute | solution.py:49
  834.4 47.8 %collective-permute-start.37 = (bf16[512,1408]{1,0:T(8,128)(2,1)}, bf16[512,1408]{1,0:T(8,128)(2,1)}, u32[]{:S(2)}, u32[]{:S(2)}) collective-permute-start(bf16[512,1408]{1,0:T(8,128)(2,1)} %pad_maximum_fusion.1), channel_id=1, source_target_pairs={{0,8},{8,0},{16,24},{24,16},{1,9},{9,1},{17,25},{25,17},{2,10},{10... | collective-permute-start | bytes 4325384 | tf_op jit(solution)/shard_map/ppermute | solution.py:45
  838.9 111.6 %collective-permute-start.47 = (bf16[352,2048]{1,0:T(8,128)(2,1)}, bf16[352,2048]{1,0:T(8,128)(2,1)}, u32[]{:S(2)}, u32[]{:S(2)}) collective-permute-start(bf16[352,2048]{1,0:T(8,128)(2,1)} %pad_maximum_fusion.6), channel_id=1, source_target_pairs={{0,16},{16,0},{8,24},{24,8},{1,17},{17,1},{9,25},{25,9},{2,18},{18... | collective-permute-start | bytes 4325384 | tf_op jit(solution)/shard_map/ppermute | solution.py:49
  849.8 100.6 %collective-permute-start.45 = (bf16[352,2048]{1,0:T(8,128)(2,1)}, bf16[352,2048]{1,0:T(8,128)(2,1)}, u32[]{:S(2)}, u32[]{:S(2)}) collective-permute-start(bf16[352,2048]{1,0:T(8,128)(2,1)} %pad_maximum_fusion.5), channel_id=1, source_target_pairs={{0,8},{8,0},{16,24},{24,16},{1,9},{9,1},{17,25},{25,17},{2,10},{10... | collective-permute-start | bytes 4325384 | tf_op jit(solution)/shard_map/ppermute | solution.py:45
  852.8 87.0 %collective-permute-start.43 = (bf16[512,1408]{1,0:T(8,128)(2,1)}, bf16[512,1408]{1,0:T(8,128)(2,1)S(1)}, u32[]{:S(2)}, u32[]{:S(2)}) collective-permute-start(bf16[512,1408]{1,0:T(8,128)(2,1)} %pad_maximum_fusion.4), channel_id=1, source_target_pairs={{0,16},{16,0},{8,24},{24,8},{1,17},{17,1},{9,25},{25,9},{2,18},{18... | collective-permute-start | bytes 4325384 | tf_op jit(solution)/shard_map/ppermute | solution.py:49
  880.7 61.5 %collective-permute-start.41 = (bf16[512,1408]{1,0:T(8,128)(2,1)}, bf16[512,1408]{1,0:T(8,128)(2,1)S(1)}, u32[]{:S(2)}, u32[]{:S(2)}) collective-permute-start(bf16[512,1408]{1,0:T(8,128)(2,1)} %pad_maximum_fusion.3), channel_id=1, source_target_pairs={{0,8},{8,0},{16,24},{24,16},{1,9},{9,1},{17,25},{25,17},{2,10},{10... | collective-permute-start | bytes 4325384 | tf_op jit(solution)/shard_map/ppermute | solution.py:45
  891.6 67.3 %copy-start.27 = (f32[512,2048]{1,0:T(8,128)}, f32[512,2048]{1,0:T(8,128)S(1)}, u32[]{:S(2)}) copy-start(f32[512,2048]{1,0:T(8,128)S(1)} %get-tuple-element.173) | copy-start | bytes 12582916
  891.7 53.9 %collective-permute-start.34 = (bf16[64,2048]{1,0:T(8,128)(2,1)S(1)}, bf16[64,2048]{1,0:T(8,128)(2,1)S(1)}, u32[]{:S(2)}, u32[]{:S(2)}) collective-permute-start(bf16[64,2048]{1,0:T(8,128)(2,1)S(1)} %get-tuple-element.112), channel_id=1, source_target_pairs={{0,8},{8,0},{16,24},{24,16},{1,9},{9,1},{17,25},{25,17},{2,10},{10... | collective-permute-start | bytes 786440 | tf_op jit(solution)/shard_map/ppermute | solution.py:45
  939.8 8.2 collective-permute-start.32
  948.2 9.2 collective-permute-start.35
  949.7 9.2 collective-permute-start.33
  (71 other events, 568.5 us)
Sparse Core Ops, SparseCore 0:
  111.3 117.4 all-gather.3
  231.0 75.4 all-gather.5
  476.6 84.6 reduce-scatter.13
  563.5 76.4 reduce-scatter.9
  642.1 96.9 reduce-scatter.11
  776.5 33.8 reduce-scatter.7
  812.8 68.3 reduce-scatter.5

commit v2 on v1

v2 whole, which is shorter than its diff:
```python
import functools

import jax
import jax.numpy as jnp
from jax import lax
from jax.experimental import pallas as pl
from jax.experimental.pallas import tpu as pltpu
from jax.sharding import PartitionSpec as P

HD = 128
TOP = 4
THETA = 1000000.0
EPSILON = 1e-06
NEG_LARGE = -1e30
MESH = pl.DeviceIdType.MESH
WIRE = pl.CostEstimate(flops=0, bytes_accessed=120_000_000, transcendentals=0)
F32 = jnp.float32
BF16 = jnp.bfloat16


def turn(values):
    half = values.shape[-1] // 2
    return jnp.concatenate([-values[..., half:], values[..., :half]], axis=-1)


def turn_back(values):
    half = values.shape[-1] // 2
    return jnp.concatenate([values[..., half:], -values[..., :half]], axis=-1)


def norm_back(incoming, values, scale_rows, gain_row):
    unit_rows = values * scale_rows[:, None]
    gain_grad = jnp.sum(incoming * unit_rows, axis=0)
    dunit = incoming * gain_row[None, :]
    back_rows = scale_rows[:, None] * (
        dunit - unit_rows * jnp.mean(dunit * unit_rows, axis=1, keepdims=True)
    )
    return (back_rows, gain_grad)


def dot(form, left, right):
    return jnp.einsum(form, left, right, preferred_element_type=F32)


def swap_x(values):
    return lax.ppermute(values, "fsdp", [(0, 1), (1, 0), (2, 3), (3, 2)])


def swap_y(values):
    return lax.ppermute(values, "fsdp", [(0, 2), (2, 0), (1, 3), (3, 1)])


def gather_sides(block):
    return [swap_x(block), swap_y(block)]


def gather_rest(block, sides):
    half = block.shape[0] // 2
    return [block, *sides, swap_y(sides[0][:half]), swap_x(sides[1][half:])]


def scatter_corner(parts):
    half = parts[0].shape[0] // 2
    return [swap_x(parts[3][:half].astype(BF16)), swap_y(parts[3][half:].astype(BF16))]


def scatter_sides(parts, corner):
    half = parts[0].shape[0] // 2
    low, high = corner
    to_y = jnp.concatenate(
        [(parts[2][:half].astype(F32) + low.astype(F32)).astype(BF16), parts[2][half:].astype(BF16)]
    )
    to_x = jnp.concatenate(
        [parts[1][:half].astype(BF16), (parts[1][half:].astype(F32) + high.astype(F32)).astype(BF16)]
    )
    return [swap_x(to_x), swap_y(to_y)]


def scatter_end(parts, sides):
    return parts[0].astype(F32) + sides[0].astype(F32) + sides[1].astype(F32)


def square_scatter(parts):
    return scatter_end(parts, scatter_sides(parts, scatter_corner(parts)))


def row_tokens(block):
    return jnp.concatenate(gather_rest(block, gather_sides(block)), axis=0)


def row_scatter(product):
    quarter = product.shape[0] // 4
    return square_scatter([product[j * quarter : (j + 1) * quarter] for j in range(4)])


def gather_shards(shard, sides, index):
    rows = shard.shape[0]
    half = rows // 2
    own, from_x, from_y, low, high = gather_rest(shard, sides)
    whole = jnp.zeros((4 * rows,) + shard.shape[1:], shard.dtype)
    for piece, start in (
        (own, index * rows),
        (from_x, (index ^ 1) * rows),
        (from_y, (index ^ 2) * rows),
        (low, (index ^ 3) * rows),
        (high, (index ^ 3) * rows + half),
    ):
        whole = lax.dynamic_update_slice(whole, piece, (start, 0))
    return whole


def scatter_terms(whole, index):
    rows = whole.shape[0] // 4
    return [lax.dynamic_slice_in_dim(whole, (index ^ j) * rows, rows) for j in range(4)]


def opening_kernel(
    chips,
    x_ref, vector_ref, routed_ref, mixer_ref, gate_ref,
    gains_ref, tables_ref, row_ref, mixers_ref, last_ref, gates_ref,
    vectors, send_v, receive_v, send_t, receive_t,
    send_n, receive_n, send_g, receive_g,
    up_sem, down_sem, in_low, in_high, to_partner, in_partner, local,
):
    nf, ne = lax.axis_size("fsdp"), lax.axis_size("expert")
    total = nf * ne
    f, e = lax.axis_index("fsdp"), lax.axis_index("expert")
    me = f * ne + e
    z, c = e // 2, lax.rem(e, 2)
    xn, yn = f ^ 1, f ^ 2
    up = (f, jnp.minimum(z + 1, chips - 1) * 2 + c)
    down = (f, jnp.maximum(z - 1, 0) * 2 + c)
    partner = (f, z * 2 + 1 - c)
    parts = ((pl.ds(0, 3), mixers_ref), (pl.ds(3, 1), last_ref))
    own_gate = pltpu.make_async_copy(gate_ref, gates_ref.at[f], local.at[2])
    own_mixer = [
        pltpu.make_async_copy(mixer_ref.at[span], ref.at[:, e], local.at[k])
        for k, (span, ref) in enumerate(parts)
    ]
    for copy in own_mixer + [own_gate]:
        copy.start()
    barrier = pltpu.get_barrier_semaphore()

    def greet(step, carry):
        peer = lax.rem(me + step, total)
        pl.semaphore_signal(
            barrier, inc=1, device_id=(peer // ne, lax.rem(peer, ne)), device_id_type=MESH
        )
        return carry

    lax.fori_loop(1, total, greet, 0)
    pl.semaphore_wait(barrier, total - 1)

    def remote(source, target, send, receive, device):
        return pltpu.make_async_remote_copy(
            src_ref=source,
            dst_ref=target,
            send_sem=send,
            recv_sem=receive,
            device_id=device,
            device_id_type=MESH,
        )

    def vector_copy(slot, peer):
        return remote(
            vector_ref, vectors.at[slot], send_v.at[peer], receive_v.at[slot],
            (peer // ne, lax.rem(peer, ne)),
        )

    def table_copy(slot, peer):
        return remote(routed_ref, tables_ref.at[slot], send_t.at[peer], receive_t.at[slot], (f, peer))

    def start_vector(step, carry):
        vector_copy(me, lax.rem(me + step, total)).start()
        return carry

    def start_table(step, carry):
        table_copy(e, lax.rem(e + step, ne)).start()
        return carry

    lax.fori_loop(1, total, start_vector, 0)
    lax.fori_loop(1, ne, start_table, 0)
    vectors[me] = vector_ref[...]
    tables_ref[e] = routed_ref[...]

    def shard(k, origin, target, send, receive, own):
        span, ref = parts[k]
        place = ref.at[:, origin * 2 + c]
        return remote(mixer_ref.at[span] if own else place, place, send, receive, target)

    def upward(k, origin, r, own=False):
        return shard(k, origin, up, up_sem.at[k, r], in_low.at[k, r], own)

    def downward(k, origin, r, own=False):
        return shard(k, origin, down, down_sem.at[k, r], in_high.at[k, r], own)

    def across(k, origin, own=False):
        return shard(k, origin, partner, to_partner.at[k, origin], in_partner.at[k, origin], own)

    for k in (0, 1):

        @pl.when(z < chips - 1)
        def _():
            upward(k, z, 0, True).start()

        @pl.when(z > 0)
        def _():
            downward(k, z, 0, True).start()

        across(k, z, True).start()

    def end_vector(step, carry):
        peer = lax.rem(me + step, total)
        vector_copy(peer, peer).wait_recv()
        return carry

    lax.fori_loop(1, total, end_vector, 0)
    blocks = gains_ref.shape[1] // 128
    per = total // blocks
    for block in range(blocks):
        gains_ref[:, block * 128 : (block + 1) * 128] = jnp.sum(
            vectors[block * per : (block + 1) * per], axis=0
        )
    half = x_ref.shape[0] // 2
    low, high = pl.ds(0, half), pl.ds(half, half)

    def piece(index, ref, origin, rows, device, slot):
        send, receive = (send_n, receive_n) if index == 0 else (send_g, receive_g)
        here, there = (origin ^ f, origin ^ device) if index == 0 else (origin, origin)
        return remote(
            ref.at[here, rows], ref.at[there, rows], send.at[slot], receive.at[slot], (device, e)
        )

    def arrived(index, ref, origin, rows, slot):
        send, receive = (send_n, receive_n) if index == 0 else (send_g, receive_g)
        place = ref.at[origin ^ f if index == 0 else origin, rows]
        return remote(place, place, send.at[slot], receive.at[slot], (xn, e))

    def outgoing(index, ref, first, second):
        return [
            piece(index, ref, f, first, xn, 0),
            piece(index, ref, f, second, yn, 1),
            piece(index, ref, f, second, xn, 2),
            piece(index, ref, f, first, yn, 3),
        ]

    def relays(index, ref, first, second):
        return [piece(index, ref, xn, first, yn, 4), piece(index, ref, yn, second, xn, 5)]

    for rows in (low, high):
        values = x_ref[rows].astype(F32)
        scale = lax.rsqrt(jnp.mean(values * values, axis=1, keepdims=True) + EPSILON)
        row_ref[0, rows] = (values * scale * gains_ref[0:1]).astype(BF16)
    own_gate.wait()
    row_out = outgoing(0, row_ref, low, high)
    row_relay = relays(0, row_ref, low, high)
    depth = gate_ref.shape[0] // 2
    first, second = pl.ds(0, depth), pl.ds(depth, depth)
    gate_out = outgoing(1, gates_ref, first, second)
    gate_relay = relays(1, gates_ref, first, second)
    for copy in row_out + gate_out:
        copy.start()
    arrived(0, row_ref, xn, low, 0).wait_recv()
    row_relay[0].start()
    arrived(0, row_ref, yn, high, 1).wait_recv()
    row_relay[1].start()

    def hop(r, carry):
        before, after = z - r, z + r
        for k in (0, 1):

            @pl.when(before >= 0)
            def _():
                upward(k, before, r - 1).wait_recv()

                @pl.when(z < chips - 1)
                def _():
                    upward(k, before, r).start()

                across(k, before).start()

            @pl.when(after < chips)
            def _():
                downward(k, after, r - 1).wait_recv()

                @pl.when(z > 0)
                def _():
                    downward(k, after, r).start()

                across(k, after).start()

        return carry

    lax.fori_loop(1, 3, hop, 0)
    arrived(1, gates_ref, xn, first, 0).wait_recv()
    gate_relay[0].start()
    arrived(1, gates_ref, yn, second, 1).wait_recv()
    gate_relay[1].start()
    lax.fori_loop(3, chips, hop, 0)

    for index, ref, (one, two) in ((0, row_ref, (low, high)), (1, gates_ref, (first, second))):
        arrived(index, ref, xn, two, 2).wait_recv()
        arrived(index, ref, yn, one, 3).wait_recv()
        arrived(index, ref, f ^ 3, one, 4).wait_recv()
        arrived(index, ref, f ^ 3, two, 5).wait_recv()
    for copy in row_out + gate_out + row_relay + gate_relay:
        copy.wait_send()
    for k in (0, 1):
        own_mixer[k].wait()

        @pl.when(z < chips - 1)
        def _():
            upward(k, z, 0, True).wait_send()

        @pl.when(z > 0)
        def _():
            downward(k, z, 0, True).wait_send()

    def finish(r, carry):
        before, after = z - r, z + r
        for k in (0, 1):

            @pl.when((before >= 0) & (z < chips - 1))
            def _():
                upward(k, before, r).wait_send()

            @pl.when((after < chips) & (z > 0))
            def _():
                downward(k, after, r).wait_send()

        return carry

    lax.fori_loop(1, chips, finish, 0)

    def shared(origin, carry):
        for k in (0, 1):
            across(k, origin).wait_send()
            across(k, origin).wait_recv()
        return carry

    lax.fori_loop(0, chips, shared, 0)

    def sent_vector(step, carry):
        peer = lax.rem(me + step, total)
        vector_copy(peer, peer).wait_send()
        return carry

    def end_table(step, carry):
        peer = lax.rem(e + step, ne)
        copy = table_copy(peer, peer)
        copy.wait_recv()
        copy.wait_send()
        return carry

    lax.fori_loop(1, total, sent_vector, 0)
    lax.fori_loop(1, ne, end_table, 0)


def opening(x, vector, routed, mixer, gate, nf):
    ne = routed.shape[0]
    chips, devices = ne // 2, nf * ne
    whole = pl.BlockSpec(memory_space=pltpu.VMEM)
    far = pl.BlockSpec(memory_space=pl.ANY)
    dma = pltpu.SemaphoreType.DMA
    return pl.pallas_call(
        functools.partial(opening_kernel, chips),
        out_shape=[
            jax.ShapeDtypeStruct((8, x.shape[1]), F32),
            jax.ShapeDtypeStruct((ne,) + routed.shape, F32),
            jax.ShapeDtypeStruct((nf,) + x.shape, BF16),
            jax.ShapeDtypeStruct((3, ne) + mixer.shape[1:], BF16),
            jax.ShapeDtypeStruct((1, ne) + mixer.shape[1:], BF16),
            jax.ShapeDtypeStruct((nf,) + gate.shape, BF16),
        ],
        in_specs=[whole] * 5,
        out_specs=[whole, whole, whole, far, far, far],
        scratch_shapes=[pltpu.VMEM((devices,) + vector.shape, F32)]
        + [dma((devices,))] * 2
        + [dma((ne,))] * 2
        + [dma((6,))] * 4
        + [dma((2, chips))] * 6
        + [dma((3,))],
        compiler_params=pltpu.CompilerParams(
            collective_id=1, has_side_effects=True, vmem_limit_bytes=24 * 1024 * 1024
        ),
        name="opening",
    )(x, vector, routed, mixer, gate)


def collect_kernel(terms_ref, sum_ref, arrived, send, receive):
    nf, ne = lax.axis_size("fsdp"), lax.axis_size("expert")
    total = nf * ne
    me = lax.axis_index("fsdp") * ne + lax.axis_index("expert")
    barrier = pltpu.get_barrier_semaphore()

    def greet(step, carry):
        peer = lax.rem(me + step, total)
        pl.semaphore_signal(
            barrier, inc=1, device_id=(peer // ne, lax.rem(peer, ne)), device_id_type=MESH
        )
        return carry

    lax.fori_loop(1, total, greet, 0)
    pl.semaphore_wait(barrier, total - 1)

    def copy_of(slot, peer):
        return pltpu.make_async_remote_copy(
            src_ref=terms_ref.at[peer],
            dst_ref=arrived.at[slot],
            send_sem=send.at[peer],
            recv_sem=receive.at[slot],
            device_id=(peer // ne, lax.rem(peer, ne)),
            device_id_type=MESH,
        )

    def begin(step, carry):
        copy_of(me, lax.rem(me + step, total)).start()
        return carry

    lax.fori_loop(1, total, begin, 0)
    arrived[me] = terms_ref[me]

    def end(step, carry):
        peer = lax.rem(me + step, total)
        copy = copy_of(peer, peer)
        copy.wait_recv()
        copy.wait_send()
        return carry

    lax.fori_loop(1, total, end, 0)
    sum_ref[...] = jnp.sum(arrived[...], axis=0)


def collect(terms):
    devices = terms.shape[0]
    return pl.pallas_call(
        collect_kernel,
        out_shape=jax.ShapeDtypeStruct(terms.shape[1:], terms.dtype),
        in_specs=[pl.BlockSpec(memory_space=pltpu.VMEM)],
        out_specs=pl.BlockSpec(memory_space=pltpu.VMEM),
        scratch_shapes=[pltpu.VMEM(terms.shape, terms.dtype)]
        + [pltpu.SemaphoreType.DMA((devices,))] * 2,
        compiler_params=pltpu.CompilerParams(collective_id=2, has_side_effects=True),
        name="collect",
    )(terms)


def places(chips):
    f, e = lax.axis_index("fsdp"), lax.axis_index("expert")
    z, c = e // 2, lax.rem(e, 2)
    up = (f, jnp.minimum(z + 1, chips - 1) * 2 + c)
    down = (f, jnp.maximum(z - 1, 0) * 2 + c)
    return f, e, z, c, up, down, (f, z * 2 + 1 - c), (f ^ 1, e), (f ^ 2, e)


def meet(chips, z, up, down, others):
    barrier = pltpu.get_barrier_semaphore()
    for peer in others:
        pl.semaphore_signal(barrier, inc=1, device_id=peer, device_id_type=MESH)

    @pl.when(z < chips - 1)
    def _():
        pl.semaphore_signal(barrier, inc=1, device_id=up, device_id_type=MESH)

    @pl.when(z > 0)
    def _():
        pl.semaphore_signal(barrier, inc=1, device_id=down, device_id_type=MESH)

    known = len(others) + jnp.where(z < chips - 1, 1, 0) + jnp.where(z > 0, 1, 0)
    pl.semaphore_wait(barrier, known)


def remote_copy(source, target, send, receive, device):
    return pltpu.make_async_remote_copy(
        src_ref=source,
        dst_ref=target,
        send_sem=send,
        recv_sem=receive,
        device_id=device,
        device_id_type=MESH,
    )


def spread_kernel(
    chips, block_ref, tokens_ref, all_ref, row_ref,
    up_sem, down_sem, in_low, in_high, to_partner, in_partner, send_n, receive_n, local,
):
    f, e, z, c, up, down, partner, side_x, side_y = places(chips)
    xn, yn = f ^ 1, f ^ 2
    own = [
        pltpu.make_async_copy(block_ref, all_ref.at[e], local.at[0]),
        pltpu.make_async_copy(tokens_ref, row_ref.at[0], local.at[1]),
    ]
    for copy in own:
        copy.start()
    meet(chips, z, up, down, (partner, side_x, side_y))

    def shard(origin, target, send, receive, first):
        place = all_ref.at[origin * 2 + c]
        return remote_copy(block_ref if first else place, place, send, receive, target)

    def upward(origin, r, first=False):
        return shard(origin, up, up_sem.at[r], in_low.at[r], first)

    def downward(origin, r, first=False):
        return shard(origin, down, down_sem.at[r], in_high.at[r], first)

    def across(origin, first=False):
        return shard(origin, partner, to_partner.at[origin], in_partner.at[origin], first)

    @pl.when(z < chips - 1)
    def _():
        upward(z, 0, True).start()

    @pl.when(z > 0)
    def _():
        downward(z, 0, True).start()

    across(z, True).start()
    half = tokens_ref.shape[0] // 2
    low, high = pl.ds(0, half), pl.ds(half, half)

    def piece(origin, rows, device, slot):
        source = tokens_ref.at[rows] if slot < 4 else row_ref.at[origin ^ f, rows]
        return remote_copy(
            source, row_ref.at[origin ^ device, rows], send_n.at[slot], receive_n.at[slot], (device, e)
        )

    def arrived(origin, rows, slot):
        place = row_ref.at[origin ^ f, rows]
        return remote_copy(place, place, send_n.at[slot], receive_n.at[slot], side_x)

    copies = [piece(f, low, xn, 0), piece(f, high, yn, 1), piece(f, high, xn, 2), piece(f, low, yn, 3)]
    relays = [piece(xn, low, yn, 4), piece(yn, high, xn, 5)]
    for copy in copies:
        copy.start()
    arrived(xn, low, 0).wait_recv()
    relays[0].start()
    arrived(yn, high, 1).wait_recv()
    relays[1].start()

    def hop(r, carry):
        before, after = z - r, z + r

        @pl.when(before >= 0)
        def _():
            upward(before, r - 1).wait_recv()

            @pl.when(z < chips - 1)
            def _():
                upward(before, r).start()

            across(before).start()

        @pl.when(after < chips)
        def _():
            downward(after, r - 1).wait_recv()

            @pl.when(z > 0)
            def _():
                downward(after, r).start()

            across(after).start()

        return carry

    lax.fori_loop(1, chips, hop, 0)
    arrived(xn, high, 2).wait_recv()
    arrived(yn, low, 3).wait_recv()
    arrived(f ^ 3, low, 4).wait_recv()
    arrived(f ^ 3, high, 5).wait_recv()
    for copy in copies + relays:
        copy.wait_send()
    for copy in own:
        copy.wait()

    @pl.when(z < chips - 1)
    def _():
        upward(z, 0, True).wait_send()

    @pl.when(z > 0)
    def _():
        downward(z, 0, True).wait_send()

    def finish(r, carry):
        before, after = z - r, z + r

        @pl.when((before >= 0) & (z < chips - 1))
        def _():
            upward(before, r).wait_send()

        @pl.when((after < chips) & (z > 0))
        def _():
            downward(after, r).wait_send()

        return carry

    lax.fori_loop(1, chips, finish, 0)

    def shared(origin, carry):
        across(origin).wait_send()
        across(origin).wait_recv()
        return carry

    lax.fori_loop(0, chips, shared, 0)


def spread(block, tokens, nf, ne, cid):
    chips = ne // 2
    dma = pltpu.SemaphoreType.DMA
    return pl.pallas_call(
        functools.partial(spread_kernel, chips),
        out_shape=[
            jax.ShapeDtypeStruct((ne,) + block.shape, block.dtype),
            jax.ShapeDtypeStruct((nf,) + tokens.shape, tokens.dtype),
        ],
        in_specs=[pl.BlockSpec(memory_space=pltpu.VMEM)] * 2,
        out_specs=[pl.BlockSpec(memory_space=pltpu.VMEM)] * 2,
        scratch_shapes=[dma((chips,))] * 6 + [dma((6,))] * 2 + [dma((2,))],
        compiler_params=pltpu.CompilerParams(
            collective_id=cid, has_side_effects=True, vmem_limit_bytes=40 * 1024 * 1024
        ),
        cost_estimate=WIRE,
        name=f"spread{cid}",
    )(block, tokens)


def combine_kernel(
    chips, terms_ref, parts_ref, sum_ref, row_sum_ref,
    theirs, going, coming, corner, onward, from_side,
    up_sem, down_sem, in_low, in_high, to_partner, in_partner, send_n, receive_n,
):
    f, e, z, c, up, down, partner, side_x, side_y = places(chips)
    meet(chips, z, up, down, (partner, side_x, side_y))

    def across(target):
        return remote_copy(
            terms_ref.at[target * 2 + 1 - c], theirs.at[target],
            to_partner.at[target], in_partner.at[target], partner,
        )

    def upward(target):
        return remote_copy(
            going.at[target], coming.at[target], up_sem.at[target], in_low.at[target], up
        )

    def downward(target, receiver):
        place = coming.at[jnp.where(target == receiver, chips, target)]
        return remote_copy(
            going.at[target], place, down_sem.at[target], in_high.at[target], down
        )

    def offer(r, carry):
        across(r).start()
        across(chips - 1 - r).start()
        return carry

    lax.fori_loop(0, chips // 2, offer, 0)
    half = parts_ref.shape[1] // 2
    low, high = pl.ds(0, half), pl.ds(half, half)

    def side(slot, source, target, device):
        return remote_copy(source, target, send_n.at[slot], receive_n.at[slot], device)

    copies = [
        side(0, parts_ref.at[3, low], corner.at[0], side_x),
        side(1, parts_ref.at[3, high], corner.at[1], side_y),
        side(2, parts_ref.at[1, low], from_side.at[0, low], side_x),
        side(3, parts_ref.at[2, high], from_side.at[1, high], side_y),
        side(4, onward.at[0], from_side.at[0, high], side_x),
        side(5, onward.at[1], from_side.at[1, low], side_y),
    ]
    for copy in copies[:4]:
        copy.start()

    def chip_term(target):
        return terms_ref[target * 2 + c].astype(F32) + theirs[target].astype(F32)

    def rise(r):
        target = chips - 1 - r

        @pl.when(target > z)
        def _():
            across(target).wait_recv()

            @pl.when(z > 0)
            def _():
                upward(target).wait_recv()
                going[target] = (chip_term(target) + coming[target].astype(F32)).astype(BF16)

            @pl.when(z == 0)
            def _():
                going[target] = chip_term(target).astype(BF16)

            upward(target).start()

    def fall(r):
        @pl.when(r < z)
        def _():
            across(r).wait_recv()

            @pl.when(z < chips - 1)
            def _():
                downward(r, z).wait_recv()
                going[r] = (chip_term(r) + coming[r].astype(F32)).astype(BF16)

            @pl.when(z == chips - 1)
            def _():
                going[r] = chip_term(r).astype(BF16)

            downward(r, z - 1).start()

    def pass_on(r, carry):
        @pl.when(z < chips // 2)
        def _():
            rise(r)

        fall(r)

        @pl.when(z >= chips // 2)
        def _():
            rise(r)

        return carry

    lax.fori_loop(0, 1, pass_on, 0)
    copies[1].wait_recv()
    onward[0] = (parts_ref[1, high].astype(F32) + corner[1].astype(F32)).astype(BF16)
    copies[4].start()
    copies[0].wait_recv()
    onward[1] = (parts_ref[2, low].astype(F32) + corner[0].astype(F32)).astype(BF16)
    copies[5].start()
    lax.fori_loop(1, chips, pass_on, 0)
    for copy in copies[2:]:
        copy.wait_recv()
    row_sum_ref[...] = (
        parts_ref[0].astype(F32) + from_side[0].astype(F32) + from_side[1].astype(F32)
    )
    across(z).wait_recv()
    sum_ref[...] = chip_term(z)

    @pl.when(z > 0)
    def _():
        upward(z).wait_recv()
        sum_ref[...] += coming[z].astype(F32)

    @pl.when(z < chips - 1)
    def _():
        downward(z, z).wait_recv()
        sum_ref[...] += coming[chips].astype(F32)

    for copy in copies:
        copy.wait_send()

    def finish(target, carry):
        across(target).wait_send()

        @pl.when(target > z)
        def _():
            upward(target).wait_send()

        @pl.when(target < z)
        def _():
            downward(target, z - 1).wait_send()

        return carry

    lax.fori_loop(0, chips, finish, 0)


def combine(terms, parts, cid):
    ne = terms.shape[0]
    chips = ne // 2
    parts = parts.reshape(4, parts.shape[0] // 4, parts.shape[1])
    block = terms.shape[1:]
    halves = (2, parts.shape[1] // 2, parts.shape[2])
    sides = (2,) + parts.shape[1:]
    dma = pltpu.SemaphoreType.DMA
    return pl.pallas_call(
        functools.partial(combine_kernel, chips),
        out_shape=[
            jax.ShapeDtypeStruct(terms.shape[1:], F32),
            jax.ShapeDtypeStruct(parts.shape[1:], F32),
        ],
        in_specs=[pl.BlockSpec(memory_space=pltpu.VMEM)] * 2,
        out_specs=[pl.BlockSpec(memory_space=pltpu.VMEM)] * 2,
        scratch_shapes=[pltpu.VMEM((chips,) + block, BF16)] * 2
        + [pltpu.VMEM((chips + 1,) + block, BF16)]
        + [pltpu.VMEM(halves, BF16)] * 2
        + [pltpu.VMEM(sides, BF16)]
        + [dma((chips,))] * 6
        + [dma((6,))] * 2,
        compiler_params=pltpu.CompilerParams(
            collective_id=cid, has_side_effects=True, vmem_limit_bytes=60 * 1024 * 1024
        ),
        cost_estimate=WIRE,
        name=f"combine{cid}",
    )(terms, parts)


def on_device(
    inputs,
    teacher,
    lengths,
    deal_order,
    routes,
    route_weights,
    norm_gains,
    mixer_weights,
    shared_weights,
    shared_gate,
    expert_gate,
    expert_up,
    expert_down,
):
    tokens_dev = inputs.shape[1]
    width = inputs.shape[2]
    nf = lax.axis_size("fsdp")
    ne = lax.axis_size("expert")
    devices = nf * ne
    row_len = tokens_dev * nf
    capacity = 3 * tokens_dev * TOP // (2 * ne)
    total_tokens = row_len * ne
    columns = mixer_weights.shape[2]
    heads_local = columns // HD
    f_index = lax.axis_index("fsdp")
    e_index = lax.axis_index("expert")

    piece = norm_gains.shape[1]
    slot = (f_index * ne + e_index) % (128 // piece)
    vector = jnp.concatenate([norm_gains, shared_gate[None]], axis=0).astype(F32)
    vector = lax.dynamic_update_slice(jnp.zeros((8, 128), F32), vector, (0, slot * piece))
    chosen = routes[0]
    weights_route = route_weights[0]
    expert_ids = jnp.arange(ne, dtype=jnp.int32)
    routed = jnp.sum(
        jnp.where(chosen.T[None] == expert_ids[:, None, None], weights_route.T[None], 0.0), axis=1
    )
    mixer_shard = jnp.transpose(mixer_weights, (1, 0, 2))
    gains, tables, row_blocks, mixer_in, mixer_out, gates = opening(
        inputs[0], vector, routed, mixer_shard, expert_gate[0], nf
    )
    first_gain, second_gain, gate_vector = gains[0], gains[1], gains[2]
    token_weight = lax.dynamic_index_in_dim(tables, e_index, axis=1, keepdims=False)
    mixer_in = mixer_in.reshape(3, width, columns)
    mixer_out = mixer_out.reshape(width, columns)
    gate_rows = gates.reshape(width, gates.shape[2])
    row_normed = row_blocks.reshape(row_len, width)

    shared_shard, up_shard, down_shard, gains = lax.optimization_barrier(
        (shared_weights, expert_up[0], expert_down[0], gains)
    )
    shared_shard = jnp.transpose(shared_shard, (1, 0, 2))
    shared_first = lax.all_gather(shared_shard[0], "expert", axis=0, tiled=True)
    up_sides = gather_sides(up_shard)

    first_len = lengths[deal_order[2 * e_index]]
    second_len = lengths[deal_order[2 * e_index + 1]]
    row_places = (
        (f_index ^ jnp.arange(nf, dtype=jnp.int32))[:, None] * tokens_dev
        + jnp.arange(tokens_dev, dtype=jnp.int32)[None]
    ).reshape(row_len)
    row_segment = (row_places >= first_len).astype(jnp.int32) + (
        row_places >= first_len + second_len
    ).astype(jnp.int32)
    row_position = (
        row_places
        - first_len * (row_segment >= 1).astype(jnp.int32)
        - second_len * (row_segment >= 2).astype(jnp.int32)
    )
    own_segment = row_segment[:tokens_dev]
    allowed = (row_segment[:, None] == row_segment[None, :]) & (
        row_places[None, :] <= row_places[:, None]
    )
    inverse = THETA ** (-(jnp.arange(HD // 2, dtype=F32) * 2.0) / HD)
    angles = row_position.astype(F32)[:, None] * inverse[None, :]
    cosine = jnp.concatenate([jnp.cos(angles)] * 2, axis=1)[:, None, :]
    sine = jnp.concatenate([jnp.sin(angles)] * 2, axis=1)[:, None, :]

    flat_inputs = inputs[0].astype(F32)
    first_scale = lax.rsqrt(jnp.mean(flat_inputs * flat_inputs, axis=1) + EPSILON)
    projected = dot("td,kde->kte", row_normed, mixer_in)

    def heads(values):
        return values.reshape(row_len, heads_local, HD)

    raw_query, raw_key = heads(projected[0]), heads(projected[1])
    queries = (raw_query * cosine + turn(raw_query) * sine).astype(BF16)
    keys = (raw_key * cosine + turn(raw_key) * sine).astype(BF16)
    values = heads(projected[2].astype(BF16))
    score_factor = HD ** (-0.5)

    def score():
        raw = dot("qhd,khd->hqk", queries, keys)
        return jnp.where(allowed[None], raw * score_factor, NEG_LARGE)

    scores = score()
    top_score = jnp.max(scores, axis=2, keepdims=True)
    shifted = jnp.exp(scores - top_score)
    row_total = jnp.sum(shifted, axis=2, keepdims=True)
    probabilities = shifted / row_total
    log_total = top_score + jnp.log(row_total)
    context = dot("hqk,khd->qhd", probabilities.astype(BF16), values)
    context = context.reshape(row_len, columns).astype(BF16)
    attn_out = row_scatter(dot("tc,dc->td", context, mixer_out))
    residual = flat_inputs + attn_out
    second_scale = lax.rsqrt(jnp.mean(residual * residual, axis=1) + EPSILON)
    mixed_in = (residual * second_scale[:, None] * second_gain[None, :]).astype(BF16)

    down_shard, mixed_in = lax.optimization_barrier((down_shard, mixed_in))
    up_rows = gather_shards(up_shard, up_sides, f_index)
    down_rows = gather_shards(down_shard, gather_sides(down_shard), f_index)
    tokens_all, row_mixed = spread(mixed_in, mixed_in, nf, ne, 3)
    row_mixed = row_mixed.reshape(row_len, width)
    second_shard, third_shard, tokens_all = lax.optimization_barrier(
        (shared_shard[1], shared_shard[2], tokens_all)
    )
    shared_second = lax.all_gather(second_shard, "expert", axis=0, tiled=True)
    shared_down = lax.all_gather(third_shard, "expert", axis=0, tiled=True)
    routed_here = token_weight > 0.0
    marks = routed_here.astype(BF16)
    upper = (
        jnp.arange(tokens_dev, dtype=jnp.int32)[:, None]
        <= jnp.arange(tokens_dev, dtype=jnp.int32)[None, :]
    ).astype(BF16)
    order = dot("st,tu->su", marks, upper) - 1.0
    slots = jnp.arange(capacity, dtype=jnp.int32).astype(F32)
    hit = (order[:, None, :] == slots[None, :, None]) & routed_here[:, None, :]
    picker = hit.astype(BF16)
    slot_weight = jnp.sum(jnp.where(hit, token_weight[:, None, :], 0.0), axis=2).reshape(
        ne * capacity, 1
    )

    def pick(blocks):
        return dot("srt,std->srd", picker, blocks).reshape(ne * capacity, width)

    def unpick(rows):
        return dot("srt,srd->std", picker, rows.reshape(ne, capacity, width)).astype(BF16)

    rows_in = pick(tokens_all).astype(BF16)
    gate_pre = dot("rd,df->rf", rows_in, gate_rows)
    up_pre = dot("rd,df->rf", rows_in, up_rows)
    hidden = (jax.nn.silu(gate_pre) * up_pre).astype(BF16)
    result = (slot_weight * dot("rf,fd->rd", hidden, down_rows)).astype(BF16)

    shared_pre = (dot("td,df->tf", row_mixed, shared_first), dot("td,df->tf", row_mixed, shared_second))
    shared_hidden = (jax.nn.silu(shared_pre[0]) * shared_pre[1]).astype(BF16)
    routed_sum, shared_out = combine(
        unpick(result), dot("tf,df->td", shared_hidden, shared_down).astype(BF16), 4
    )
    gate_value = jax.nn.sigmoid(
        jnp.sum(mixed_in.astype(F32) * gate_vector[None, :], axis=1)
    )

    block_total = residual + gate_value[:, None] * shared_out + routed_sum
    out_block = block_total.astype(BF16)[None]
    valid_mask = (own_segment < 2).astype(F32)
    valid_count = jnp.sum(lengths).astype(F32)
    dtotal = (
        total_tokens
        / valid_count
        * valid_mask[:, None]
        * (block_total - teacher[0].astype(F32))
    )

    dshared_out = (gate_value[:, None] * dtotal).astype(BF16)
    dlogit = jnp.sum(dtotal * shared_out, axis=1) * gate_value * (1.0 - gate_value)
    dtotal_all, row_dout = spread(dtotal.astype(BF16), dshared_out, nf, ne, 5)
    row_dout = row_dout.reshape(row_len, width)
    down_term = dot("td,tf->df", row_dout, shared_hidden).astype(BF16)
    row_dout, dtotal_all, down_term = lax.optimization_barrier((row_dout, dtotal_all, down_term))
    shared_sigmoid = jax.nn.sigmoid(shared_pre[0])
    dshared_hidden = dot("td,df->tf", row_dout, shared_down)
    dshared_gate = (
        dshared_hidden * shared_pre[1] * shared_sigmoid * (1.0 + shared_pre[0] * (1.0 - shared_sigmoid))
    ).astype(BF16)
    dshared_up = (dshared_hidden * shared_pre[0] * shared_sigmoid).astype(BF16)
    dmixed_terms = (
        dot("tf,df->td", dshared_gate, shared_first) + dot("tf,df->td", dshared_up, shared_second)
    ).astype(BF16)

    def scatter_columns(term):
        return lax.psum_scatter(term.astype(BF16), "expert", scatter_dimension=0, tiled=True)

    grad_shared_down = scatter_columns(down_term)
    gate_term = dot("td,tf->df", row_mixed, dshared_gate).astype(BF16)
    up_term = dot("td,tf->df", row_mixed, dshared_up).astype(BF16)

    dresult = (slot_weight * pick(dtotal_all)).astype(BF16)
    gate_sigmoid = jax.nn.sigmoid(gate_pre)
    activated = gate_pre * gate_sigmoid
    dhidden = dot("rd,fd->rf", dresult, down_rows)
    dgate = (dhidden * up_pre * gate_sigmoid * (1.0 + gate_pre * (1.0 - gate_sigmoid))).astype(BF16)
    dup = (dhidden * activated).astype(BF16)
    dreturn = (dot("rf,df->rd", dgate, gate_rows) + dot("rf,df->rd", dup, up_rows)).astype(BF16)
    grad_gate_term = dot("rd,rf->df", rows_in, dgate).astype(BF16)
    grad_down_term = dot("rf,rd->fd", hidden, dresult).astype(BF16)
    terms = [scatter_terms(term, f_index) for term in (grad_down_term, grad_gate_term)]
    corners = [scatter_corner(terms[0])]
    dreturned, up_term, gate_term, terms, corners = lax.optimization_barrier(
        (unpick(dreturn), up_term, gate_term, terms, corners)
    )
    grad_shared_gates = scatter_columns(gate_term)
    corners.append(scatter_corner(terms[1]))
    sides = [scatter_sides(terms[0], corners[0])]
    from_experts, dmixed_shared = combine(dreturned, dmixed_terms, 6)
    from_experts, up_term, corners, sides, grad_shared_down = lax.optimization_barrier(
        (from_experts, up_term, corners, sides, grad_shared_down)
    )
    grad_shared_ups = scatter_columns(up_term)

    dmixed = dmixed_shared + dlogit[:, None] * gate_vector[None, :] + from_experts
    vector_term = jnp.sum(dlogit[:, None] * mixed_in.astype(F32), axis=0)
    dresidual_norm, second_gain_grad = norm_back(dmixed, residual, second_scale, second_gain)
    dresidual = dtotal + dresidual_norm
    dattn = dresidual.astype(BF16)
    dattn, rows_again, dup = lax.optimization_barrier((dattn, rows_in, dup))
    row_dattn = row_tokens(dattn)
    grad_up_term = dot("rd,rf->df", rows_again, dup).astype(BF16)
    row_dattn, corners, grad_up_term, grad_shared_gates = lax.optimization_barrier(
        (row_dattn, corners, grad_up_term, grad_shared_gates)
    )
    sides.append(scatter_sides(terms[1], corners[1]))
    terms.append(scatter_terms(grad_up_term, f_index))
    corners.append(scatter_corner(terms[2]))

    dcontext = dot("td,dc->tc", row_dattn, mixer_out).astype(BF16)
    mixer_out_term = dot("td,tc->dc", row_dattn, context).astype(BF16)
    dcontext, mixer_out_term, sides = lax.optimization_barrier((dcontext, mixer_out_term, sides))
    dcontext = heads(dcontext)
    probabilities_again = jnp.exp(score() - log_total)
    dprobs = dot("qhd,khd->hqk", dcontext, values)
    delta_rows = jnp.sum(probabilities_again * dprobs, axis=2, keepdims=True)
    dscores = (probabilities_again * (dprobs - delta_rows)).astype(BF16)
    dqueries = dot("hqk,khd->qhd", dscores, keys) * score_factor
    dkeys = dot("hqk,qhd->khd", dscores, queries) * score_factor
    dvalues = dot("hqk,qhd->khd", probabilities_again.astype(BF16), dcontext)

    def back(incoming):
        return (incoming * cosine + turn_back(incoming * sine)).reshape(row_len, columns)

    dprojected = jnp.stack(
        [back(dqueries), back(dkeys), dvalues.reshape(row_len, columns)], axis=0
    ).astype(BF16)
    dprojected, grad_shared_ups, corners[2] = lax.optimization_barrier(
        (dprojected, grad_shared_ups, corners[2])
    )
    sides.append(scatter_sides(terms[2], corners[2]))
    mixer_term = dot("td,kte->kde", row_normed, dprojected).astype(BF16)
    mixer_term = jnp.concatenate([mixer_term, mixer_out_term[None]], axis=0)
    grad_mixer = lax.psum_scatter(mixer_term, "expert", scatter_dimension=1, tiled=True)
    dnormed = dot("kte,kde->td", dprojected, mixer_in).astype(BF16)
    dnormed, sides[2] = lax.optimization_barrier((row_scatter(dnormed), sides[2]))
    grad_expert_down, grad_expert_gate, grad_expert_up = [
        scatter_end(parts, side)[None] for parts, side in zip(terms, sides)
    ]
    dflat, first_gain_grad = norm_back(dnormed, flat_inputs, first_scale, first_gain)
    grad_input = (dresidual + dflat)[None]

    grad_shared = jnp.stack([grad_shared_gates, grad_shared_ups, grad_shared_down], axis=1)
    grad_shared = grad_shared.astype(F32)
    terms = jnp.stack([first_gain_grad, second_gain_grad, vector_term]).reshape(3, devices, piece)
    terms = jnp.pad(jnp.transpose(terms, (1, 0, 2)), ((0, 0), (0, 5), (0, 128 - piece)))
    sums = collect(terms)
    (grad_mixer, sums, grad_shared, grad_expert_down, grad_expert_gate, grad_expert_up) = (
        lax.optimization_barrier(
            (grad_mixer, sums, grad_shared, grad_expert_down, grad_expert_gate, grad_expert_up)
        )
    )
    grad_mixer = jnp.transpose(grad_mixer, (1, 0, 2)).astype(F32)
    grad_gains = sums[:2, :piece]
    grad_shared_gate = sums[2, :piece]
    return (
        out_block,
        grad_input,
        grad_gains,
        grad_mixer,
        grad_shared,
        grad_shared_gate,
        grad_expert_gate,
        grad_expert_up,
        grad_expert_down,
    )


def solution(mesh):
    rows = P("expert", "fsdp", None)
    both = P(("fsdp", "expert"))
    gains = P(None, ("fsdp", "expert"))
    shared = P("expert", None, "fsdp")
    return jax.shard_map(
        on_device,
        mesh=mesh,
        in_specs=(rows, rows, P(), P(), rows, rows, gains, shared, shared, both, rows, rows, rows),
        out_specs=(rows, rows, gains, shared, shared, both, rows, rows, rows),
        check_vma=False,
    )
```

time: 1000 us -> 828 us (0.83)
  Pallas kernels: 402 us -> 299 us
  matrix products: 188 us -> 165 us
  starting transfers between devices: 54 us -> 34 us
  waiting for transfers between devices: 176 us -> 161 us
  local copies, waits for them, and re-layouts: 89.6 us -> 79.5 us
    pallas_call x4, Pallas kernels: 306 us -> 204 us  [the longest x2 115 us: combine(): pl.pallas_call(functools.partial(combine_kernel, chips), out_shape=[jax.S...]
    ppermute x24 -> x16, waiting for transfers between devices: 167 us -> 106 us  [swap_y(): return lax.ppermute(values, 'fsdp', [(0, 2), (2, 0), (1, 3), (3, 1)])]
    ppermute x24 -> x16, waiting for transfers between devices: 8.9 us -> 40.2 us  [swap_x(): return lax.ppermute(values, 'fsdp', [(0, 1), (1, 0), (2, 3), (3, 2)])]
    dot_general x34 -> x35, matrix products: 188 us -> 165 us  [dot(): return jnp.einsum(form, left, right, preferred_element_type=F32)]
    reduce_scatter x1, waiting for transfers between devices: 0.01 us -> 14.7 us  [on_device(): lax.psum_scatter(mixer_term, 'expert', scatter_dimension=1, tiled=True)]
    unnamed x172 -> x219, local copies, waits for them, and re-layouts: 24.4 us -> 38.9 us
    slice x21 -> x16, local copies, waits for them, and re-layouts: 25.4 us -> 12.9 us  [the longest x3 5.32 us: scatter_sides(): parts[2][half:].astype(BF16)]
    ppermute x24 -> x16, starting transfers between devices: 28.4 us -> 16 us  [swap_y(): return lax.ppermute(values, 'fsdp', [(0, 2), (2, 0), (1, 3), (3, 1)])]
  transfers between devices with their start and end apart: 55 -> 39, of which waited for: 22 -> 17; matrix products, arithmetic and copies ran while one was open for 30% -> 28% of each run, Pallas kernels for 32% -> 16%
where the time goes in v2:
time: 828 us; the launch traced here: 818 us
  Pallas kernels  299 us (36%)
  matrix products  165 us (20%)
  waiting for transfers between devices  161 us (19%)
  local copies, waits for them, and re-layouts  79.5 us (10%)
  other arithmetic  57.1 us (7%)
  starting transfers between devices  34 us (4%)
  between operations  21.8 us (3%)
    dot_general x35, matrix products, dot(): return jnp.einsum(form, left, right, preferred_element_type=F32)  165 us
    pallas_call x2, Pallas kernels, combine(): pl.pallas_call(functools.partial(combine_kernel, chips), out_shape=[jax.S...  115 us
    ppermute x16, waiting for transfers between devices, swap_y(): return lax.ppermute(values, 'fsdp', [(0, 2), (2, 0), (1, 3), (3, 1)])  106 us
    pallas_call x2, Pallas kernels, spread(): pl.pallas_call(functools.partial(spread_kernel, chips), out_shape=[jax.Sh...  89.4 us
    pallas_call x1, Pallas kernels, opening(): pl.pallas_call(functools.partial(opening_kernel, chips), out_shape=[jax.S...  82 us
    ppermute x16, waiting for transfers between devices, swap_x(): return lax.ppermute(values, 'fsdp', [(0, 1), (1, 0), (2, 3), (3, 2)])  40.2 us
    unnamed x219, local copies, waits for them, and re-layouts  38.9 us
    ppermute x16, starting transfers between devices, swap_x(): return lax.ppermute(values, 'fsdp', [(0, 1), (1, 0), (2, 3), (3, 2)])  17.3 us
  transfers between devices with their start and end apart: 39, of which 17 were waited for; matrix products, arithmetic and copies ran while one was open for 28% of the time, Pallas kernels for 16%

profile of v2, /device:TPU:0, one launch (start us, length us, event | category | flops | bytes accessed | tf_op | source)
XLA Modules:
  0.0 817.9 jit_solution(17786451673682700789)
XLA Ops:
  12.8 82.0 %opening.1 = (f32[8,2048]{1,0:T(8,128)S(1)}, f32[8,8,128]{2,1,0:T(8,128)S(1)}, bf16[4,128,2048]{2,1,0:T(8,128)(2,1)S(1)}, bf16[3,8,256,512]{3,2,1,0:T(8,128)(2,1...) custom-call(bf16[128,2048]{1,0:T(8,128)(2,1)S(1)} %bitcast.188, ...), custom_call_target="tpu_custom_call" | custom-call | tf_op jit(solution)/shard_map/opening/pallas_call | solution.py:365
  94.8 2.6 copy-done.11
  97.4 2.5 copy-done.12
  105.9 6.6 convolution_bitcast_fusion
  129.1 7.4 collective-permute-done.2
  139.9 10.5 %collective-permute-done.3 = bf16[128,2048]{1,0:T(8,128)(2,1)S(1)} collective-permute-done((bf16[128,2048]{1,0:T(8,128)(2,1)S(1)}, bf16[128,2048]{1,0:T(8,128)(2,1)S(1)}, u32[]{:S(2)}, u32[]{:S(2)}) %collective-permute-start.3) | collective-permute-done | bytes 524320 | tf_op jit(solution)/shard_map/ppermute | solution.py:50
  152.9 44.2 %spread3.1 = (bf16[8,128,2048]{2,1,0:T(8,128)(2,1)S(1)}, bf16[4,128,2048]{2,1,0:T(8,128)(2,1)S(1)}) custom-call(bf16[128,2048]{1,0:T(8,128)(2,1)S(1)} %multiply_convert_fusion.9.block_ref.tokens_ref, bf16[128,2048]{1,0:T(8,128)(2,1)S(1)} %multiply_convert_fusion.9.block_ref.tokens_ref), custom_call_target="tpu_custom_call" | custom-call | bytes 120000000 | tf_op jit(solution)/shard_map/spread3/pallas_call | solution.py:611
  205.4 2.2 constant_dynamic-update-slice_fusion.14
  210.0 5.0 fusion.72
  217.9 17.8 %collective-permute-done.4 = bf16[512,1408]{1,0:T(8,128)(2,1)} collective-permute-done((bf16[512,1408]{1,0:T(8,128)(2,1)}, bf16[512,1408]{1,0:T(8,128)(2,1)}, u32[]{:S(2)}, u32[]{:S(2)}) %collective-permute-start.4) | collective-permute-done | bytes 1441824 | tf_op jit(solution)/shard_map/ppermute | solution.py:46
  243.5 36.2 %collective-permute-done.6 = bf16[256,1408]{1,0:T(8,128)(2,1)S(1)} collective-permute-done((bf16[256,1408]{1,0:T(8,128)(2,1)S(1)}, bf16[256,1408]{1,0:T(8,128)(2,1)S(1)}, u32[]{:S(2)}, u32[]{:S(2)}) %collective-permute-start.6) | collective-permute-done | bytes 720928 | tf_op jit(solution)/shard_map/ppermute | solution.py:50
  281.7 6.9 multiply_convert_fusion.3
  290.8 7.8 collective-permute-done.10
  298.8 7.4 collective-permute-done.11
  306.3 5.2 multiply_convert_fusion
  311.5 3.4 convolution_convert_fusion.7.terms_ref
  314.9 7.6 fusion.3
  322.5 8.1 multiply_convert_fusion.7
  330.6 7.9 convolution_convert_fusion.10
  338.5 43.6 %combine4.1 = (f32[128,2048]{1,0:T(8,128)}, f32[128,2048]{1,0:T(8,128)}) custom-call(bf16[8,128,2048]{2,1,0:T(8,128)(2,1)} %convolution_convert_fusion.7.terms_ref, bf16[4,128,2048]{2,1,0:T(8,128)(2,1)} %bitcast.227), custom_call_target="tpu_custom_call" | custom-call | bytes 120000000 | tf_op jit(solution)/shard_map/combine4/pallas_call | solution.py:779
  382.2 2.6 multiply_reduce_fusion.3
  385.7 45.2 %spread5.1 = (bf16[8,128,2048]{2,1,0:T(8,128)(2,1)S(1)}, bf16[4,128,2048]{2,1,0:T(8,128)(2,1)S(1)}) custom-call(bf16[128,2048]{1,0:T(8,128)(2,1)S(1)} %get-tuple-element.228.block_ref, bf16[128,2048]{1,0:T(8,128)(2,1)S(1)} %get-tuple-element.227.tokens_ref), custom_call_target="tpu_custom_call" | custom-call | bytes 120000000 | tf_op jit(solution)/shard_map/spread5/pallas_call | solution.py:611
  434.3 5.2 convolution_convert_fusion.5
  439.6 3.2 fusion.40
  444.9 5.4 convolution_convert_fusion.2
  450.3 2.5 copy-done.34
  454.8 11.4 %multiply_convert_fusion.1 = (bf16[768,1408]{1,0:T(8,128)(2,1)}, bf16[768,1408]{1,0:T(8,128)(2,1)}) fusion(f32[768,1408]{1,0:T(8,128)} %copy-done.90, f32[768,1408]{1,0:T(8,128)} %get-tuple-element.268, bf16[768,2048]{1,0:T(8,128)(2,1)} %copy-done.44, bf16[1408,2048]{1,0:T(8,128)(2,1)S(1)} %bitcast.214), kind=kOutput, calls=%fused_computation.16 | convolution fusion | flops 4443242496 | bytes 21889024 | tf_op jit(solution)/shard_map/rd,fd->rf/dot_general | solution.py:42
  466.3 6.8 fusion.73
  473.1 5.3 add_convert_fusion
  478.5 3.5 convolution_convert_fusion.6.terms_ref
  482.0 5.6 convolution_convert_fusion.1
  487.6 3.0 constant_dynamic-slice_fusion.6
  493.0 5.1 multiply_convert_fusion.5
  499.2 5.3 convolution_convert_fusion.3
  504.5 4.5 constant_dynamic-slice_fusion.11
  509.0 5.3 convolution_convert_fusion.4
  514.4 6.3 fusion.74
  526.2 2.1 collective-permute-start.17
  530.3 7.3 add_convert_fusion.1
  537.6 71.4 %combine6.1 = (f32[128,2048]{1,0:T(8,128)}, f32[128,2048]{1,0:T(8,128)}) custom-call(bf16[8,128,2048]{2,1,0:T(8,128)(2,1)} %convolution_convert_fusion.6.terms_ref, bf16[4,128,2048]{2,1,0:T(8,128)(2,1)} %bitcast.226), custom_call_target="tpu_custom_call" | custom-call | bytes 120000000 | tf_op jit(solution)/shard_map/combine6/pallas_call | solution.py:779
  612.4 2.1 slice.234
  614.6 2.4 multiply_reduce_fusion.1
  621.7 7.3 convolution_convert_fusion
  629.8 2.3 collective-permute-done.19
  637.0 3.4 collective-permute-done.20
  643.2 2.4 pad_maximum_fusion.5
  649.1 3.2 constant_dynamic-slice_fusion.4
  654.3 4.4 convolution_convert_fusion.9
  658.8 2.8 convolution_convert_fusion.11
  661.6 18.8 %collective-permute-done.23 = bf16[512,1408]{1,0:T(8,128)(2,1)} collective-permute-done((bf16[512,1408]{1,0:T(8,128)(2,1)}, bf16[512,1408]{1,0:T(8,128)(2,1)}, u32[]{:S(2)}, u32[]{:S(2)}) %collective-permute-start.23) | collective-permute-done | bytes 1441824 | tf_op jit(solution)/shard_map/ppermute | solution.py:50
  680.4 3.2 collective-permute-done.22
  683.8 3.9 copy.62
  687.7 3.3 multiply_reduce_fusion
  698.6 7.0 convert_bitcast_fusion
  705.7 6.9 pad_maximum_fusion
  714.5 4.0 add_bitcast_fusion.1
  718.5 7.3 bitcast_convert_fusion
  732.5 2.6 collective-permute-done.28
  737.5 4.2 add_bitcast_fusion.2
  741.7 2.4 maximum_convert_fusion
  744.1 26.9 %collective-permute-done.29 = bf16[128,2048]{1,0:T(8,128)(2,1)S(1)} collective-permute-done((bf16[128,2048]{1,0:T(8,128)(2,1)S(1)}, bf16[128,2048]{1,0:T(8,128)(2,1)S(1)}, u32[]{:S(2)}, u32[]{:S(2)}) %collective-permute-start.29) | collective-permute-done | bytes 524320 | tf_op jit(solution)/shard_map/ppermute | solution.py:50
  772.5 12.2 %collect.1 = f32[8,128]{1,0:T(8,128)} custom-call(f32[32,8,128]{2,1,0:T(8,128)} %pad.4.terms_ref), custom_call_target="tpu_custom_call" | custom-call | tf_op jit(solution)/shard_map/collect/pallas_call | solution.py:436
  786.1 4.3 add_bitcast_fusion
  790.4 14.7 %reduce-scatter.11.cloned.1.call-done = bf16[4,256,512]{1,2,0:T(8,128)(2,1)} async-done(((bf16[4,2048,512]{1,2,0:T(8,128)(2,1)}), bf16[4,256,512]{1,2,0:T(8,128)(2,1)}) %reduce-scatter.11.cloned.1.call-update) | async-done | bytes 1048592 | tf_op jit(solution)/shard_map/reduce_scatter | solution.py:1051
  (397 shorter events, 122.1 us)
Async XLA Ops:
  7.2 307.7 %all-gather.9.cloned.1.call-start = ((), (), s32[]{:S(2)}) async-start(), calls=%async_computation.10 | async-start | bytes 6488064 | tf_op jit(solution)/shard_map/all_gather | solution.py:854
  12.8 88.4 %copy-start.47 = (bf16[256,3,1408]{2,0,1:T(8,128)(2,1)S(1)}, bf16[256,3,1408]{2,0,1:T(8,128)(2,1)}, u32[]{:S(2)}) copy-start(bf16[256,3,1408]{2,0,1:T(8,128)(2,1)} %param.21) | copy-start | bytes 6488068
  101.2 25.2 %copy-start.8 = (bf16[1,8,256,512]{3,2,1,0:T(8,128)(2,1)}, bf16[1,8,256,512]{3,2,1,0:T(8,128)(2,1)S(1)}, u32[]{:S(2)}) copy-start(bf16[1,8,256,512]{3,2,1,0:T(8,128)(2,1)S(1)} %get-tuple-element.82) | copy-start | bytes 6291460
  102.7 219.9 %all-gather.5.cloned.1.call-start = ((), (), s32[]{:S(2)}) async-start(), calls=%async_computation.4 | async-start | bytes 6488064 | tf_op jit(solution)/shard_map/all_gather | solution.py:918
  127.7 23.1 %copy-start.4 = (bf16[1,128,2048]{2,1,0:T(8,128)(2,1)S(1)}, bf16[1,128,2048]{2,1,0:T(8,128)(2,1)}, u32[]{:S(2)}) copy-start(bf16[1,128,2048]{2,1,0:T(8,128)(2,1)} %param.13) | copy-start | bytes 1572868
  127.8 8.7 %collective-permute-start.2 = (bf16[64,2048]{1,0:T(8,128)(2,1)S(1)}, bf16[64,2048]{1,0:T(8,128)(2,1)S(1)}, u32[]{:S(2)}, u32[]{:S(2)}) collective-permute-start(bf16[64,2048]{1,0:T(8,128)(2,1)S(1)} %get-tuple-element.225), channel_id=1, source_target_pairs={{0,8},{8,0},{16,24},{24,16},{1,9},{9,1},{17,25},{25,17},{2,10},{10... | collective-permute-start | bytes 786440 | tf_op jit(solution)/shard_map/ppermute | solution.py:46
  128.5 8.4 %collective-permute-start = (bf16[64,2048]{1,0:T(8,128)(2,1)S(1)}, bf16[64,2048]{1,0:T(8,128)(2,1)S(1)}, u32[]{:S(2)}, u32[]{:S(2)}) collective-permute-start(bf16[64,2048]{1,0:T(8,128)(2,1)S(1)} %get-tuple-element.226), channel_id=1, source_target_pairs={{0,16},{16,0},{8,24},{24,8},{1,17},{17,1},{9,25},{25,9},{2,18},{18... | collective-permute-start | bytes 786440 | tf_op jit(solution)/shard_map/ppermute | solution.py:50
  137.0 13.3 %collective-permute-start.3 = (bf16[128,2048]{1,0:T(8,128)(2,1)S(1)}, bf16[128,2048]{1,0:T(8,128)(2,1)S(1)}, u32[]{:S(2)}, u32[]{:S(2)}) collective-permute-start(bf16[128,2048]{1,0:T(8,128)(2,1)S(1)} %pad_maximum_fusion.9), channel_id=1, source_target_pairs={{0,16},{16,0},{8,24},{24,8},{1,17},{17,1},{9,25},{25,9},{2,18},{18... | collective-permute-start | bytes 1572872 | tf_op jit(solution)/shard_map/ppermute | solution.py:50
  137.6 13.1 %collective-permute-start.1 = (bf16[128,2048]{1,0:T(8,128)(2,1)S(1)}, bf16[128,2048]{1,0:T(8,128)(2,1)S(1)}, u32[]{:S(2)}, u32[]{:S(2)}) collective-permute-start(bf16[128,2048]{1,0:T(8,128)(2,1)S(1)} %pad_maximum_fusion.8), channel_id=1, source_target_pairs={{0,8},{8,0},{16,24},{24,16},{1,9},{9,1},{17,25},{25,17},{2,10},{10... | collective-permute-start | bytes 1572872 | tf_op jit(solution)/shard_map/ppermute | solution.py:46
  139.9 77.8 %copy-start.68 = (f32[1,2048]{1,0:T(1,128)}, f32[1,2048]{1,0:T(1,128)S(1)}, u32[]{:S(2)}) copy-start(f32[1,2048]{1,0:T(1,128)S(1)} %get-tuple-element.252) | copy-start | bytes 24580
  151.7 52.6 %copy-start.75 = (f32[128]{0:T(128)}, f32[128]{0:T(128)S(1)}, u32[]{:S(2)}) copy-start(f32[128]{0:T(128)S(1)} %add_rsqrt_fusion.1) | copy-start | bytes 1540
  152.9 64.8 %copy-start = (bf16[128,2048]{1,0:T(8,128)(2,1)}, bf16[128,2048]{1,0:T(8,128)(2,1)S(1)}, u32[]{:S(2)}) copy-start(bf16[128,2048]{1,0:T(8,128)(2,1)S(1)} %multiply_convert_fusion.9.block_ref.tokens_ref) | copy-start | bytes 1572868
  199.1 131.4 %all-gather.7.cloned.1.call-start = ((), (), s32[]{:S(2)}) async-start(), calls=%async_computation.5 | async-start | bytes 6488064 | tf_op jit(solution)/shard_map/all_gather | solution.py:919
  199.2 38.1 %collective-permute-start.5 = (bf16[512,1408]{1,0:T(8,128)(2,1)}, bf16[512,1408]{1,0:T(8,128)(2,1)}, u32[]{:S(2)}, u32[]{:S(2)}) collective-permute-start(bf16[512,1408]{1,0:T(8,128)(2,1)} %bitcast.234), channel_id=1, source_target_pairs={{0,16},{16,0},{8,24},{24,8},{1,17},{17,1},{9,25},{25,9},{2,18},{18... | collective-permute-start | bytes 4325384 | tf_op jit(solution)/shard_map/ppermute | solution.py:50
  200.9 34.8 %collective-permute-start.4 = (bf16[512,1408]{1,0:T(8,128)(2,1)}, bf16[512,1408]{1,0:T(8,128)(2,1)}, u32[]{:S(2)}, u32[]{:S(2)}) collective-permute-start(bf16[512,1408]{1,0:T(8,128)(2,1)} %bitcast.235), channel_id=1, source_target_pairs={{0,8},{8,0},{16,24},{24,16},{1,9},{9,1},{17,25},{25,17},{2,10},{10... | collective-permute-start | bytes 4325384 | tf_op jit(solution)/shard_map/ppermute | solution.py:46
  202.5 406.6 %reduce-scatter.5.cloned.1.call-start = ((), (), s32[]{:S(2)}) async-start(), calls=%async_computation.6 | async-start | bytes 6488064 | tf_op jit(solution)/shard_map/reduce_scatter | solution.py:983
  204.9 179.8 %copy-start.77 = (f32[128]{0:T(128)}, f32[128]{0:T(128)S(1)}, u32[]{:S(2)}) copy-start(f32[128]{0:T(128)S(1)} %compare_select_fusion) | copy-start | bytes 1540
  207.6 81.1 %collective-permute-start.9 = (bf16[352,2048]{1,0:T(8,128)(2,1)}, bf16[352,2048]{1,0:T(8,128)(2,1)S(1)}, u32[]{:S(2)}, u32[]{:S(2)}) collective-permute-start(bf16[352,2048]{1,0:T(8,128)(2,1)} %bitcast.237), channel_id=1, source_target_pairs={{0,16},{16,0},{8,24},{24,8},{1,17},{17,1},{9,25},{25,9},{2,18},{18... | collective-permute-start | bytes 4325384 | tf_op jit(solution)/shard_map/ppermute | solution.py:50
  208.1 73.1 %collective-permute-start.8 = (bf16[352,2048]{1,0:T(8,128)(2,1)}, bf16[352,2048]{1,0:T(8,128)(2,1)S(1)}, u32[]{:S(2)}, u32[]{:S(2)}) collective-permute-start(bf16[352,2048]{1,0:T(8,128)(2,1)} %bitcast.238), channel_id=1, source_target_pairs={{0,8},{8,0},{16,24},{24,16},{1,9},{9,1},{17,25},{25,17},{2,10},{10... | collective-permute-start | bytes 4325384 | tf_op jit(solution)/shard_map/ppermute | solution.py:46
  209.3 72.4 %copy-start.41 = (bf16[8,96,2048]{2,1,0:T(8,128)(2,1)}, bf16[8,96,2048]{2,1,0:T(8,128)(2,1)S(1)}, u32[]{:S(2)}) copy-start(bf16[8,96,2048]{2,1,0:T(8,128)(2,1)S(1)} %convolution_convert_fusion.8) | copy-start | bytes 9437188
  215.0 66.7 %copy-start.90 = (f32[768,1408]{1,0:T(8,128)}, f32[768,1408]{1,0:T(8,128)S(1)}, u32[]{:S(2)}) copy-start(f32[768,1408]{1,0:T(8,128)S(1)} %fusion.72) | copy-start | bytes 12976132
  217.9 19.4 %copy-start.83 = (f32[128]{0:T(128)}, f32[128]{0:T(128)S(1)}, u32[]{:S(2)}) copy-start(f32[128]{0:T(128)S(1)} %fusion.21) | copy-start | bytes 1540
  236.9 42.8 %collective-permute-start.6 = (bf16[256,1408]{1,0:T(8,128)(2,1)S(1)}, bf16[256,1408]{1,0:T(8,128)(2,1)S(1)}, u32[]{:S(2)}, u32[]{:S(2)}) collective-permute-start(bf16[256,1408]{1,0:T(8,128)(2,1)S(1)} %slice.271), channel_id=1, source_target_pairs={{0,16},{16,0},{8,24},{24,8},{1,17},{17,1},{9,25},{25,9},{2,18},{18... | collective-permute-start | bytes 2162696 | tf_op jit(solution)/shard_map/ppermute | solution.py:50
  238.5 42.6 %collective-permute-start.7 = (bf16[256,1408]{1,0:T(8,128)(2,1)S(1)}, bf16[256,1408]{1,0:T(8,128)(2,1)S(1)}, u32[]{:S(2)}, u32[]{:S(2)}) collective-permute-start(bf16[256,1408]{1,0:T(8,128)(2,1)S(1)} %slice.272), channel_id=1, source_target_pairs={{0,8},{8,0},{16,24},{24,16},{1,9},{9,1},{17,25},{25,17},{2,10},{10... | collective-permute-start | bytes 2162696 | tf_op jit(solution)/shard_map/ppermute | solution.py:46
  281.2 17.4 %collective-permute-start.10 = (bf16[176,2048]{1,0:T(8,128)(2,1)S(1)}, bf16[176,2048]{1,0:T(8,128)(2,1)S(1)}, u32[]{:S(2)}, u32[]{:S(2)}) collective-permute-start(bf16[176,2048]{1,0:T(8,128)(2,1)S(1)} %slice.273), channel_id=1, source_target_pairs={{0,16},{16,0},{8,24},{24,8},{1,17},{17,1},{9,25},{25,9},{2,18},{18... | collective-permute-start | bytes 2162696 | tf_op jit(solution)/shard_map/ppermute | solution.py:50
  288.7 17.6 %copy-start.93 = (bf16[768,1408]{1,0:T(8,128)(2,1)}, bf16[768,1408]{1,0:T(8,128)(2,1)S(1)}, u32[]{:S(2)}) copy-start(bf16[768,1408]{1,0:T(8,128)(2,1)S(1)} %get-tuple-element.267) | copy-start | bytes 6488068
  288.7 17.5 %collective-permute-start.11 = (bf16[176,2048]{1,0:T(8,128)(2,1)S(1)}, bf16[176,2048]{1,0:T(8,128)(2,1)S(1)}, u32[]{:S(2)}, u32[]{:S(2)}) collective-permute-start(bf16[176,2048]{1,0:T(8,128)(2,1)S(1)} %slice.274), channel_id=1, source_target_pairs={{0,8},{8,0},{16,24},{24,16},{1,9},{9,1},{17,25},{25,17},{2,10},{10... | collective-permute-start | bytes 2162696 | tf_op jit(solution)/shard_map/ppermute | solution.py:46
  338.5 43.7 %copy-start.20 = (f32[128,2048]{1,0:T(8,128)S(1)}, f32[128,2048]{1,0:T(8,128)}, u32[]{:S(2)}) copy-start(f32[128,2048]{1,0:T(8,128)} %copy-done.19) | copy-start | bytes 3145732
  338.5 43.7 %copy-start.35 = (bf16[1,128,2048]{2,1,0:T(8,128)(2,1)S(1)}, bf16[1,128,2048]{2,1,0:T(8,128)(2,1)}, u32[]{:S(2)}) copy-start(bf16[1,128,2048]{2,1,0:T(8,128)(2,1)} %param.14) | copy-start | bytes 1572868
  384.7 49.5 %copy-start.87 = (bf16[512,1408]{1,0:T(8,128)(2,1)S(1)}, bf16[512,1408]{1,0:T(8,128)(2,1)}, u32[]{:S(2)}) copy-start(bf16[512,1408]{1,0:T(8,128)(2,1)} %get-tuple-element.269) | copy-start | bytes 4325380
  439.5 202.4 %reduce-scatter.7.cloned.1.call-start = ((), (), s32[]{:S(2)}) async-start(), calls=%async_computation.7 | async-start | bytes 6488064 | tf_op jit(solution)/shard_map/reduce_scatter | solution.py:983
  444.9 21.4 %slice-start.2 = ((s8[5767168]{0:T(1024)(128)(4,1)}), s8[4194304]{0:T(1024)(128)(4,1)S(1)}, s32[]{:S(2)}) async-start(s8[5767168]{0:T(1024)(128)(4,1)} %bitcast.198), calls=%async_computation.13 | async-start | bytes 8388608
  444.9 28.2 %slice-start.6 = ((s8[5767168]{0:T(1024)(128)(4,1)}), s8[4194304]{0:T(1024)(128)(4,1)S(1)}, s32[]{:S(2)}) async-start(s8[5767168]{0:T(1024)(128)(4,1)} %bitcast.215), calls=%async_computation.17 | async-start | bytes 8388608
  454.0 60.3 %collective-permute-start.13 = (bf16[176,2048]{1,0:T(8,128)(2,1)}, bf16[176,2048]{1,0:T(8,128)(2,1)}, u32[]{:S(2)}, u32[]{:S(2)}) collective-permute-start(bf16[176,2048]{1,0:T(8,128)(2,1)} %get-tuple-element.199), channel_id=1, source_target_pairs={{0,16},{16,0},{8,24},{24,8},{1,17},{17,1},{9,25},{25,9},{2,18},{18... | collective-permute-start | bytes 2162696 | tf_op jit(solution)/shard_map/ppermute | solution.py:50
  454.0 60.3 %collective-permute-start.12 = (bf16[176,2048]{1,0:T(8,128)(2,1)}, bf16[176,2048]{1,0:T(8,128)(2,1)}, u32[]{:S(2)}, u32[]{:S(2)}) collective-permute-start(bf16[176,2048]{1,0:T(8,128)(2,1)} %get-tuple-element.200), channel_id=1, source_target_pairs={{0,8},{8,0},{16,24},{24,16},{1,9},{9,1},{17,25},{25,17},{2,10},{10... | collective-permute-start | bytes 2162696 | tf_op jit(solution)/shard_map/ppermute | solution.py:46
  454.8 18.3 %slice-start.7 = ((s8[5767168]{0:T(1024)(128)(4,1)}), s8[1572864]{0:T(1024)(128)(4,1)S(1)}, s32[]{:S(2)}) async-start(s8[5767168]{0:T(1024)(128)(4,1)} %bitcast.215), calls=%async_computation.18 | async-start | bytes 3145728
  478.5 12.2 %slice-start.8 = ((s8[5767168]{0:T(1024)(128)(4,1)}), s8[4194304]{0:T(1024)(128)(4,1)S(1)}, s32[]{:S(2)}) async-start(s8[5767168]{0:T(1024)(128)(4,1)} %bitcast.262), calls=%async_computation.19 | async-start | bytes 8388608
  514.4 183.4 %reduce-scatter.9.cloned.1.call-start = ((), (), s32[]{:S(2)}) async-start(), calls=%async_computation.8 | async-start | bytes 6488064 | tf_op jit(solution)/shard_map/reduce_scatter | solution.py:983
  523.4 85.6 %collective-permute-start.16 = (bf16[352,2048]{1,0:T(8,128)(2,1)}, bf16[352,2048]{1,0:T(8,128)(2,1)}, u32[]{:S(2)}, u32[]{:S(2)}) collective-permute-start(bf16[352,2048]{1,0:T(8,128)(2,1)} %pad_maximum_fusion.2), channel_id=1, source_target_pairs={{0,8},{8,0},{16,24},{24,16},{1,9},{9,1},{17,25},{25,17},{2,10},{10... | collective-permute-start | bytes 4325384 | tf_op jit(solution)/shard_map/ppermute | solution.py:46
  526.2 82.9 %collective-permute-start.17 = (bf16[352,2048]{1,0:T(8,128)(2,1)S(1)}, bf16[352,2048]{1,0:T(8,128)(2,1)}, u32[]{:S(2)}, u32[]{:S(2)}) collective-permute-start(bf16[352,2048]{1,0:T(8,128)(2,1)S(1)} %pad_maximum_fusion.3), channel_id=1, source_target_pairs={{0,16},{16,0},{8,24},{24,8},{1,17},{17,1},{9,25},{25,9},{2,18},{18... | collective-permute-start | bytes 4325384 | tf_op jit(solution)/shard_map/ppermute | solution.py:50
  529.6 79.4 %collective-permute-start.15 = (bf16[256,1408]{1,0:T(8,128)(2,1)}, bf16[256,1408]{1,0:T(8,128)(2,1)S(1)}, u32[]{:S(2)}, u32[]{:S(2)}) collective-permute-start(bf16[256,1408]{1,0:T(8,128)(2,1)} %get-tuple-element.229), channel_id=1, source_target_pairs={{0,16},{16,0},{8,24},{24,8},{1,17},{17,1},{9,25},{25,9},{2,18},{18... | collective-permute-start | bytes 2162696 | tf_op jit(solution)/shard_map/ppermute | solution.py:50
  529.6 79.4 %collective-permute-start.14 = (bf16[256,1408]{1,0:T(8,128)(2,1)}, bf16[256,1408]{1,0:T(8,128)(2,1)S(1)}, u32[]{:S(2)}, u32[]{:S(2)}) collective-permute-start(bf16[256,1408]{1,0:T(8,128)(2,1)} %get-tuple-element.230), channel_id=1, source_target_pairs={{0,8},{8,0},{16,24},{24,16},{1,9},{9,1},{17,25},{25,17},{2,10},{10... | collective-permute-start | bytes 2162696 | tf_op jit(solution)/shard_map/ppermute | solution.py:46
  610.2 194.9 %reduce-scatter.11.cloned.1.call-start = ((), (), s32[]{:S(2)}) async-start(), calls=%async_computation.9 | async-start | bytes 9437184 | tf_op jit(solution)/shard_map/reduce_scatter | solution.py:1051
  618.6 13.4 %collective-permute-start.19 = (bf16[128,2048]{1,0:T(8,128)(2,1)S(1)}, bf16[128,2048]{1,0:T(8,128)(2,1)S(1)}, u32[]{:S(2)}, u32[]{:S(2)}) collective-permute-start(bf16[128,2048]{1,0:T(8,128)(2,1)S(1)} %get-tuple-element.113), channel_id=1, source_target_pairs={{0,16},{16,0},{8,24},{24,8},{1,17},{17,1},{9,25},{25,9},{2,18},{18... | collective-permute-start | bytes 1572872 | tf_op jit(solution)/shard_map/ppermute | solution.py:50
  620.1 13.3 %collective-permute-start.18 = (bf16[128,2048]{1,0:T(8,128)(2,1)S(1)}, bf16[128,2048]{1,0:T(8,128)(2,1)S(1)}, u32[]{:S(2)}, u32[]{:S(2)}) collective-permute-start(bf16[128,2048]{1,0:T(8,128)(2,1)S(1)} %get-tuple-element.113), channel_id=1, source_target_pairs={{0,8},{8,0},{16,24},{24,16},{1,9},{9,1},{17,25},{25,17},{2,10},{10... | collective-permute-start | bytes 1572872 | tf_op jit(solution)/shard_map/ppermute | solution.py:46
  628.9 12.9 %copy-start.28 = (bf16[512,1408]{1,0:T(8,128)(2,1)S(1)}, bf16[512,1408]{1,0:T(8,128)(2,1)}, u32[]{:S(2)}) copy-start(bf16[512,1408]{1,0:T(8,128)(2,1)} %get-tuple-element.124) | copy-start | bytes 4325380
  632.0 9.1 %collective-permute-start.21 = (bf16[64,2048]{1,0:T(8,128)(2,1)S(1)}, bf16[64,2048]{1,0:T(8,128)(2,1)S(1)}, u32[]{:S(2)}, u32[]{:S(2)}) collective-permute-start(bf16[64,2048]{1,0:T(8,128)(2,1)S(1)} %slice.277), channel_id=1, source_target_pairs={{0,8},{8,0},{16,24},{24,16},{1,9},{9,1},{17,25},{25,17},{2,10},{10... | collective-permute-start | bytes 786440 | tf_op jit(solution)/shard_map/ppermute | solution.py:46
  633.5 6.9 collective-permute-start.20
  645.6 34.8 %collective-permute-start.23 = (bf16[512,1408]{1,0:T(8,128)(2,1)}, bf16[512,1408]{1,0:T(8,128)(2,1)}, u32[]{:S(2)}, u32[]{:S(2)}) collective-permute-start(bf16[512,1408]{1,0:T(8,128)(2,1)} %pad_maximum_fusion.5), channel_id=1, source_target_pairs={{0,16},{16,0},{8,24},{24,8},{1,17},{17,1},{9,25},{25,9},{2,18},{18... | collective-permute-start | bytes 4325384 | tf_op jit(solution)/shard_map/ppermute | solution.py:50
  648.8 34.8 %collective-permute-start.22 = (bf16[512,1408]{1,0:T(8,128)(2,1)}, bf16[512,1408]{1,0:T(8,128)(2,1)}, u32[]{:S(2)}, u32[]{:S(2)}) collective-permute-start(bf16[512,1408]{1,0:T(8,128)(2,1)} %pad_maximum_fusion.4), channel_id=1, source_target_pairs={{0,8},{8,0},{16,24},{24,16},{1,9},{9,1},{17,25},{25,17},{2,10},{10... | collective-permute-start | bytes 4325384 | tf_op jit(solution)/shard_map/ppermute | solution.py:46
  652.3 45.5 %collective-permute-start.24 = (bf16[256,1408]{1,0:T(8,128)(2,1)}, bf16[256,1408]{1,0:T(8,128)(2,1)}, u32[]{:S(2)}, u32[]{:S(2)}) collective-permute-start(bf16[256,1408]{1,0:T(8,128)(2,1)} %get-tuple-element.197), channel_id=1, source_target_pairs={{0,8},{8,0},{16,24},{24,16},{1,9},{9,1},{17,25},{25,17},{2,10},{10... | collective-permute-start | bytes 2162696 | tf_op jit(solution)/shard_map/ppermute | solution.py:46
  654.0 43.8 %collective-permute-start.25 = (bf16[256,1408]{1,0:T(8,128)(2,1)}, bf16[256,1408]{1,0:T(8,128)(2,1)}, u32[]{:S(2)}, u32[]{:S(2)}) collective-permute-start(bf16[256,1408]{1,0:T(8,128)(2,1)} %get-tuple-element.198), channel_id=1, source_target_pairs={{0,16},{16,0},{8,24},{24,8},{1,17},{17,1},{9,25},{25,9},{2,18},{18... | collective-permute-start | bytes 2162696 | tf_op jit(solution)/shard_map/ppermute | solution.py:50
  661.6 26.1 %copy-start.49 = (bf16[1,512,512]{1,2,0:T(8,128)(2,1)S(1)}, bf16[1,512,512]{1,2,0:T(8,128)(2,1)}, u32[]{:S(2)}) copy-start(bf16[1,512,512]{1,2,0:T(8,128)(2,1)} %copy-done.48) | copy-start | bytes 1572868
  725.9 9.2 %collective-permute-start.28 = (bf16[64,2048]{1,0:T(8,128)(2,1)S(1)}, bf16[64,2048]{1,0:T(8,128)(2,1)S(1)}, u32[]{:S(2)}, u32[]{:S(2)}) collective-permute-start(bf16[64,2048]{1,0:T(8,128)(2,1)S(1)} %get-tuple-element.219), channel_id=1, source_target_pairs={{0,8},{8,0},{16,24},{24,16},{1,9},{9,1},{17,25},{25,17},{2,10},{10... | collective-permute-start | bytes 786440 | tf_op jit(solution)/shard_map/ppermute | solution.py:46
  726.0 9.2 %collective-permute-start.26 = (bf16[64,2048]{1,0:T(8,128)(2,1)S(1)}, bf16[64,2048]{1,0:T(8,128)(2,1)S(1)}, u32[]{:S(2)}, u32[]{:S(2)}) collective-permute-start(bf16[64,2048]{1,0:T(8,128)(2,1)S(1)} %get-tuple-element.220), channel_id=1, source_target_pairs={{0,16},{16,0},{8,24},{24,8},{1,17},{17,1},{9,25},{25,9},{2,18},{18... | collective-permute-start | bytes 786440 | tf_op jit(solution)/shard_map/ppermute | solution.py:50
  729.3 41.9 %collective-permute-start.30 = (bf16[512,1408]{1,0:T(8,128)(2,1)S(1)}, bf16[512,1408]{1,0:T(8,128)(2,1)}, u32[]{:S(2)}, u32[]{:S(2)}) collective-permute-start(bf16[512,1408]{1,0:T(8,128)(2,1)S(1)} %pad_maximum_fusion.6), channel_id=1, source_target_pairs={{0,8},{8,0},{16,24},{24,16},{1,9},{9,1},{17,25},{25,17},{2,10},{10... | collective-permute-start | bytes 4325384 | tf_op jit(solution)/shard_map/ppermute | solution.py:46
  730.4 40.8 %collective-permute-start.31 = (bf16[512,1408]{1,0:T(8,128)(2,1)S(1)}, bf16[512,1408]{1,0:T(8,128)(2,1)}, u32[]{:S(2)}, u32[]{:S(2)}) collective-permute-start(bf16[512,1408]{1,0:T(8,128)(2,1)S(1)} %pad_maximum_fusion.7), channel_id=1, source_target_pairs={{0,16},{16,0},{8,24},{24,8},{1,17},{17,1},{9,25},{25,9},{2,18},{18... | collective-permute-start | bytes 4325384 | tf_op jit(solution)/shard_map/ppermute | solution.py:50
  735.4 35.6 %collective-permute-start.29 = (bf16[128,2048]{1,0:T(8,128)(2,1)S(1)}, bf16[128,2048]{1,0:T(8,128)(2,1)S(1)}, u32[]{:S(2)}, u32[]{:S(2)}) collective-permute-start(bf16[128,2048]{1,0:T(8,128)(2,1)S(1)} %pad_maximum_fusion.11), channel_id=1, source_target_pairs={{0,16},{16,0},{8,24},{24,8},{1,17},{17,1},{9,25},{25,9},{2,18},{18... | collective-permute-start | bytes 1572872 | tf_op jit(solution)/shard_map/ppermute | solution.py:50
  736.6 34.4 %collective-permute-start.27 = (bf16[128,2048]{1,0:T(8,128)(2,1)S(1)}, bf16[128,2048]{1,0:T(8,128)(2,1)S(1)}, u32[]{:S(2)}, u32[]{:S(2)}) collective-permute-start(bf16[128,2048]{1,0:T(8,128)(2,1)S(1)} %pad_maximum_fusion.10), channel_id=1, source_target_pairs={{0,8},{8,0},{16,24},{24,16},{1,9},{9,1},{17,25},{25,17},{2,10},{10... | collective-permute-start | bytes 1572872 | tf_op jit(solution)/shard_map/ppermute | solution.py:46
  741.7 29.5 %copy-start.67 = (f32[1,2048]{1,0:T(1,128)S(1)}, f32[1,2048]{1,0:T(1,128)}, u32[]{:S(2)}) copy-start(f32[1,2048]{1,0:T(1,128)} %get-tuple-element.251) | copy-start | bytes 24580
  741.7 29.5 %copy-start.79 = (f32[128]{0:T(128)S(1)}, f32[128]{0:T(128)}, u32[]{:S(2)}) copy-start(f32[128]{0:T(128)} %add_rsqrt_fusion) | copy-start | bytes 1540
  744.1 27.1 %copy-start.5 = (bf16[1,128,2048]{2,1,0:T(8,128)(2,1)S(1)}, bf16[1,128,2048]{2,1,0:T(8,128)(2,1)}, u32[]{:S(2)}) copy-start(bf16[1,128,2048]{2,1,0:T(8,128)(2,1)} %param.13) | copy-start | bytes 1572868
  744.1 27.6 %copy-start.70 = (f32[1,32,64]{2,0,1:T(1,128)S(1)}, f32[1,32,64]{2,0,1:T(1,128)}, u32[]{:S(2)}) copy-start(f32[1,32,64]{2,0,1:T(1,128)} %stack.31) | copy-start | bytes 24580
  744.1 40.6 %copy-start.40 = (f32[128,2048]{1,0:T(8,128)S(1)}, f32[128,2048]{1,0:T(8,128)}, u32[]{:S(2)}) copy-start(f32[128,2048]{1,0:T(8,128)} %get-tuple-element.183) | copy-start | bytes 3145732
  (81 other events, 324.3 us)
Sparse Core Ops, SparseCore 0:
  102.8 61.0 all-gather.8
  199.3 58.9 all-gather.4
  259.9 59.0 all-gather.6
  439.6 62.9 reduce-scatter.4
  514.5 79.6 reduce-scatter.6
  610.2 67.5 reduce-scatter.8
  712.7 92.3 reduce-scatter.10

commit v3 on v2

--- a/solution.py
+++ b/solution.py
@@ -943,6 +943,7 @@
     hidden = (jax.nn.silu(gate_pre) * up_pre).astype(BF16)
     result = (slot_weight * dot("rf,fd->rd", hidden, down_rows)).astype(BF16)
 
+
     shared_pre = (dot("td,df->tf", row_mixed, shared_first), dot("td,df->tf", row_mixed, shared_second))
     shared_hidden = (jax.nn.silu(shared_pre[0]) * shared_pre[1]).astype(BF16)
     routed_sum, shared_out = combine(
@@ -975,9 +976,7 @@
         dshared_hidden * shared_pre[1] * shared_sigmoid * (1.0 + shared_pre[0] * (1.0 - shared_sigmoid))
     ).astype(BF16)
     dshared_up = (dshared_hidden * shared_pre[0] * shared_sigmoid).astype(BF16)
-    dmixed_terms = (
-        dot("tf,df->td", dshared_gate, shared_first) + dot("tf,df->td", dshared_up, shared_second)
-    ).astype(BF16)
+    dmixed_first = dot("tf,df->td", dshared_gate, shared_first)
 
     def scatter_columns(term):
         return lax.psum_scatter(term.astype(BF16), "expert", scatter_dimension=0, tiled=True)
@@ -989,20 +988,25 @@
     dresult = (slot_weight * pick(dtotal_all)).astype(BF16)
     gate_sigmoid = jax.nn.sigmoid(gate_pre)
     activated = gate_pre * gate_sigmoid
+    grad_down_term = dot("rf,rd->fd", hidden, dresult).astype(BF16)
+    dresult, grad_down_term = lax.optimization_barrier((dresult, grad_down_term))
+    terms = [scatter_terms(grad_down_term, f_index)]
+    corners = [scatter_corner(terms[0])]
     dhidden = dot("rd,fd->rf", dresult, down_rows)
     dgate = (dhidden * up_pre * gate_sigmoid * (1.0 + gate_pre * (1.0 - gate_sigmoid))).astype(BF16)
     dup = (dhidden * activated).astype(BF16)
     dreturn = (dot("rf,df->rd", dgate, gate_rows) + dot("rf,df->rd", dup, up_rows)).astype(BF16)
+    dreturn, corners = lax.optimization_barrier((dreturn, corners))
+    sides = [scatter_sides(terms[0], corners[0])]
     grad_gate_term = dot("rd,rf->df", rows_in, dgate).astype(BF16)
-    grad_down_term = dot("rf,rd->fd", hidden, dresult).astype(BF16)
-    terms = [scatter_terms(term, f_index) for term in (grad_down_term, grad_gate_term)]
-    corners = [scatter_corner(terms[0])]
-    dreturned, up_term, gate_term, terms, corners = lax.optimization_barrier(
-        (unpick(dreturn), up_term, gate_term, terms, corners)
+    terms.append(scatter_terms(grad_gate_term, f_index))
+    corners.append(scatter_corner(terms[1]))
+    dmixed_terms = (dmixed_first + dot("tf,df->td", dshared_up, shared_second)).astype(BF16)
+    dreturned, up_term, gate_term, corners = lax.optimization_barrier(
+        (unpick(dreturn), up_term, gate_term, corners)
     )
     grad_shared_gates = scatter_columns(gate_term)
-    corners.append(scatter_corner(terms[1]))
-    sides = [scatter_sides(terms[0], corners[0])]
+    sides.append(scatter_sides(terms[1], corners[1]))
     from_experts, dmixed_shared = combine(dreturned, dmixed_terms, 6)
     from_experts, up_term, corners, sides, grad_shared_down = lax.optimization_barrier(
         (from_experts, up_term, corners, sides, grad_shared_down)
@@ -1017,16 +1021,15 @@
     dattn, rows_again, dup = lax.optimization_barrier((dattn, rows_in, dup))
     row_dattn = row_tokens(dattn)
     grad_up_term = dot("rd,rf->df", rows_again, dup).astype(BF16)
-    row_dattn, corners, grad_up_term, grad_shared_gates = lax.optimization_barrier(
-        (row_dattn, corners, grad_up_term, grad_shared_gates)
-    )
-    sides.append(scatter_sides(terms[1], corners[1]))
+    row_dattn, grad_up_term, grad_shared_gates = lax.optimization_barrier(
+        (row_dattn, grad_up_term, grad_shared_gates)
+    )
     terms.append(scatter_terms(grad_up_term, f_index))
     corners.append(scatter_corner(terms[2]))
 
     dcontext = dot("td,dc->tc", row_dattn, mixer_out).astype(BF16)
     mixer_out_term = dot("td,tc->dc", row_dattn, context).astype(BF16)
-    dcontext, mixer_out_term, sides = lax.optimization_barrier((dcontext, mixer_out_term, sides))
+    dcontext, mixer_out_term = lax.optimization_barrier((dcontext, mixer_out_term))
     dcontext = heads(dcontext)
     probabilities_again = jnp.exp(score() - log_total)
     dprobs = dot("qhd,khd->hqk", dcontext, values)
@@ -1042,12 +1045,11 @@
     dprojected = jnp.stack(
         [back(dqueries), back(dkeys), dvalues.reshape(row_len, columns)], axis=0
     ).astype(BF16)
-    dprojected, grad_shared_ups, corners[2] = lax.optimization_barrier(
-        (dprojected, grad_shared_ups, corners[2])
-    )
+    dprojected, corners[2] = lax.optimization_barrier((dprojected, corners[2]))
     sides.append(scatter_sides(terms[2], corners[2]))
     mixer_term = dot("td,kte->kde", row_normed, dprojected).astype(BF16)
     mixer_term = jnp.concatenate([mixer_term, mixer_out_term[None]], axis=0)
+    mixer_term, grad_shared_ups = lax.optimization_barrier((mixer_term, grad_shared_ups))
     grad_mixer = lax.psum_scatter(mixer_term, "expert", scatter_dimension=1, tiled=True)
     dnormed = dot("kte,kde->td", dprojected, mixer_in).astype(BF16)
     dnormed, sides[2] = lax.optimization_barrier((row_scatter(dnormed), sides[2]))

time: 828 us -> 793 us (0.958)
  waiting for transfers between devices: 161 us -> 145 us
  local copies, waits for them, and re-layouts: 79.5 us -> 65 us
    ppermute x16, waiting for transfers between devices: 106 us -> 94.6 us  [swap_y(): return lax.ppermute(values, 'fsdp', [(0, 2), (2, 0), (1, 3), (3, 1)])]
    unnamed x219 -> x201, local copies, waits for them, and re-layouts: 38.9 us -> 36.1 us
  transfers between devices with their start and end apart: 39 -> 39, of which waited for: 17 -> 18; matrix products, arithmetic and copies ran while one was open for 28% -> 29% of each run, Pallas kernels for 16% -> 17%
where the time goes in v3:
time: 793 us; the launch traced here: 784 us
  Pallas kernels  303 us (38%)
  matrix products  161 us (20%)
  waiting for transfers between devices  145 us (18%)
  local copies, waits for them, and re-layouts  65 us (8%)
  other arithmetic  54.1 us (7%)
  starting transfers between devices  33.8 us (4%)
  between operations  22 us (3%)
    dot_general x35, matrix products, dot(): return jnp.einsum(form, left, right, preferred_element_type=F32)  161 us
    pallas_call x2, Pallas kernels, combine(): pl.pallas_call(functools.partial(combine_kernel, chips), out_shape=[jax.S...  119 us
    ppermute x16, waiting for transfers between devices, swap_y(): return lax.ppermute(values, 'fsdp', [(0, 2), (2, 0), (1, 3), (3, 1)])  94.6 us
    pallas_call x2, Pallas kernels, spread(): pl.pallas_call(functools.partial(spread_kernel, chips), out_shape=[jax.Sh...  89.3 us
    pallas_call x1, Pallas kernels, opening(): pl.pallas_call(functools.partial(opening_kernel, chips), out_shape=[jax.S...  82 us
    ppermute x16, waiting for transfers between devices, swap_x(): return lax.ppermute(values, 'fsdp', [(0, 1), (1, 0), (2, 3), (3, 2)])  41.3 us
    unnamed x201, local copies, waits for them, and re-layouts  36.1 us
    ppermute x16, starting transfers between devices, swap_x(): return lax.ppermute(values, 'fsdp', [(0, 1), (1, 0), (2, 3), (3, 2)])  18.4 us
  transfers between devices with their start and end apart: 39, of which 18 were waited for; matrix products, arithmetic and copies ran while one was open for 29% of the time, Pallas kernels for 17%

profile of v3, /device:TPU:0, one launch (start us, length us, event | category | flops | bytes accessed | tf_op | source)
XLA Modules:
  0.0 783.9 jit_solution(12515741099454233871)
XLA Ops:
  12.8 82.0 %opening.1 = (f32[8,2048]{1,0:T(8,128)S(1)}, f32[8,8,128]{2,1,0:T(8,128)S(1)}, bf16[4,128,2048]{2,1,0:T(8,128)(2,1)S(1)}, bf16[3,8,256,512]{3,2,1,0:T(8,128)(2,1...) custom-call(bf16[128,2048]{1,0:T(8,128)(2,1)S(1)} %bitcast.188, ...), custom_call_target="tpu_custom_call" | custom-call | tf_op jit(solution)/shard_map/opening/pallas_call | solution.py:365
  94.8 2.6 copy-done.11
  97.4 2.5 copy-done.12
  105.9 6.6 convolution_bitcast_fusion
  129.1 7.4 collective-permute-done.2
  139.9 10.5 %collective-permute-done.3 = bf16[128,2048]{1,0:T(8,128)(2,1)S(1)} collective-permute-done((bf16[128,2048]{1,0:T(8,128)(2,1)S(1)}, bf16[128,2048]{1,0:T(8,128)(2,1)S(1)}, u32[]{:S(2)}, u32[]{:S(2)}) %collective-permute-start.3) | collective-permute-done | bytes 524320 | tf_op jit(solution)/shard_map/ppermute | solution.py:50
  152.9 44.2 %spread3.1 = (bf16[8,128,2048]{2,1,0:T(8,128)(2,1)S(1)}, bf16[4,128,2048]{2,1,0:T(8,128)(2,1)S(1)}) custom-call(bf16[128,2048]{1,0:T(8,128)(2,1)S(1)} %multiply_convert_fusion.9.block_ref.tokens_ref, bf16[128,2048]{1,0:T(8,128)(2,1)S(1)} %multiply_convert_fusion.9.block_ref.tokens_ref), custom_call_target="tpu_custom_call" | custom-call | bytes 120000000 | tf_op jit(solution)/shard_map/spread3/pallas_call | solution.py:611
  197.1 2.0 copy-done.6
  205.2 2.1 constant_dynamic-update-slice_fusion.14
  209.8 5.0 fusion.71
  217.7 18.1 %collective-permute-done.4 = bf16[512,1408]{1,0:T(8,128)(2,1)} collective-permute-done((bf16[512,1408]{1,0:T(8,128)(2,1)}, bf16[512,1408]{1,0:T(8,128)(2,1)}, u32[]{:S(2)}, u32[]{:S(2)}) %collective-permute-start.4) | collective-permute-done | bytes 1441824 | tf_op jit(solution)/shard_map/ppermute | solution.py:46
  243.5 36.2 %collective-permute-done.6 = bf16[256,1408]{1,0:T(8,128)(2,1)S(1)} collective-permute-done((bf16[256,1408]{1,0:T(8,128)(2,1)S(1)}, bf16[256,1408]{1,0:T(8,128)(2,1)S(1)}, u32[]{:S(2)}, u32[]{:S(2)}) %collective-permute-start.6) | collective-permute-done | bytes 720928 | tf_op jit(solution)/shard_map/ppermute | solution.py:50
  281.7 7.2 multiply_convert_fusion.3
  291.1 7.6 collective-permute-done.10
  298.8 7.7 collective-permute-done.11
  306.5 5.2 multiply_convert_fusion
  311.8 3.4 convolution_convert_fusion.7.terms_ref
  315.2 7.6 fusion.3
  322.8 8.1 %multiply_convert_fusion.7 = (bf16[512,1408]{1,0:T(8,128)(2,1)}, f32[512,1408]{1,0:T(8,128)}) fusion(f32[512,1408]{1,0:T(8,128)} %fusion.3, bf16[512,2048]{1,0:T(8,128)(2,1)S(1)} %bitcast.204, bf16[2048,1408]{1,0:T(8,128)(2,1)} %all-gather.5.cloned.1.call-done), kind=kOutput, calls=%fused_computation.41 | convolution fusion | flops 2957115392 | bytes 15073280 | tf_op jit(solution)/shard_map/td,df->tf/dot_general | solution.py:42
  330.9 7.8 %convolution_convert_fusion.10 = bf16[512,2048]{1,0:T(8,128)(2,1)} fusion(bf16[512,1408]{1,0:T(8,128)(2,1)} %get-tuple-element.256, bf16[2048,1408]{1,0:T(8,128)(2,1)} %all-gather.7.cloned.1.call-done), kind=kOutput, calls=%fused_computation.35 | convolution fusion | flops 2953838592 | bytes 9306112 | tf_op jit(solution)/shard_map/tf,df->td/dot_general | solution.py:42
  338.8 43.5 %combine4.1 = (f32[128,2048]{1,0:T(8,128)}, f32[128,2048]{1,0:T(8,128)}) custom-call(bf16[8,128,2048]{2,1,0:T(8,128)(2,1)} %convolution_convert_fusion.7.terms_ref, bf16[4,128,2048]{2,1,0:T(8,128)(2,1)} %bitcast.227), custom_call_target="tpu_custom_call" | custom-call | bytes 120000000 | tf_op jit(solution)/shard_map/combine4/pallas_call | solution.py:779
  385.2 45.1 %spread5.1 = (bf16[8,128,2048]{2,1,0:T(8,128)(2,1)S(1)}, bf16[4,128,2048]{2,1,0:T(8,128)(2,1)S(1)}) custom-call(bf16[128,2048]{1,0:T(8,128)(2,1)S(1)} %get-tuple-element.217.block_ref, bf16[128,2048]{1,0:T(8,128)(2,1)S(1)} %get-tuple-element.216.tokens_ref), custom_call_target="tpu_custom_call" | custom-call | bytes 120000000 | tf_op jit(solution)/shard_map/spread5/pallas_call | solution.py:611
  430.4 2.0 copy-done.2
  433.9 5.3 convolution_convert_fusion.5
  439.2 3.2 fusion.40
  444.6 5.1 convolution_convert_fusion.4
  451.3 2.7 copy-done.24
  454.8 10.1 %multiply_convert_fusion.1 = (bf16[768,1408]{1,0:T(8,128)(2,1)}, bf16[768,1408]{1,0:T(8,128)(2,1)}) fusion(f32[768,1408]{1,0:T(8,128)} %copy-done.77, f32[768,1408]{1,0:T(8,128)} %get-tuple-element.255, bf16[768,2048]{1,0:T(8,128)(2,1)S(1)} %fusion, bf16[1408,2048]{1,0:T(8,128)(2,1)S(1)} %bitcast.214), kind=kOutput, calls=%fused_computation.16 | convolution fusion | flops 4443242496 | bytes 21889024 | tf_op jit(solution)/shard_map/rd,fd->rf/dot_general | solution.py:42
  464.9 7.1 convolution_convert_fusion.1
  473.6 2.0 copy-done.25
  476.9 2.0 collective-permute-start.15
  479.0 5.1 fusion.72
  484.1 7.3 multiply_convert_fusion.5
  491.5 6.5 add_convert_fusion
  498.0 5.3 convolution_convert_fusion.2
  503.3 6.6 convolution_convert_fusion.3
  509.9 5.3 convolution_convert_fusion.6.terms_ref
  515.3 2.4 add_convert_fusion.6
  519.9 2.3 add_convert_fusion.4
  527.8 3.4 fusion.73
  531.3 4.8 add_convert_fusion.1
  536.1 75.8 %combine6.1 = (f32[128,2048]{1,0:T(8,128)}, f32[128,2048]{1,0:T(8,128)}) custom-call(bf16[8,128,2048]{2,1,0:T(8,128)(2,1)} %convolution_convert_fusion.6.terms_ref, bf16[4,128,2048]{2,1,0:T(8,128)(2,1)} %bitcast.226), custom_call_target="tpu_custom_call" | custom-call | bytes 120000000 | tf_op jit(solution)/shard_map/combine6/pallas_call | solution.py:779
  613.4 2.1 multiply_reduce_fusion.1
  617.2 2.1 collective-permute-start.20
  619.3 6.9 convolution_convert_fusion
  632.9 3.8 collective-permute-done.22
  638.2 4.4 convolution_convert_fusion.9
  642.5 2.9 convolution_convert_fusion.11
  645.6 3.0 copy.62
  648.6 3.1 constant_dynamic-slice_fusion.6
  651.7 2.5 collective-permute-start.24
  660.7 3.3 collective-permute-done.24
  665.5 5.5 convert_bitcast_fusion
  671.1 6.8 pad_maximum_fusion
  678.7 4.4 add_bitcast_fusion.1
  683.1 7.2 bitcast_convert_fusion
  693.1 2.1 add_convert_fusion.2
  702.7 4.6 add_bitcast_fusion.2
  707.4 32.7 %collective-permute-done.29 = bf16[128,2048]{1,0:T(8,128)(2,1)S(1)} collective-permute-done((bf16[128,2048]{1,0:T(8,128)(2,1)S(1)}, bf16[128,2048]{1,0:T(8,128)(2,1)S(1)}, u32[]{:S(2)}, u32[]{:S(2)}) %collective-permute-start.29) | collective-permute-done | bytes 524320 | tf_op jit(solution)/shard_map/ppermute | solution.py:50
  741.6 12.7 %collect.1 = f32[8,128]{1,0:T(8,128)} custom-call(f32[32,8,128]{2,1,0:T(8,128)} %pad.4.terms_ref), custom_call_target="tpu_custom_call" | custom-call | tf_op jit(solution)/shard_map/collect/pallas_call | solution.py:436
  755.6 4.5 add_bitcast_fusion
  760.1 2.4 maximum_convert_fusion
  762.5 8.4 %reduce-scatter.11.cloned.1.call-done = bf16[4,256,512]{1,2,0:T(8,128)(2,1)} async-done(((bf16[4,2048,512]{1,2,0:T(8,128)(2,1)}), bf16[4,256,512]{1,2,0:T(8,128)(2,1)}) %reduce-scatter.11.cloned.1.call-update) | async-done | bytes 1048592 | tf_op jit(solution)/shard_map/reduce_scatter | solution.py:1053
  774.7 2.0 copy.63
  (373 shorter events, 108.0 us)
Async XLA Ops:
  7.2 308.0 %all-gather.9.cloned.1.call-start = ((), (), s32[]{:S(2)}) async-start(), calls=%async_computation.10 | async-start | bytes 6488064 | tf_op jit(solution)/shard_map/all_gather | solution.py:854
  12.8 88.4 %copy-start.43 = (bf16[256,3,1408]{2,0,1:T(8,128)(2,1)S(1)}, bf16[256,3,1408]{2,0,1:T(8,128)(2,1)}, u32[]{:S(2)}) copy-start(bf16[256,3,1408]{2,0,1:T(8,128)(2,1)} %param.21) | copy-start | bytes 6488068
  101.2 25.2 %copy-start.8 = (bf16[1,8,256,512]{3,2,1,0:T(8,128)(2,1)}, bf16[1,8,256,512]{3,2,1,0:T(8,128)(2,1)S(1)}, u32[]{:S(2)}) copy-start(bf16[1,8,256,512]{3,2,1,0:T(8,128)(2,1)S(1)} %get-tuple-element.75) | copy-start | bytes 6291460
  102.7 220.1 %all-gather.5.cloned.1.call-start = ((), (), s32[]{:S(2)}) async-start(), calls=%async_computation.4 | async-start | bytes 6488064 | tf_op jit(solution)/shard_map/all_gather | solution.py:918
  114.3 10.8 %copy-start.44 = (bf16[1,512,512]{1,2,0:T(8,128)(2,1)}, bf16[1,512,512]{1,2,0:T(8,128)(2,1)S(1)}, u32[]{:S(2)}) copy-start(bf16[1,512,512]{1,2,0:T(8,128)(2,1)S(1)} %slice.312) | copy-start | bytes 1572868
  127.7 23.1 %copy-start.4 = (bf16[1,128,2048]{2,1,0:T(8,128)(2,1)S(1)}, bf16[1,128,2048]{2,1,0:T(8,128)(2,1)}, u32[]{:S(2)}) copy-start(bf16[1,128,2048]{2,1,0:T(8,128)(2,1)} %param.13) | copy-start | bytes 1572868
  127.8 8.7 %collective-permute-start.2 = (bf16[64,2048]{1,0:T(8,128)(2,1)S(1)}, bf16[64,2048]{1,0:T(8,128)(2,1)S(1)}, u32[]{:S(2)}, u32[]{:S(2)}) collective-permute-start(bf16[64,2048]{1,0:T(8,128)(2,1)S(1)} %get-tuple-element.214), channel_id=1, source_target_pairs={{0,8},{8,0},{16,24},{24,16},{1,9},{9,1},{17,25},{25,17},{2,10},{10... | collective-permute-start | bytes 786440 | tf_op jit(solution)/shard_map/ppermute | solution.py:46
  128.5 8.4 %collective-permute-start = (bf16[64,2048]{1,0:T(8,128)(2,1)S(1)}, bf16[64,2048]{1,0:T(8,128)(2,1)S(1)}, u32[]{:S(2)}, u32[]{:S(2)}) collective-permute-start(bf16[64,2048]{1,0:T(8,128)(2,1)S(1)} %get-tuple-element.215), channel_id=1, source_target_pairs={{0,16},{16,0},{8,24},{24,8},{1,17},{17,1},{9,25},{25,9},{2,18},{18... | collective-permute-start | bytes 786440 | tf_op jit(solution)/shard_map/ppermute | solution.py:50
  137.1 13.3 %collective-permute-start.3 = (bf16[128,2048]{1,0:T(8,128)(2,1)S(1)}, bf16[128,2048]{1,0:T(8,128)(2,1)S(1)}, u32[]{:S(2)}, u32[]{:S(2)}) collective-permute-start(bf16[128,2048]{1,0:T(8,128)(2,1)S(1)} %pad_maximum_fusion.9), channel_id=1, source_target_pairs={{0,16},{16,0},{8,24},{24,8},{1,17},{17,1},{9,25},{25,9},{2,18},{18... | collective-permute-start | bytes 1572872 | tf_op jit(solution)/shard_map/ppermute | solution.py:50
  137.7 13.2 %collective-permute-start.1 = (bf16[128,2048]{1,0:T(8,128)(2,1)S(1)}, bf16[128,2048]{1,0:T(8,128)(2,1)S(1)}, u32[]{:S(2)}, u32[]{:S(2)}) collective-permute-start(bf16[128,2048]{1,0:T(8,128)(2,1)S(1)} %pad_maximum_fusion.8), channel_id=1, source_target_pairs={{0,8},{8,0},{16,24},{24,16},{1,9},{9,1},{17,25},{25,17},{2,10},{10... | collective-permute-start | bytes 1572872 | tf_op jit(solution)/shard_map/ppermute | solution.py:46
  139.9 11.8 %copy-start.56 = (f32[1,2048]{1,0:T(1,128)}, f32[1,2048]{1,0:T(1,128)S(1)}, u32[]{:S(2)}) copy-start(f32[1,2048]{1,0:T(1,128)S(1)} %get-tuple-element.240) | copy-start | bytes 24580
  139.9 77.5 %copy-start.61 = (f32[1,2048]{1,0:T(1,128)}, f32[1,2048]{1,0:T(1,128)S(1)}, u32[]{:S(2)}) copy-start(f32[1,2048]{1,0:T(1,128)S(1)} %get-tuple-element.239) | copy-start | bytes 24580
  151.8 51.0 %copy-start.65 = (f32[128]{0:T(128)}, f32[128]{0:T(128)S(1)}, u32[]{:S(2)}) copy-start(f32[128]{0:T(128)S(1)} %add_rsqrt_fusion.1) | copy-start | bytes 1540
  152.9 64.6 %copy-start = (bf16[128,2048]{1,0:T(8,128)(2,1)}, bf16[128,2048]{1,0:T(8,128)(2,1)S(1)}, u32[]{:S(2)}) copy-start(bf16[128,2048]{1,0:T(8,128)(2,1)S(1)} %multiply_convert_fusion.9.block_ref.tokens_ref) | copy-start | bytes 1572868
  199.2 131.7 %all-gather.7.cloned.1.call-start = ((), (), s32[]{:S(2)}) async-start(), calls=%async_computation.5 | async-start | bytes 6488064 | tf_op jit(solution)/shard_map/all_gather | solution.py:919
  199.2 38.1 %collective-permute-start.5 = (bf16[512,1408]{1,0:T(8,128)(2,1)}, bf16[512,1408]{1,0:T(8,128)(2,1)}, u32[]{:S(2)}, u32[]{:S(2)}) collective-permute-start(bf16[512,1408]{1,0:T(8,128)(2,1)} %bitcast.234), channel_id=1, source_target_pairs={{0,16},{16,0},{8,24},{24,8},{1,17},{17,1},{9,25},{25,9},{2,18},{18... | collective-permute-start | bytes 4325384 | tf_op jit(solution)/shard_map/ppermute | solution.py:50
  201.0 34.8 %collective-permute-start.4 = (bf16[512,1408]{1,0:T(8,128)(2,1)}, bf16[512,1408]{1,0:T(8,128)(2,1)}, u32[]{:S(2)}, u32[]{:S(2)}) collective-permute-start(bf16[512,1408]{1,0:T(8,128)(2,1)} %bitcast.235), channel_id=1, source_target_pairs={{0,8},{8,0},{16,24},{24,16},{1,9},{9,1},{17,25},{25,17},{2,10},{10... | collective-permute-start | bytes 4325384 | tf_op jit(solution)/shard_map/ppermute | solution.py:46
  202.5 409.5 %reduce-scatter.5.cloned.1.call-start = ((), (), s32[]{:S(2)}) async-start(), calls=%async_computation.6 | async-start | bytes 6488064 | tf_op jit(solution)/shard_map/reduce_scatter | solution.py:982
  207.3 81.7 %collective-permute-start.9 = (bf16[352,2048]{1,0:T(8,128)(2,1)}, bf16[352,2048]{1,0:T(8,128)(2,1)S(1)}, u32[]{:S(2)}, u32[]{:S(2)}) collective-permute-start(bf16[352,2048]{1,0:T(8,128)(2,1)} %bitcast.237), channel_id=1, source_target_pairs={{0,16},{16,0},{8,24},{24,8},{1,17},{17,1},{9,25},{25,9},{2,18},{18... | collective-permute-start | bytes 4325384 | tf_op jit(solution)/shard_map/ppermute | solution.py:50
  207.8 73.4 %collective-permute-start.8 = (bf16[352,2048]{1,0:T(8,128)(2,1)}, bf16[352,2048]{1,0:T(8,128)(2,1)S(1)}, u32[]{:S(2)}, u32[]{:S(2)}) collective-permute-start(bf16[352,2048]{1,0:T(8,128)(2,1)} %bitcast.238), channel_id=1, source_target_pairs={{0,8},{8,0},{16,24},{24,16},{1,9},{9,1},{17,25},{25,17},{2,10},{10... | collective-permute-start | bytes 4325384 | tf_op jit(solution)/shard_map/ppermute | solution.py:46
  209.1 72.6 %copy-start.34 = (bf16[8,96,2048]{2,1,0:T(8,128)(2,1)}, bf16[8,96,2048]{2,1,0:T(8,128)(2,1)S(1)}, u32[]{:S(2)}) copy-start(bf16[8,96,2048]{2,1,0:T(8,128)(2,1)S(1)} %convolution_convert_fusion.8) | copy-start | bytes 9437188
  214.8 66.9 %copy-start.77 = (f32[768,1408]{1,0:T(8,128)}, f32[768,1408]{1,0:T(8,128)S(1)}, u32[]{:S(2)}) copy-start(f32[768,1408]{1,0:T(8,128)S(1)} %fusion.71) | copy-start | bytes 12976132
  217.7 24.2 %copy-start.70 = (f32[128]{0:T(128)}, f32[128]{0:T(128)S(1)}, u32[]{:S(2)}) copy-start(f32[128]{0:T(128)S(1)} %fusion.21) | copy-start | bytes 1540
  236.9 42.8 %collective-permute-start.6 = (bf16[256,1408]{1,0:T(8,128)(2,1)S(1)}, bf16[256,1408]{1,0:T(8,128)(2,1)S(1)}, u32[]{:S(2)}, u32[]{:S(2)}) collective-permute-start(bf16[256,1408]{1,0:T(8,128)(2,1)S(1)} %slice.271), channel_id=1, source_target_pairs={{0,16},{16,0},{8,24},{24,8},{1,17},{17,1},{9,25},{25,9},{2,18},{18... | collective-permute-start | bytes 2162696 | tf_op jit(solution)/shard_map/ppermute | solution.py:50
  238.5 42.6 %collective-permute-start.7 = (bf16[256,1408]{1,0:T(8,128)(2,1)S(1)}, bf16[256,1408]{1,0:T(8,128)(2,1)S(1)}, u32[]{:S(2)}, u32[]{:S(2)}) collective-permute-start(bf16[256,1408]{1,0:T(8,128)(2,1)S(1)} %slice.272), channel_id=1, source_target_pairs={{0,8},{8,0},{16,24},{24,16},{1,9},{9,1},{17,25},{25,17},{2,10},{10... | collective-permute-start | bytes 2162696 | tf_op jit(solution)/shard_map/ppermute | solution.py:46
  281.3 17.4 %collective-permute-start.10 = (bf16[176,2048]{1,0:T(8,128)(2,1)S(1)}, bf16[176,2048]{1,0:T(8,128)(2,1)S(1)}, u32[]{:S(2)}, u32[]{:S(2)}) collective-permute-start(bf16[176,2048]{1,0:T(8,128)(2,1)S(1)} %slice.273), channel_id=1, source_target_pairs={{0,16},{16,0},{8,24},{24,8},{1,17},{17,1},{9,25},{25,9},{2,18},{18... | collective-permute-start | bytes 2162696 | tf_op jit(solution)/shard_map/ppermute | solution.py:50
  288.9 17.6 %copy-start.80 = (bf16[768,1408]{1,0:T(8,128)(2,1)}, bf16[768,1408]{1,0:T(8,128)(2,1)S(1)}, u32[]{:S(2)}) copy-start(bf16[768,1408]{1,0:T(8,128)(2,1)S(1)} %get-tuple-element.254) | copy-start | bytes 6488068
  289.0 17.4 %collective-permute-start.11 = (bf16[176,2048]{1,0:T(8,128)(2,1)S(1)}, bf16[176,2048]{1,0:T(8,128)(2,1)S(1)}, u32[]{:S(2)}, u32[]{:S(2)}) collective-permute-start(bf16[176,2048]{1,0:T(8,128)(2,1)S(1)} %slice.274), channel_id=1, source_target_pairs={{0,8},{8,0},{16,24},{24,16},{1,9},{9,1},{17,25},{25,17},{2,10},{10... | collective-permute-start | bytes 2162696 | tf_op jit(solution)/shard_map/ppermute | solution.py:46
  338.8 43.6 %copy-start.20 = (f32[128,2048]{1,0:T(8,128)S(1)}, f32[128,2048]{1,0:T(8,128)}, u32[]{:S(2)}) copy-start(f32[128,2048]{1,0:T(8,128)} %copy-done.19) | copy-start | bytes 3145732
  338.8 43.6 %copy-start.28 = (bf16[1,128,2048]{2,1,0:T(8,128)(2,1)S(1)}, bf16[1,128,2048]{2,1,0:T(8,128)(2,1)}, u32[]{:S(2)}) copy-start(bf16[1,128,2048]{2,1,0:T(8,128)(2,1)} %param.14) | copy-start | bytes 1572868
  384.3 49.6 %copy-start.75 = (bf16[512,1408]{1,0:T(8,128)(2,1)S(1)}, bf16[512,1408]{1,0:T(8,128)(2,1)}, u32[]{:S(2)}) copy-start(bf16[512,1408]{1,0:T(8,128)(2,1)} %get-tuple-element.256) | copy-start | bytes 4325380
  439.2 199.0 %reduce-scatter.7.cloned.1.call-start = ((), (), s32[]{:S(2)}) async-start(), calls=%async_computation.7 | async-start | bytes 6488064 | tf_op jit(solution)/shard_map/reduce_scatter | solution.py:982
  442.5 12.2 %slice-start.4 = ((s8[5767168]{0:T(1024)(128)(4,1)}), s8[4194304]{0:T(1024)(128)(4,1)S(1)}, s32[]{:S(2)}) async-start(s8[5767168]{0:T(1024)(128)(4,1)} %bitcast.213), calls=%async_computation.15 | async-start | bytes 8388608
  444.6 10.2 %slice-start.5 = ((s8[5767168]{0:T(1024)(128)(4,1)}), s8[1572864]{0:T(1024)(128)(4,1)S(1)}, s32[]{:S(2)}) async-start(s8[5767168]{0:T(1024)(128)(4,1)} %bitcast.213), calls=%async_computation.16 | async-start | bytes 3145728
  449.7 29.3 %slice-start.2 = ((s8[5767168]{0:T(1024)(128)(4,1)}), s8[4194304]{0:T(1024)(128)(4,1)S(1)}, s32[]{:S(2)}) async-start(s8[5767168]{0:T(1024)(128)(4,1)} %bitcast.198), calls=%async_computation.13 | async-start | bytes 8388608
  454.0 55.9 %collective-permute-start.12 = (bf16[176,2048]{1,0:T(8,128)(2,1)}, bf16[176,2048]{1,0:T(8,128)(2,1)}, u32[]{:S(2)}, u32[]{:S(2)}) collective-permute-start(bf16[176,2048]{1,0:T(8,128)(2,1)} %get-tuple-element.195), channel_id=1, source_target_pairs={{0,8},{8,0},{16,24},{24,16},{1,9},{9,1},{17,25},{25,17},{2,10},{10... | collective-permute-start | bytes 2162696 | tf_op jit(solution)/shard_map/ppermute | solution.py:46
  454.0 55.9 %collective-permute-start.13 = (bf16[176,2048]{1,0:T(8,128)(2,1)}, bf16[176,2048]{1,0:T(8,128)(2,1)}, u32[]{:S(2)}, u32[]{:S(2)}) collective-permute-start(bf16[176,2048]{1,0:T(8,128)(2,1)} %get-tuple-element.196), channel_id=1, source_target_pairs={{0,16},{16,0},{8,24},{24,8},{1,17},{17,1},{9,25},{25,9},{2,18},{18... | collective-permute-start | bytes 2162696 | tf_op jit(solution)/shard_map/ppermute | solution.py:50
  454.7 10.2 %copy-start.35 = (bf16[8,96,2048]{2,1,0:T(8,128)(2,1)S(1)}, bf16[8,96,2048]{2,1,0:T(8,128)(2,1)}, u32[]{:S(2)}) copy-start(bf16[8,96,2048]{2,1,0:T(8,128)(2,1)} %copy-done.34) | copy-start | bytes 9437188
  454.8 24.2 %slice-start.3 = ((s8[5767168]{0:T(1024)(128)(4,1)}), s8[1572864]{0:T(1024)(128)(4,1)S(1)}, s32[]{:S(2)}) async-start(s8[5767168]{0:T(1024)(128)(4,1)} %bitcast.198), calls=%async_computation.14 | async-start | bytes 3145728
  475.6 39.6 %collective-permute-start.14 = (bf16[256,1408]{1,0:T(8,128)(2,1)}, bf16[256,1408]{1,0:T(8,128)(2,1)}, u32[]{:S(2)}, u32[]{:S(2)}) collective-permute-start(bf16[256,1408]{1,0:T(8,128)(2,1)} %get-tuple-element.189), channel_id=1, source_target_pairs={{0,8},{8,0},{16,24},{24,16},{1,9},{9,1},{17,25},{25,17},{2,10},{10... | collective-permute-start | bytes 2162696 | tf_op jit(solution)/shard_map/ppermute | solution.py:46
  476.9 38.3 %collective-permute-start.15 = (bf16[256,1408]{1,0:T(8,128)(2,1)}, bf16[256,1408]{1,0:T(8,128)(2,1)}, u32[]{:S(2)}, u32[]{:S(2)}) collective-permute-start(bf16[256,1408]{1,0:T(8,128)(2,1)} %get-tuple-element.190), channel_id=1, source_target_pairs={{0,16},{16,0},{8,24},{24,8},{1,17},{17,1},{9,25},{25,9},{2,18},{18... | collective-permute-start | bytes 2162696 | tf_op jit(solution)/shard_map/ppermute | solution.py:50
  479.0 12.5 %slice-start.6 = ((s8[5767168]{0:T(1024)(128)(4,1)}), s8[4194304]{0:T(1024)(128)(4,1)S(1)}, s32[]{:S(2)}) async-start(s8[5767168]{0:T(1024)(128)(4,1)} %bitcast.215), calls=%async_computation.17 | async-start | bytes 8388608
  515.2 163.2 %reduce-scatter.9.cloned.1.call-start = ((), (), s32[]{:S(2)}) async-start(), calls=%async_computation.8 | async-start | bytes 6488064 | tf_op jit(solution)/shard_map/reduce_scatter | solution.py:982
  517.8 94.1 %collective-permute-start.16 = (bf16[352,2048]{1,0:T(8,128)(2,1)S(1)}, bf16[352,2048]{1,0:T(8,128)(2,1)}, u32[]{:S(2)}, u32[]{:S(2)}) collective-permute-start(bf16[352,2048]{1,0:T(8,128)(2,1)S(1)} %pad_maximum_fusion.2), channel_id=1, source_target_pairs={{0,8},{8,0},{16,24},{24,16},{1,9},{9,1},{17,25},{25,17},{2,10},{10... | collective-permute-start | bytes 4325384 | tf_op jit(solution)/shard_map/ppermute | solution.py:46
  519.2 92.7 %collective-permute-start.17 = (bf16[352,2048]{1,0:T(8,128)(2,1)}, bf16[352,2048]{1,0:T(8,128)(2,1)}, u32[]{:S(2)}, u32[]{:S(2)}) collective-permute-start(bf16[352,2048]{1,0:T(8,128)(2,1)} %pad_maximum_fusion.3), channel_id=1, source_target_pairs={{0,16},{16,0},{8,24},{24,8},{1,17},{17,1},{9,25},{25,9},{2,18},{18... | collective-permute-start | bytes 4325384 | tf_op jit(solution)/shard_map/ppermute | solution.py:50
  523.5 88.5 %collective-permute-start.18 = (bf16[512,1408]{1,0:T(8,128)(2,1)}, bf16[512,1408]{1,0:T(8,128)(2,1)}, u32[]{:S(2)}, u32[]{:S(2)}) collective-permute-start(bf16[512,1408]{1,0:T(8,128)(2,1)} %pad_maximum_fusion.4), channel_id=1, source_target_pairs={{0,8},{8,0},{16,24},{24,16},{1,9},{9,1},{17,25},{25,17},{2,10},{10... | collective-permute-start | bytes 4325384 | tf_op jit(solution)/shard_map/ppermute | solution.py:46
  526.0 86.0 %collective-permute-start.19 = (bf16[512,1408]{1,0:T(8,128)(2,1)}, bf16[512,1408]{1,0:T(8,128)(2,1)}, u32[]{:S(2)}, u32[]{:S(2)}) collective-permute-start(bf16[512,1408]{1,0:T(8,128)(2,1)} %pad_maximum_fusion.5), channel_id=1, source_target_pairs={{0,16},{16,0},{8,24},{24,8},{1,17},{17,1},{9,25},{25,9},{2,18},{18... | collective-permute-start | bytes 4325384 | tf_op jit(solution)/shard_map/ppermute | solution.py:50
  612.1 158.8 %reduce-scatter.11.cloned.1.call-start = ((), (), s32[]{:S(2)}) async-start(), calls=%async_computation.9 | async-start | bytes 9437184 | tf_op jit(solution)/shard_map/reduce_scatter | solution.py:1053
  617.1 9.9 %collective-permute-start.21 = (bf16[128,2048]{1,0:T(8,128)(2,1)S(1)}, bf16[128,2048]{1,0:T(8,128)(2,1)S(1)}, u32[]{:S(2)}, u32[]{:S(2)}) collective-permute-start(bf16[128,2048]{1,0:T(8,128)(2,1)S(1)} %get-tuple-element.108), channel_id=1, source_target_pairs={{0,16},{16,0},{8,24},{24,8},{1,17},{17,1},{9,25},{25,9},{2,18},{18... | collective-permute-start | bytes 1572872 | tf_op jit(solution)/shard_map/ppermute | solution.py:50
  617.2 13.1 %collective-permute-start.20 = (bf16[128,2048]{1,0:T(8,128)(2,1)S(1)}, bf16[128,2048]{1,0:T(8,128)(2,1)S(1)}, u32[]{:S(2)}, u32[]{:S(2)}) collective-permute-start(bf16[128,2048]{1,0:T(8,128)(2,1)S(1)} %get-tuple-element.108), channel_id=1, source_target_pairs={{0,8},{8,0},{16,24},{24,16},{1,9},{9,1},{17,25},{25,17},{2,10},{10... | collective-permute-start | bytes 1572872 | tf_op jit(solution)/shard_map/ppermute | solution.py:46
  626.2 12.0 %copy-start.50 = (bf16[4,128,512]{2,1,0:T(8,128)(2,1)S(1)}, bf16[4,128,512]{2,1,0:T(8,128)(2,1)}, u32[]{:S(2)}) copy-start(bf16[4,128,512]{2,1,0:T(8,128)(2,1)} %copy-done.49) | copy-start | bytes 1572868
  627.0 10.4 %collective-permute-start.23 = (bf16[64,2048]{1,0:T(8,128)(2,1)S(1)}, bf16[64,2048]{1,0:T(8,128)(2,1)S(1)}, u32[]{:S(2)}, u32[]{:S(2)}) collective-permute-start(bf16[64,2048]{1,0:T(8,128)(2,1)S(1)} %slice.277), channel_id=1, source_target_pairs={{0,8},{8,0},{16,24},{24,16},{1,9},{9,1},{17,25},{25,17},{2,10},{10... | collective-permute-start | bytes 786440 | tf_op jit(solution)/shard_map/ppermute | solution.py:46
  630.3 6.4 collective-permute-start.22
  651.7 12.3 %collective-permute-start.24 = (bf16[256,1408]{1,0:T(8,128)(2,1)S(1)}, bf16[256,1408]{1,0:T(8,128)(2,1)}, u32[]{:S(2)}, u32[]{:S(2)}) collective-permute-start(bf16[256,1408]{1,0:T(8,128)(2,1)S(1)} %get-tuple-element.183), channel_id=1, source_target_pairs={{0,8},{8,0},{16,24},{24,16},{1,9},{9,1},{17,25},{25,17},{2,10},{10... | collective-permute-start | bytes 2162696 | tf_op jit(solution)/shard_map/ppermute | solution.py:46
  654.1 11.4 %collective-permute-start.25 = (bf16[256,1408]{1,0:T(8,128)(2,1)S(1)}, bf16[256,1408]{1,0:T(8,128)(2,1)}, u32[]{:S(2)}, u32[]{:S(2)}) collective-permute-start(bf16[256,1408]{1,0:T(8,128)(2,1)S(1)} %get-tuple-element.184), channel_id=1, source_target_pairs={{0,16},{16,0},{8,24},{24,8},{1,17},{17,1},{9,25},{25,9},{2,18},{18... | collective-permute-start | bytes 2162696 | tf_op jit(solution)/shard_map/ppermute | solution.py:50
  690.4 8.2 %collective-permute-start.28 = (bf16[64,2048]{1,0:T(8,128)(2,1)S(1)}, bf16[64,2048]{1,0:T(8,128)(2,1)S(1)}, u32[]{:S(2)}, u32[]{:S(2)}) collective-permute-start(bf16[64,2048]{1,0:T(8,128)(2,1)S(1)} %get-tuple-element.208), channel_id=1, source_target_pairs={{0,8},{8,0},{16,24},{24,16},{1,9},{9,1},{17,25},{25,17},{2,10},{10... | collective-permute-start | bytes 786440 | tf_op jit(solution)/shard_map/ppermute | solution.py:46
  691.6 8.8 %collective-permute-start.26 = (bf16[64,2048]{1,0:T(8,128)(2,1)S(1)}, bf16[64,2048]{1,0:T(8,128)(2,1)S(1)}, u32[]{:S(2)}, u32[]{:S(2)}) collective-permute-start(bf16[64,2048]{1,0:T(8,128)(2,1)S(1)} %get-tuple-element.209), channel_id=1, source_target_pairs={{0,16},{16,0},{8,24},{24,8},{1,17},{17,1},{9,25},{25,9},{2,18},{18... | collective-permute-start | bytes 786440 | tf_op jit(solution)/shard_map/ppermute | solution.py:50
  695.3 45.0 %collective-permute-start.30 = (bf16[512,1408]{1,0:T(8,128)(2,1)S(1)}, bf16[512,1408]{1,0:T(8,128)(2,1)}, u32[]{:S(2)}, u32[]{:S(2)}) collective-permute-start(bf16[512,1408]{1,0:T(8,128)(2,1)S(1)} %pad_maximum_fusion.6), channel_id=1, source_target_pairs={{0,8},{8,0},{16,24},{24,16},{1,9},{9,1},{17,25},{25,17},{2,10},{10... | collective-permute-start | bytes 4325384 | tf_op jit(solution)/shard_map/ppermute | solution.py:46
  696.1 44.3 %collective-permute-start.31 = (bf16[512,1408]{1,0:T(8,128)(2,1)S(1)}, bf16[512,1408]{1,0:T(8,128)(2,1)}, u32[]{:S(2)}, u32[]{:S(2)}) collective-permute-start(bf16[512,1408]{1,0:T(8,128)(2,1)S(1)} %pad_maximum_fusion.7), channel_id=1, source_target_pairs={{0,16},{16,0},{8,24},{24,8},{1,17},{17,1},{9,25},{25,9},{2,18},{18... | collective-permute-start | bytes 4325384 | tf_op jit(solution)/shard_map/ppermute | solution.py:50
  700.6 39.5 %collective-permute-start.29 = (bf16[128,2048]{1,0:T(8,128)(2,1)S(1)}, bf16[128,2048]{1,0:T(8,128)(2,1)S(1)}, u32[]{:S(2)}, u32[]{:S(2)}) collective-permute-start(bf16[128,2048]{1,0:T(8,128)(2,1)S(1)} %pad_maximum_fusion.11), channel_id=1, source_target_pairs={{0,16},{16,0},{8,24},{24,8},{1,17},{17,1},{9,25},{25,9},{2,18},{18... | collective-permute-start | bytes 1572872 | tf_op jit(solution)/shard_map/ppermute | solution.py:50
  702.5 37.8 %copy-start.60 = (f32[1,2048]{1,0:T(1,128)S(1)}, f32[1,2048]{1,0:T(1,128)}, u32[]{:S(2)}) copy-start(f32[1,2048]{1,0:T(1,128)} %get-tuple-element.238) | copy-start | bytes 24580
  702.5 37.6 %collective-permute-start.27 = (bf16[128,2048]{1,0:T(8,128)(2,1)S(1)}, bf16[128,2048]{1,0:T(8,128)(2,1)S(1)}, u32[]{:S(2)}, u32[]{:S(2)}) collective-permute-start(bf16[128,2048]{1,0:T(8,128)(2,1)S(1)} %pad_maximum_fusion.10), channel_id=1, source_target_pairs={{0,8},{8,0},{16,24},{24,16},{1,9},{9,1},{17,25},{25,17},{2,10},{10... | collective-permute-start | bytes 1572872 | tf_op jit(solution)/shard_map/ppermute | solution.py:46
  707.4 33.0 %copy-start.5 = (bf16[1,128,2048]{2,1,0:T(8,128)(2,1)S(1)}, bf16[1,128,2048]{2,1,0:T(8,128)(2,1)}, u32[]{:S(2)}) copy-start(bf16[1,128,2048]{2,1,0:T(8,128)(2,1)} %param.13) | copy-start | bytes 1572868
  707.4 46.9 %copy-start.33 = (f32[128,2048]{1,0:T(8,128)S(1)}, f32[128,2048]{1,0:T(8,128)}, u32[]{:S(2)}) copy-start(f32[128,2048]{1,0:T(8,128)} %get-tuple-element.169) | copy-start | bytes 3145732
  (72 other events, 261.7 us)
Sparse Core Ops, SparseCore 0:
  102.8 61.0 all-gather.8
  199.3 58.8 all-gather.4
  259.8 59.0 all-gather.6
  439.3 62.9 reduce-scatter.4
  515.3 73.6 reduce-scatter.6
  612.2 66.1 reduce-scatter.8
  680.8 90.1 reduce-scatter.10

commit v4 on v3

--- a/solution.py
+++ b/solution.py
@@ -381,7 +381,7 @@
         + [dma((2, chips))] * 6
         + [dma((3,))],
         compiler_params=pltpu.CompilerParams(
-            collective_id=1, has_side_effects=True, vmem_limit_bytes=24 * 1024 * 1024
+            collective_id=1, has_side_effects=True, vmem_limit_bytes=60 * 1024 * 1024
         ),
         name="opening",
     )(x, vector, routed, mixer, gate)
@@ -1029,7 +1029,8 @@
 
     dcontext = dot("td,dc->tc", row_dattn, mixer_out).astype(BF16)
     mixer_out_term = dot("td,tc->dc", row_dattn, context).astype(BF16)
-    dcontext, mixer_out_term = lax.optimization_barrier((dcontext, mixer_out_term))
+    mixer_base = jnp.pad(mixer_out_term[None], ((3, 0), (0, 0), (0, 0)))
+    dcontext, mixer_base = lax.optimization_barrier((dcontext, mixer_base))
     dcontext = heads(dcontext)
     probabilities_again = jnp.exp(score() - log_total)
     dprobs = dot("qhd,khd->hqk", dcontext, values)
@@ -1048,7 +1049,7 @@
     dprojected, corners[2] = lax.optimization_barrier((dprojected, corners[2]))
     sides.append(scatter_sides(terms[2], corners[2]))
     mixer_term = dot("td,kte->kde", row_normed, dprojected).astype(BF16)
-    mixer_term = jnp.concatenate([mixer_term, mixer_out_term[None]], axis=0)
+    mixer_term = lax.dynamic_update_slice(mixer_base, mixer_term, (0, 0, 0))
     mixer_term, grad_shared_ups = lax.optimization_barrier((mixer_term, grad_shared_ups))
     grad_mixer = lax.psum_scatter(mixer_term, "expert", scatter_dimension=1, tiled=True)
     dnormed = dot("kte,kde->td", dprojected, mixer_in).astype(BF16)

time: 793 us -> 789 us (level)
  local copies, waits for them, and re-layouts: 65 us -> 56 us
  matrix products: 161 us -> 169 us
    ppermute x16, waiting for transfers between devices: 41.3 us -> 32.2 us  [swap_x(): return lax.ppermute(values, 'fsdp', [(0, 1), (1, 0), (2, 3), (3, 2)])]
    unnamed x201 -> x193, local copies, waits for them, and re-layouts: 36.1 us -> 27.5 us
    dot_general x35, matrix products: 161 us -> 169 us  [dot(): return jnp.einsum(form, left, right, preferred_element_type=F32)]
  transfers between devices with their start and end apart: 39 -> 39, of which waited for: 18 -> 17; matrix products, arithmetic and copies ran while one was open for 29% -> 29% of each run, Pallas kernels for 17% -> 17%
where the time goes in v4:
time: 789 us; the launch traced here: 779 us
  Pallas kernels  308 us (39%)
  matrix products  169 us (21%)
  waiting for transfers between devices  142 us (18%)
  local copies, waits for them, and re-layouts  56 us (7%)
  other arithmetic  49 us (6%)
  starting transfers between devices  32.9 us (4%)
  between operations  21.9 us (3%)
    dot_general x35, matrix products, dot(): return jnp.einsum(form, left, right, preferred_element_type=F32)  169 us
    pallas_call x2, Pallas kernels, combine(): pl.pallas_call(functools.partial(combine_kernel, chips), out_shape=[jax.S...  121 us
    ppermute x16, waiting for transfers between devices, swap_y(): return lax.ppermute(values, 'fsdp', [(0, 2), (2, 0), (1, 3), (3, 1)])  94.7 us
    pallas_call x2, Pallas kernels, spread(): pl.pallas_call(functools.partial(spread_kernel, chips), out_shape=[jax.Sh...  89.4 us
    pallas_call x1, Pallas kernels, opening(): pl.pallas_call(functools.partial(opening_kernel, chips), out_shape=[jax.S...  85.2 us
    ppermute x16, waiting for transfers between devices, swap_x(): return lax.ppermute(values, 'fsdp', [(0, 1), (1, 0), (2, 3), (3, 2)])  32.2 us
    unnamed x193, local copies, waits for them, and re-layouts  27.5 us
    ppermute x16, starting transfers between devices, swap_x(): return lax.ppermute(values, 'fsdp', [(0, 1), (1, 0), (2, 3), (3, 2)])  18.9 us
  transfers between devices with their start and end apart: 39, of which 17 were waited for; matrix products, arithmetic and copies ran while one was open for 29% of the time, Pallas kernels for 17%

profile of v4, /device:TPU:0, one launch (start us, length us, event | category | flops | bytes accessed | tf_op | source)
XLA Modules:
  0.0 779.1 jit_solution(15803137461515539011)
XLA Ops:
  7.3 2.5 copy.78
  12.6 85.2 %opening.1 = (f32[8,2048]{1,0:T(8,128)}, f32[8,8,128]{2,1,0:T(8,128)}, bf16[4,128,2048]{2,1,0:T(8,128)(2,1)}, bf16[3,8,256,512]{3,2,1,0:T(8,128)(2,1)}, bf16[1,8...) custom-call(bf16[128,2048]{1,0:T(8,128)(2,1)} %bitcast.199, f32[8,128]{1,0:T(8,128)} %copy-done.58, ...), custom_call_target="tpu_custom_call" | custom-call | tf_op jit(solution)/shard_map/opening/pallas_call | solution.py:365
  102.5 6.7 convolution_bitcast_fusion
  124.3 7.6 collective-permute-done.2
  136.0 9.6 %collective-permute-done.3 = bf16[128,2048]{1,0:T(8,128)(2,1)S(1)} collective-permute-done((bf16[128,2048]{1,0:T(8,128)(2,1)S(1)}, bf16[128,2048]{1,0:T(8,128)(2,1)S(1)}, u32[]{:S(2)}, u32[]{:S(2)}) %collective-permute-start.3) | collective-permute-done | bytes 524320 | tf_op jit(solution)/shard_map/ppermute | solution.py:50
  147.8 45.7 %spread3.1 = (bf16[8,128,2048]{2,1,0:T(8,128)(2,1)S(1)}, bf16[4,128,2048]{2,1,0:T(8,128)(2,1)S(1)}) custom-call(bf16[128,2048]{1,0:T(8,128)(2,1)S(1)} %multiply_convert_fusion.9.block_ref.tokens_ref, bf16[128,2048]{1,0:T(8,128)(2,1)S(1)} %multiply_convert_fusion.9.block_ref.tokens_ref), custom_call_target="tpu_custom_call" | custom-call | bytes 120000000 | tf_op jit(solution)/shard_map/spread3/pallas_call | solution.py:611
  193.5 2.0 copy-done.3
  197.1 1.9 collective-permute-start.4
  207.6 10.4 %fusion.72 = f32[768,1408]{1,0:T(8,128)} fusion(bf16[768,2048]{1,0:T(8,128)(2,1)S(1)} %bitcast.207, bf16[2048,1408]{1,0:T(8,128)(2,1)} %bitcast.256), kind=kOutput, calls=%fused_computation.220 | convolution fusion | flops 4429185024 | bytes 13238272 | tf_op jit(solution)/shard_map/rd,df->rf/dot_general | solution.py:42
  219.1 12.8 %collective-permute-done.4 = bf16[512,1408]{1,0:T(8,128)(2,1)} collective-permute-done((bf16[512,1408]{1,0:T(8,128)(2,1)}, bf16[512,1408]{1,0:T(8,128)(2,1)}, u32[]{:S(2)}, u32[]{:S(2)}) %collective-permute-start.4) | collective-permute-done | bytes 1441824 | tf_op jit(solution)/shard_map/ppermute | solution.py:46
  239.6 36.5 %collective-permute-done.6 = bf16[256,1408]{1,0:T(8,128)(2,1)S(1)} collective-permute-done((bf16[256,1408]{1,0:T(8,128)(2,1)S(1)}, bf16[256,1408]{1,0:T(8,128)(2,1)S(1)}, u32[]{:S(2)}, u32[]{:S(2)}) %collective-permute-start.6) | collective-permute-done | bytes 720928 | tf_op jit(solution)/shard_map/ppermute | solution.py:50
  278.1 6.8 multiply_convert_fusion.3
  287.1 8.1 %collective-permute-done.10 = bf16[176,2048]{1,0:T(8,128)(2,1)S(1)} collective-permute-done((bf16[176,2048]{1,0:T(8,128)(2,1)S(1)}, bf16[176,2048]{1,0:T(8,128)(2,1)S(1)}, u32[]{:S(2)}, u32[]{:S(2)}) %collective-permute-start.10) | collective-permute-done | bytes 720928 | tf_op jit(solution)/shard_map/ppermute | solution.py:50
  295.3 7.1 collective-permute-done.11
  302.5 5.2 multiply_convert_fusion
  307.7 3.3 convolution_convert_fusion.7.terms_ref
  311.0 7.6 fusion.3
  318.7 8.3 %multiply_convert_fusion.7 = (bf16[512,1408]{1,0:T(8,128)(2,1)}, f32[512,1408]{1,0:T(8,128)}) fusion(f32[512,1408]{1,0:T(8,128)} %fusion.3, bf16[512,2048]{1,0:T(8,128)(2,1)S(1)} %bitcast.190, bf16[2048,1408]{1,0:T(8,128)(2,1)} %all-gather.5.cloned.1.call-done), kind=kOutput, calls=%fused_computation.40 | convolution fusion | flops 2957115392 | bytes 15073280 | tf_op jit(solution)/shard_map/td,df->tf/dot_general | solution.py:42
  326.9 7.8 %convolution_convert_fusion.10 = bf16[512,2048]{1,0:T(8,128)(2,1)} fusion(bf16[512,1408]{1,0:T(8,128)(2,1)} %get-tuple-element.256, bf16[2048,1408]{1,0:T(8,128)(2,1)} %all-gather.7.cloned.1.call-done), kind=kOutput, calls=%fused_computation.34 | convolution fusion | flops 2953838592 | bytes 9306112 | tf_op jit(solution)/shard_map/tf,df->td/dot_general | solution.py:42
  334.8 44.8 %combine4.1 = (f32[128,2048]{1,0:T(8,128)}, f32[128,2048]{1,0:T(8,128)}) custom-call(bf16[8,128,2048]{2,1,0:T(8,128)(2,1)} %convolution_convert_fusion.7.terms_ref, bf16[4,128,2048]{2,1,0:T(8,128)(2,1)} %bitcast.215), custom_call_target="tpu_custom_call" | custom-call | bytes 120000000 | tf_op jit(solution)/shard_map/combine4/pallas_call | solution.py:779
  379.6 2.5 multiply_reduce_fusion.3
  382.4 43.7 %spread5.1 = (bf16[8,128,2048]{2,1,0:T(8,128)(2,1)S(1)}, bf16[4,128,2048]{2,1,0:T(8,128)(2,1)S(1)}) custom-call(bf16[128,2048]{1,0:T(8,128)(2,1)S(1)} %get-tuple-element.217.block_ref, bf16[128,2048]{1,0:T(8,128)(2,1)S(1)} %get-tuple-element.216.tokens_ref), custom_call_target="tpu_custom_call" | custom-call | bytes 120000000 | tf_op jit(solution)/shard_map/spread5/pallas_call | solution.py:611
  426.1 1.9 copy-done.2
  429.4 5.2 convolution_convert_fusion.5
  434.7 3.4 fusion.41
  438.5 5.2 convolution_convert_fusion.4
  448.4 9.4 %multiply_convert_fusion.1 = (bf16[768,1408]{1,0:T(8,128)(2,1)}, bf16[768,1408]{1,0:T(8,128)(2,1)}) fusion(f32[768,1408]{1,0:T(8,128)S(1)} %bitcast.267, f32[768,1408]{1,0:T(8,128)} %get-tuple-element.255, bf16[768,2048]{1,0:T(8,128)(2,1)S(1)} %fusion, bf16[1408,2048]{1,0:T(8,128)(2,1)S(1)} %bitcast.203), kind=kOutput, calls=%fused_computation.15 | convolution fusion | flops 4443242496 | bytes 21889024 | tf_op jit(solution)/shard_map/rd,fd->rf/dot_general | solution.py:42
  457.9 7.0 convolution_convert_fusion.1
  466.3 2.0 copy-done.17
  469.1 1.8 collective-permute-start.15
  470.9 7.9 %fusion.73 = f32[768,2048]{1,0:T(8,128)S(1)} fusion(bf16[768,1408]{1,0:T(8,128)(2,1)S(1)} %copy-done.78, bf16[2048,1408]{1,0:T(8,128)(2,1)} %bitcast.257), kind=kOutput, calls=%fused_computation.221 | convolution fusion | flops 4429185024 | bytes 14221312 | tf_op jit(solution)/shard_map/rf,df->rd/dot_general | solution.py:42
  478.9 5.2 multiply_convert_fusion.5
  484.0 8.7 %add_convert_fusion = bf16[768,2048]{1,0:T(8,128)(2,1)} fusion(f32[768,2048]{1,0:T(8,128)S(1)} %fusion.73, bf16[768,1408]{1,0:T(8,128)(2,1)} %get-tuple-element.110, bf16[2048,1408]{1,0:T(8,128)(2,1)S(1)} %bitcast.201), kind=kOutput, calls=%fused_computation.9 | convolution fusion | flops 4432330752 | bytes 17367040 | tf_op jit(solution)/shard_map/rf,df->rd/dot_general | solution.py:42
  492.7 5.3 convolution_convert_fusion.2
  498.0 6.6 convolution_convert_fusion.3
  504.6 5.3 convolution_convert_fusion.6.terms_ref
  510.0 2.3 add_convert_fusion.6
  515.0 2.2 add_convert_fusion.4
  521.5 3.4 fusion.74
  525.0 4.7 add_convert_fusion.1
  529.6 76.7 %combine6.1 = (f32[128,2048]{1,0:T(8,128)}, f32[128,2048]{1,0:T(8,128)}) custom-call(bf16[8,128,2048]{2,1,0:T(8,128)(2,1)} %convolution_convert_fusion.6.terms_ref, bf16[4,128,2048]{2,1,0:T(8,128)(2,1)} %bitcast.214), custom_call_target="tpu_custom_call" | custom-call | bytes 120000000 | tf_op jit(solution)/shard_map/combine6/pallas_call | solution.py:779
  607.9 2.7 multiply_reduce_fusion.1
  614.2 6.9 convolution_convert_fusion
  628.2 4.5 collective-permute-done.22
  634.2 3.1 constant_dynamic-slice_fusion.6
  637.3 1.9 collective-permute-start.24
  639.2 3.0 fusion.10
  642.2 4.0 pad.8
  646.2 2.9 convolution_convert_fusion.11
  649.4 3.3 multiply_reduce_fusion
  659.9 5.7 bitcast_dynamic-update-slice_fusion
  665.5 7.4 reduce-scatter.9.cloned.1.call-done
  674.3 4.3 add_bitcast_fusion.1
  678.5 7.3 bitcast_convert_fusion
  689.0 2.1 add_convert_fusion.2
  692.6 1.8 collective-permute-done.28
  694.3 2.4 collective-permute-done.26
  699.1 4.6 add_bitcast_fusion.2
  703.6 32.3 %collective-permute-done.29 = bf16[128,2048]{1,0:T(8,128)(2,1)S(1)} collective-permute-done((bf16[128,2048]{1,0:T(8,128)(2,1)S(1)}, bf16[128,2048]{1,0:T(8,128)(2,1)S(1)}, u32[]{:S(2)}, u32[]{:S(2)}) %collective-permute-start.29) | collective-permute-done | bytes 524320 | tf_op jit(solution)/shard_map/ppermute | solution.py:50
  737.4 11.9 %collect.1 = f32[8,128]{1,0:T(8,128)} custom-call(f32[32,8,128]{2,1,0:T(8,128)} %pad.9.terms_ref), custom_call_target="tpu_custom_call" | custom-call | tf_op jit(solution)/shard_map/collect/pallas_call | solution.py:436
  750.7 4.5 add_bitcast_fusion
  755.2 2.4 maximum_convert_fusion
  757.6 7.8 reduce-scatter.11.cloned.1.call-done
  769.3 2.7 copy.63
  (364 shorter events, 97.7 us)
Async XLA Ops:
  7.2 90.6 %copy-start.32 = (bf16[256,3,1408]{2,0,1:T(8,128)(2,1)S(1)}, bf16[256,3,1408]{2,0,1:T(8,128)(2,1)}, u32[]{:S(2)}) copy-start(bf16[256,3,1408]{2,0,1:T(8,128)(2,1)} %param.21) | copy-start | bytes 6488068
  7.2 303.8 %all-gather.9.cloned.1.call-start = ((), (), s32[]{:S(2)}) async-start(), calls=%async_computation.10 | async-start | bytes 6488064 | tf_op jit(solution)/shard_map/all_gather | solution.py:854
  99.2 219.5 %all-gather.5.cloned.1.call-start = ((), (), s32[]{:S(2)}) async-start(), calls=%async_computation.4 | async-start | bytes 6488064 | tf_op jit(solution)/shard_map/all_gather | solution.py:918
  123.1 22.6 %copy-start.14 = (bf16[1,128,2048]{2,1,0:T(8,128)(2,1)S(1)}, bf16[1,128,2048]{2,1,0:T(8,128)(2,1)}, u32[]{:S(2)}) copy-start(bf16[1,128,2048]{2,1,0:T(8,128)(2,1)} %param.13) | copy-start | bytes 1572868
  123.2 8.6 %collective-permute-start.2 = (bf16[64,2048]{1,0:T(8,128)(2,1)S(1)}, bf16[64,2048]{1,0:T(8,128)(2,1)S(1)}, u32[]{:S(2)}, u32[]{:S(2)}) collective-permute-start(bf16[64,2048]{1,0:T(8,128)(2,1)S(1)} %get-tuple-element.214), channel_id=1, source_target_pairs={{0,8},{8,0},{16,24},{24,16},{1,9},{9,1},{17,25},{25,17},{2,10},{10... | collective-permute-start | bytes 786440 | tf_op jit(solution)/shard_map/ppermute | solution.py:46
  123.7 8.3 %collective-permute-start = (bf16[64,2048]{1,0:T(8,128)(2,1)S(1)}, bf16[64,2048]{1,0:T(8,128)(2,1)S(1)}, u32[]{:S(2)}, u32[]{:S(2)}) collective-permute-start(bf16[64,2048]{1,0:T(8,128)(2,1)S(1)} %get-tuple-element.215), channel_id=1, source_target_pairs={{0,16},{16,0},{8,24},{24,8},{1,17},{17,1},{9,25},{25,9},{2,18},{18... | collective-permute-start | bytes 786440 | tf_op jit(solution)/shard_map/ppermute | solution.py:50
  132.1 13.4 %collective-permute-start.3 = (bf16[128,2048]{1,0:T(8,128)(2,1)S(1)}, bf16[128,2048]{1,0:T(8,128)(2,1)S(1)}, u32[]{:S(2)}, u32[]{:S(2)}) collective-permute-start(bf16[128,2048]{1,0:T(8,128)(2,1)S(1)} %pad_maximum_fusion.8), channel_id=1, source_target_pairs={{0,16},{16,0},{8,24},{24,8},{1,17},{17,1},{9,25},{25,9},{2,18},{18... | collective-permute-start | bytes 1572872 | tf_op jit(solution)/shard_map/ppermute | solution.py:50
  132.8 12.9 %collective-permute-start.1 = (bf16[128,2048]{1,0:T(8,128)(2,1)S(1)}, bf16[128,2048]{1,0:T(8,128)(2,1)S(1)}, u32[]{:S(2)}, u32[]{:S(2)}) collective-permute-start(bf16[128,2048]{1,0:T(8,128)(2,1)S(1)} %pad_maximum_fusion.7), channel_id=1, source_target_pairs={{0,8},{8,0},{16,24},{24,16},{1,9},{9,1},{17,25},{25,17},{2,10},{10... | collective-permute-start | bytes 1572872 | tf_op jit(solution)/shard_map/ppermute | solution.py:46
  136.0 10.8 %copy-start.46 = (f32[1,2048]{1,0:T(1,128)}, f32[1,2048]{1,0:T(1,128)S(1)}, u32[]{:S(2)}) copy-start(f32[1,2048]{1,0:T(1,128)S(1)} %get-tuple-element.240) | copy-start | bytes 24580
  136.0 82.9 %copy-start.51 = (f32[1,2048]{1,0:T(1,128)}, f32[1,2048]{1,0:T(1,128)S(1)}, u32[]{:S(2)}) copy-start(f32[1,2048]{1,0:T(1,128)S(1)} %get-tuple-element.239) | copy-start | bytes 24580
  146.7 55.9 %copy-start.59 = (f32[128]{0:T(128)}, f32[128]{0:T(128)S(1)}, u32[]{:S(2)}) copy-start(f32[128]{0:T(128)S(1)} %add_rsqrt_fusion.1) | copy-start | bytes 1540
  147.8 71.1 %copy-start = (bf16[128,2048]{1,0:T(8,128)(2,1)}, bf16[128,2048]{1,0:T(8,128)(2,1)S(1)}, u32[]{:S(2)}) copy-start(bf16[128,2048]{1,0:T(8,128)(2,1)S(1)} %multiply_convert_fusion.9.block_ref.tokens_ref) | copy-start | bytes 1572868
  195.5 131.4 %all-gather.7.cloned.1.call-start = ((), (), s32[]{:S(2)}) async-start(), calls=%async_computation.5 | async-start | bytes 6488064 | tf_op jit(solution)/shard_map/all_gather | solution.py:919
  195.6 38.1 %collective-permute-start.5 = (bf16[512,1408]{1,0:T(8,128)(2,1)}, bf16[512,1408]{1,0:T(8,128)(2,1)}, u32[]{:S(2)}, u32[]{:S(2)}) collective-permute-start(bf16[512,1408]{1,0:T(8,128)(2,1)} %bitcast.224), channel_id=1, source_target_pairs={{0,16},{16,0},{8,24},{24,8},{1,17},{17,1},{9,25},{25,9},{2,18},{18... | collective-permute-start | bytes 4325384 | tf_op jit(solution)/shard_map/ppermute | solution.py:50
  197.1 34.8 %collective-permute-start.4 = (bf16[512,1408]{1,0:T(8,128)(2,1)}, bf16[512,1408]{1,0:T(8,128)(2,1)}, u32[]{:S(2)}, u32[]{:S(2)}) collective-permute-start(bf16[512,1408]{1,0:T(8,128)(2,1)} %bitcast.225), channel_id=1, source_target_pairs={{0,8},{8,0},{16,24},{24,16},{1,9},{9,1},{17,25},{25,17},{2,10},{10... | collective-permute-start | bytes 4325384 | tf_op jit(solution)/shard_map/ppermute | solution.py:46
  199.0 407.4 %reduce-scatter.5.cloned.1.call-start = ((), (), s32[]{:S(2)}) async-start(), calls=%async_computation.6 | async-start | bytes 6488064 | tf_op jit(solution)/shard_map/reduce_scatter | solution.py:982
  205.7 79.3 %collective-permute-start.9 = (bf16[352,2048]{1,0:T(8,128)(2,1)S(1)}, bf16[352,2048]{1,0:T(8,128)(2,1)S(1)}, u32[]{:S(2)}, u32[]{:S(2)}) collective-permute-start(bf16[352,2048]{1,0:T(8,128)(2,1)S(1)} %bitcast.227), channel_id=1, source_target_pairs={{0,16},{16,0},{8,24},{24,8},{1,17},{17,1},{9,25},{25,9},{2,18},{18... | collective-permute-start | bytes 4325384 | tf_op jit(solution)/shard_map/ppermute | solution.py:50
  206.1 71.3 %collective-permute-start.8 = (bf16[352,2048]{1,0:T(8,128)(2,1)S(1)}, bf16[352,2048]{1,0:T(8,128)(2,1)S(1)}, u32[]{:S(2)}, u32[]{:S(2)}) collective-permute-start(bf16[352,2048]{1,0:T(8,128)(2,1)S(1)} %bitcast.228), channel_id=1, source_target_pairs={{0,8},{8,0},{16,24},{24,16},{1,9},{9,1},{17,25},{25,17},{2,10},{10... | collective-permute-start | bytes 4325384 | tf_op jit(solution)/shard_map/ppermute | solution.py:46
  207.5 70.5 %copy-start.27 = (bf16[8,96,2048]{2,1,0:T(8,128)(2,1)}, bf16[8,96,2048]{2,1,0:T(8,128)(2,1)S(1)}, u32[]{:S(2)}) copy-start(bf16[8,96,2048]{2,1,0:T(8,128)(2,1)S(1)} %convolution_convert_fusion.8) | copy-start | bytes 9437188
  218.7 59.4 %slice-start.10 = ((s8[4325376]{0:T(1024)(128)(4,1)}), s8[4194304]{0:T(1024)(128)(4,1)S(1)}, s32[]{:S(2)}) async-start(s8[4325376]{0:T(1024)(128)(4,1)} %bitcast.264), calls=%async_computation.21 | async-start | bytes 8388608
  219.1 18.9 %copy-start.65 = (f32[128]{0:T(128)}, f32[128]{0:T(128)S(1)}, u32[]{:S(2)}) copy-start(f32[128]{0:T(128)S(1)} %fusion.22) | copy-start | bytes 1540
  233.0 43.0 %collective-permute-start.6 = (bf16[256,1408]{1,0:T(8,128)(2,1)S(1)}, bf16[256,1408]{1,0:T(8,128)(2,1)S(1)}, u32[]{:S(2)}, u32[]{:S(2)}) collective-permute-start(bf16[256,1408]{1,0:T(8,128)(2,1)S(1)} %slice.271), channel_id=1, source_target_pairs={{0,16},{16,0},{8,24},{24,8},{1,17},{17,1},{9,25},{25,9},{2,18},{18... | collective-permute-start | bytes 2162696 | tf_op jit(solution)/shard_map/ppermute | solution.py:50
  234.9 43.2 %slice-start.11 = ((s8[4325376]{0:T(1024)(128)(4,1)}), s8[131072]{0:T(1024)(128)(4,1)S(1)}, s32[]{:S(2)}) async-start(s8[4325376]{0:T(1024)(128)(4,1)} %bitcast.264), calls=%async_computation.22 | async-start | bytes 262144
  234.9 42.5 %collective-permute-start.7 = (bf16[256,1408]{1,0:T(8,128)(2,1)S(1)}, bf16[256,1408]{1,0:T(8,128)(2,1)S(1)}, u32[]{:S(2)}, u32[]{:S(2)}) collective-permute-start(bf16[256,1408]{1,0:T(8,128)(2,1)S(1)} %slice.272), channel_id=1, source_target_pairs={{0,8},{8,0},{16,24},{24,16},{1,9},{9,1},{17,25},{25,17},{2,10},{10... | collective-permute-start | bytes 2162696 | tf_op jit(solution)/shard_map/ppermute | solution.py:46
  277.6 17.6 %collective-permute-start.10 = (bf16[176,2048]{1,0:T(8,128)(2,1)S(1)}, bf16[176,2048]{1,0:T(8,128)(2,1)S(1)}, u32[]{:S(2)}, u32[]{:S(2)}) collective-permute-start(bf16[176,2048]{1,0:T(8,128)(2,1)S(1)} %slice.273), channel_id=1, source_target_pairs={{0,16},{16,0},{8,24},{24,8},{1,17},{17,1},{9,25},{25,9},{2,18},{18... | collective-permute-start | bytes 2162696 | tf_op jit(solution)/shard_map/ppermute | solution.py:50
  284.9 17.5 %copy-start.76 = (bf16[768,1408]{1,0:T(8,128)(2,1)}, bf16[768,1408]{1,0:T(8,128)(2,1)S(1)}, u32[]{:S(2)}) copy-start(bf16[768,1408]{1,0:T(8,128)(2,1)S(1)} %get-tuple-element.254) | copy-start | bytes 6488068
  285.0 17.4 %collective-permute-start.11 = (bf16[176,2048]{1,0:T(8,128)(2,1)S(1)}, bf16[176,2048]{1,0:T(8,128)(2,1)S(1)}, u32[]{:S(2)}, u32[]{:S(2)}) collective-permute-start(bf16[176,2048]{1,0:T(8,128)(2,1)S(1)} %slice.274), channel_id=1, source_target_pairs={{0,8},{8,0},{16,24},{24,16},{1,9},{9,1},{17,25},{25,17},{2,10},{10... | collective-permute-start | bytes 2162696 | tf_op jit(solution)/shard_map/ppermute | solution.py:46
  334.8 44.8 %copy-start.10 = (f32[128,2048]{1,0:T(8,128)S(1)}, f32[128,2048]{1,0:T(8,128)}, u32[]{:S(2)}) copy-start(f32[128,2048]{1,0:T(8,128)} %copy-done.9) | copy-start | bytes 3145732
  334.8 44.8 %copy-start.20 = (bf16[1,128,2048]{2,1,0:T(8,128)(2,1)S(1)}, bf16[1,128,2048]{2,1,0:T(8,128)(2,1)}, u32[]{:S(2)}) copy-start(bf16[1,128,2048]{2,1,0:T(8,128)(2,1)} %param.14) | copy-start | bytes 1572868
  382.1 44.0 %copy-start.12 = (f32[128,2048]{1,0:T(8,128)}, f32[128,2048]{1,0:T(8,128)S(1)}, u32[]{:S(2)}) copy-start(f32[128,2048]{1,0:T(8,128)S(1)} %get-tuple-element.172) | copy-start | bytes 3145732
  382.1 47.2 %copy-start.72 = (bf16[512,1408]{1,0:T(8,128)(2,1)S(1)}, bf16[512,1408]{1,0:T(8,128)(2,1)}, u32[]{:S(2)}) copy-start(bf16[512,1408]{1,0:T(8,128)(2,1)} %get-tuple-element.256) | copy-start | bytes 4325380
  434.6 199.6 %reduce-scatter.7.cloned.1.call-start = ((), (), s32[]{:S(2)}) async-start(), calls=%async_computation.7 | async-start | bytes 6488064 | tf_op jit(solution)/shard_map/reduce_scatter | solution.py:982
  438.1 10.3 %slice-start.2 = ((s8[5767168]{0:T(1024)(128)(4,1)}), s8[4194304]{0:T(1024)(128)(4,1)S(1)}, s32[]{:S(2)}) async-start(s8[5767168]{0:T(1024)(128)(4,1)} %bitcast.202), calls=%async_computation.13 | async-start | bytes 8388608
  438.1 10.3 %slice-start.12 = ((s8[4325376]{0:T(1024)(128)(4,1)}), s8[4194304]{0:T(1024)(128)(4,1)S(1)}, s32[]{:S(2)}) async-start(s8[4325376]{0:T(1024)(128)(4,1)} %bitcast.266), calls=%async_computation.23 | async-start | bytes 8388608
  438.5 9.9 %slice-start.3 = ((s8[5767168]{0:T(1024)(128)(4,1)}), s8[1572864]{0:T(1024)(128)(4,1)S(1)}, s32[]{:S(2)}) async-start(s8[5767168]{0:T(1024)(128)(4,1)} %bitcast.202), calls=%async_computation.14 | async-start | bytes 3145728
  438.5 9.9 %slice-start.13 = ((s8[4325376]{0:T(1024)(128)(4,1)}), s8[131072]{0:T(1024)(128)(4,1)S(1)}, s32[]{:S(2)}) async-start(s8[4325376]{0:T(1024)(128)(4,1)} %bitcast.266), calls=%async_computation.24 | async-start | bytes 262144
  446.8 57.8 %collective-permute-start.12 = (bf16[176,2048]{1,0:T(8,128)(2,1)}, bf16[176,2048]{1,0:T(8,128)(2,1)}, u32[]{:S(2)}, u32[]{:S(2)}) collective-permute-start(bf16[176,2048]{1,0:T(8,128)(2,1)} %get-tuple-element.195), channel_id=1, source_target_pairs={{0,8},{8,0},{16,24},{24,16},{1,9},{9,1},{17,25},{25,17},{2,10},{10... | collective-permute-start | bytes 2162696 | tf_op jit(solution)/shard_map/ppermute | solution.py:46
  447.7 56.9 %collective-permute-start.13 = (bf16[176,2048]{1,0:T(8,128)(2,1)}, bf16[176,2048]{1,0:T(8,128)(2,1)}, u32[]{:S(2)}, u32[]{:S(2)}) collective-permute-start(bf16[176,2048]{1,0:T(8,128)(2,1)} %get-tuple-element.196), channel_id=1, source_target_pairs={{0,16},{16,0},{8,24},{24,8},{1,17},{17,1},{9,25},{25,9},{2,18},{18... | collective-permute-start | bytes 2162696 | tf_op jit(solution)/shard_map/ppermute | solution.py:50
  468.2 41.6 %collective-permute-start.14 = (bf16[256,1408]{1,0:T(8,128)(2,1)}, bf16[256,1408]{1,0:T(8,128)(2,1)}, u32[]{:S(2)}, u32[]{:S(2)}) collective-permute-start(bf16[256,1408]{1,0:T(8,128)(2,1)} %get-tuple-element.189), channel_id=1, source_target_pairs={{0,8},{8,0},{16,24},{24,16},{1,9},{9,1},{17,25},{25,17},{2,10},{10... | collective-permute-start | bytes 2162696 | tf_op jit(solution)/shard_map/ppermute | solution.py:46
  469.1 40.8 %collective-permute-start.15 = (bf16[256,1408]{1,0:T(8,128)(2,1)}, bf16[256,1408]{1,0:T(8,128)(2,1)}, u32[]{:S(2)}, u32[]{:S(2)}) collective-permute-start(bf16[256,1408]{1,0:T(8,128)(2,1)} %get-tuple-element.190), channel_id=1, source_target_pairs={{0,16},{16,0},{8,24},{24,8},{1,17},{17,1},{9,25},{25,9},{2,18},{18... | collective-permute-start | bytes 2162696 | tf_op jit(solution)/shard_map/ppermute | solution.py:50
  470.9 13.2 %slice-start = ((s8[5767168]{0:T(1024)(128)(4,1)}), s8[4194304]{0:T(1024)(128)(4,1)S(1)}, s32[]{:S(2)}) async-start(s8[5767168]{0:T(1024)(128)(4,1)} %bitcast.200), calls=%async_computation.11 | async-start | bytes 8388608
  509.9 163.0 %reduce-scatter.9.cloned.1.call-start = ((), (), s32[]{:S(2)}) async-start(), calls=%async_computation.8 | async-start | bytes 6488064 | tf_op jit(solution)/shard_map/reduce_scatter | solution.py:982
  513.6 92.7 %collective-permute-start.16 = (bf16[352,2048]{1,0:T(8,128)(2,1)}, bf16[352,2048]{1,0:T(8,128)(2,1)}, u32[]{:S(2)}, u32[]{:S(2)}) collective-permute-start(bf16[352,2048]{1,0:T(8,128)(2,1)} %pad_maximum_fusion.1), channel_id=1, source_target_pairs={{0,8},{8,0},{16,24},{24,16},{1,9},{9,1},{17,25},{25,17},{2,10},{10... | collective-permute-start | bytes 4325384 | tf_op jit(solution)/shard_map/ppermute | solution.py:46
  514.6 91.8 %collective-permute-start.17 = (bf16[352,2048]{1,0:T(8,128)(2,1)S(1)}, bf16[352,2048]{1,0:T(8,128)(2,1)}, u32[]{:S(2)}, u32[]{:S(2)}) collective-permute-start(bf16[352,2048]{1,0:T(8,128)(2,1)S(1)} %pad_maximum_fusion.2), channel_id=1, source_target_pairs={{0,16},{16,0},{8,24},{24,8},{1,17},{17,1},{9,25},{25,9},{2,18},{18... | collective-permute-start | bytes 4325384 | tf_op jit(solution)/shard_map/ppermute | solution.py:50
  517.3 89.1 %collective-permute-start.18 = (bf16[512,1408]{1,0:T(8,128)(2,1)S(1)}, bf16[512,1408]{1,0:T(8,128)(2,1)}, u32[]{:S(2)}, u32[]{:S(2)}) collective-permute-start(bf16[512,1408]{1,0:T(8,128)(2,1)S(1)} %pad_maximum_fusion.3), channel_id=1, source_target_pairs={{0,8},{8,0},{16,24},{24,16},{1,9},{9,1},{17,25},{25,17},{2,10},{10... | collective-permute-start | bytes 4325384 | tf_op jit(solution)/shard_map/ppermute | solution.py:46
  519.8 86.6 %collective-permute-start.19 = (bf16[512,1408]{1,0:T(8,128)(2,1)}, bf16[512,1408]{1,0:T(8,128)(2,1)}, u32[]{:S(2)}, u32[]{:S(2)}) collective-permute-start(bf16[512,1408]{1,0:T(8,128)(2,1)} %pad_maximum_fusion.4), channel_id=1, source_target_pairs={{0,16},{16,0},{8,24},{24,8},{1,17},{17,1},{9,25},{25,9},{2,18},{18... | collective-permute-start | bytes 4325384 | tf_op jit(solution)/shard_map/ppermute | solution.py:50
  606.6 158.8 %reduce-scatter.11.cloned.1.call-start = ((), (), s32[]{:S(2)}) async-start(), calls=%async_computation.9 | async-start | bytes 9437184 | tf_op jit(solution)/shard_map/reduce_scatter | solution.py:1054
  612.1 11.1 %collective-permute-start.21 = (bf16[128,2048]{1,0:T(8,128)(2,1)S(1)}, bf16[128,2048]{1,0:T(8,128)(2,1)S(1)}, u32[]{:S(2)}, u32[]{:S(2)}) collective-permute-start(bf16[128,2048]{1,0:T(8,128)(2,1)S(1)} %get-tuple-element.108), channel_id=1, source_target_pairs={{0,16},{16,0},{8,24},{24,8},{1,17},{17,1},{9,25},{25,9},{2,18},{18... | collective-permute-start | bytes 1572872 | tf_op jit(solution)/shard_map/ppermute | solution.py:50
  612.6 13.7 %collective-permute-start.20 = (bf16[128,2048]{1,0:T(8,128)(2,1)S(1)}, bf16[128,2048]{1,0:T(8,128)(2,1)S(1)}, u32[]{:S(2)}, u32[]{:S(2)}) collective-permute-start(bf16[128,2048]{1,0:T(8,128)(2,1)S(1)} %get-tuple-element.108), channel_id=1, source_target_pairs={{0,8},{8,0},{16,24},{24,16},{1,9},{9,1},{17,25},{25,17},{2,10},{10... | collective-permute-start | bytes 1572872 | tf_op jit(solution)/shard_map/ppermute | solution.py:46
  623.2 10.2 %collective-permute-start.23 = (bf16[64,2048]{1,0:T(8,128)(2,1)S(1)}, bf16[64,2048]{1,0:T(8,128)(2,1)S(1)}, u32[]{:S(2)}, u32[]{:S(2)}) collective-permute-start(bf16[64,2048]{1,0:T(8,128)(2,1)S(1)} %slice.277), channel_id=1, source_target_pairs={{0,8},{8,0},{16,24},{24,16},{1,9},{9,1},{17,25},{25,17},{2,10},{10... | collective-permute-start | bytes 786440 | tf_op jit(solution)/shard_map/ppermute | solution.py:46
  626.3 6.4 collective-permute-start.22
  637.3 21.1 %collective-permute-start.24 = (bf16[256,1408]{1,0:T(8,128)(2,1)}, bf16[256,1408]{1,0:T(8,128)(2,1)}, u32[]{:S(2)}, u32[]{:S(2)}) collective-permute-start(bf16[256,1408]{1,0:T(8,128)(2,1)} %get-tuple-element.183), channel_id=1, source_target_pairs={{0,8},{8,0},{16,24},{24,16},{1,9},{9,1},{17,25},{25,17},{2,10},{10... | collective-permute-start | bytes 2162696 | tf_op jit(solution)/shard_map/ppermute | solution.py:46
  639.2 19.2 %collective-permute-start.25 = (bf16[256,1408]{1,0:T(8,128)(2,1)}, bf16[256,1408]{1,0:T(8,128)(2,1)}, u32[]{:S(2)}, u32[]{:S(2)}) collective-permute-start(bf16[256,1408]{1,0:T(8,128)(2,1)} %get-tuple-element.184), channel_id=1, source_target_pairs={{0,16},{16,0},{8,24},{24,8},{1,17},{17,1},{9,25},{25,9},{2,18},{18... | collective-permute-start | bytes 2162696 | tf_op jit(solution)/shard_map/ppermute | solution.py:50
  686.0 8.4 %collective-permute-start.28 = (bf16[64,2048]{1,0:T(8,128)(2,1)S(1)}, bf16[64,2048]{1,0:T(8,128)(2,1)S(1)}, u32[]{:S(2)}, u32[]{:S(2)}) collective-permute-start(bf16[64,2048]{1,0:T(8,128)(2,1)S(1)} %get-tuple-element.208), channel_id=1, source_target_pairs={{0,8},{8,0},{16,24},{24,16},{1,9},{9,1},{17,25},{25,17},{2,10},{10... | collective-permute-start | bytes 786440 | tf_op jit(solution)/shard_map/ppermute | solution.py:46
  687.5 9.2 %collective-permute-start.26 = (bf16[64,2048]{1,0:T(8,128)(2,1)S(1)}, bf16[64,2048]{1,0:T(8,128)(2,1)S(1)}, u32[]{:S(2)}, u32[]{:S(2)}) collective-permute-start(bf16[64,2048]{1,0:T(8,128)(2,1)S(1)} %get-tuple-element.209), channel_id=1, source_target_pairs={{0,16},{16,0},{8,24},{24,8},{1,17},{17,1},{9,25},{25,9},{2,18},{18... | collective-permute-start | bytes 786440 | tf_op jit(solution)/shard_map/ppermute | solution.py:50
  691.2 44.9 %collective-permute-start.30 = (bf16[512,1408]{1,0:T(8,128)(2,1)S(1)}, bf16[512,1408]{1,0:T(8,128)(2,1)}, u32[]{:S(2)}, u32[]{:S(2)}) collective-permute-start(bf16[512,1408]{1,0:T(8,128)(2,1)S(1)} %pad_maximum_fusion.5), channel_id=1, source_target_pairs={{0,8},{8,0},{16,24},{24,16},{1,9},{9,1},{17,25},{25,17},{2,10},{10... | collective-permute-start | bytes 4325384 | tf_op jit(solution)/shard_map/ppermute | solution.py:46
  691.9 44.2 %collective-permute-start.31 = (bf16[512,1408]{1,0:T(8,128)(2,1)S(1)}, bf16[512,1408]{1,0:T(8,128)(2,1)}, u32[]{:S(2)}, u32[]{:S(2)}) collective-permute-start(bf16[512,1408]{1,0:T(8,128)(2,1)S(1)} %pad_maximum_fusion.6), channel_id=1, source_target_pairs={{0,16},{16,0},{8,24},{24,8},{1,17},{17,1},{9,25},{25,9},{2,18},{18... | collective-permute-start | bytes 4325384 | tf_op jit(solution)/shard_map/ppermute | solution.py:50
  696.9 39.0 %collective-permute-start.29 = (bf16[128,2048]{1,0:T(8,128)(2,1)S(1)}, bf16[128,2048]{1,0:T(8,128)(2,1)S(1)}, u32[]{:S(2)}, u32[]{:S(2)}) collective-permute-start(bf16[128,2048]{1,0:T(8,128)(2,1)S(1)} %pad_maximum_fusion.10), channel_id=1, source_target_pairs={{0,16},{16,0},{8,24},{24,8},{1,17},{17,1},{9,25},{25,9},{2,18},{18... | collective-permute-start | bytes 1572872 | tf_op jit(solution)/shard_map/ppermute | solution.py:50
  698.4 37.7 %copy-start.50 = (f32[1,2048]{1,0:T(1,128)S(1)}, f32[1,2048]{1,0:T(1,128)}, u32[]{:S(2)}) copy-start(f32[1,2048]{1,0:T(1,128)} %get-tuple-element.238) | copy-start | bytes 24580
  698.4 37.7 %copy-start.61 = (f32[128]{0:T(128)S(1)}, f32[128]{0:T(128)}, u32[]{:S(2)}) copy-start(f32[128]{0:T(128)} %add_rsqrt_fusion) | copy-start | bytes 1540
  698.4 37.5 %collective-permute-start.27 = (bf16[128,2048]{1,0:T(8,128)(2,1)S(1)}, bf16[128,2048]{1,0:T(8,128)(2,1)S(1)}, u32[]{:S(2)}, u32[]{:S(2)}) collective-permute-start(bf16[128,2048]{1,0:T(8,128)(2,1)S(1)} %pad_maximum_fusion.9), channel_id=1, source_target_pairs={{0,8},{8,0},{16,24},{24,16},{1,9},{9,1},{17,25},{25,17},{2,10},{10... | collective-permute-start | bytes 1572872 | tf_op jit(solution)/shard_map/ppermute | solution.py:46
  703.6 32.5 %copy-start.15 = (bf16[1,128,2048]{2,1,0:T(8,128)(2,1)S(1)}, bf16[1,128,2048]{2,1,0:T(8,128)(2,1)}, u32[]{:S(2)}) copy-start(bf16[1,128,2048]{2,1,0:T(8,128)(2,1)} %param.13) | copy-start | bytes 1572868
  703.6 33.0 %copy-start.53 = (f32[1,32,64]{2,0,1:T(1,128)S(1)}, f32[1,32,64]{2,0,1:T(1,128)}, u32[]{:S(2)}) copy-start(f32[1,32,64]{2,0,1:T(1,128)} %stack.31) | copy-start | bytes 24580
  703.6 45.7 %copy-start.26 = (f32[128,2048]{1,0:T(8,128)S(1)}, f32[128,2048]{1,0:T(8,128)}, u32[]{:S(2)}) copy-start(f32[128,2048]{1,0:T(8,128)} %get-tuple-element.169) | copy-start | bytes 3145732
  (68 other events, 266.6 us)
Sparse Core Ops, SparseCore 0:
  99.3 61.0 all-gather.8
  195.7 58.8 all-gather.4
  256.2 59.0 all-gather.6
  434.7 63.3 reduce-scatter.4
  510.0 74.5 reduce-scatter.6
  606.7 66.2 reduce-scatter.8
  675.2 90.1 reduce-scatter.10

commit v5 on v4

--- a/solution.py
+++ b/solution.py
@@ -618,7 +618,7 @@
         out_specs=[pl.BlockSpec(memory_space=pltpu.VMEM)] * 2,
         scratch_shapes=[dma((chips,))] * 6 + [dma((6,))] * 2 + [dma((2,))],
         compiler_params=pltpu.CompilerParams(
-            collective_id=cid, has_side_effects=True, vmem_limit_bytes=40 * 1024 * 1024
+            collective_id=cid, has_side_effects=True, vmem_limit_bytes=60 * 1024 * 1024
         ),
         cost_estimate=WIRE,
         name=f"spread{cid}",

time: 789 us -> 799 us (1.013)
    unnamed x193 -> x175, local copies, waits for them, and re-layouts: 27.5 us -> 22.2 us
  transfers between devices with their start and end apart: 39 -> 39, of which waited for: 17 -> 16; matrix products, arithmetic and copies ran while one was open for 29% -> 29% of each run, Pallas kernels for 17% -> 17%
where the time goes in v5:
time: 799 us; the launch traced here: 790 us
  Pallas kernels  313 us (39%)
  matrix products  174 us (22%)
  waiting for transfers between devices  143 us (18%)
  other arithmetic  53.7 us (7%)
  local copies, waits for them, and re-layouts  48.6 us (6%)
  starting transfers between devices  35.9 us (4%)
  between operations  21.7 us (3%)
    dot_general x35, matrix products, dot(): return jnp.einsum(form, left, right, preferred_element_type=F32)  174 us
    pallas_call x2, Pallas kernels, combine(): pl.pallas_call(functools.partial(combine_kernel, chips), out_shape=[jax.S...  119 us
    pallas_call x2, Pallas kernels, spread(): pl.pallas_call(functools.partial(spread_kernel, chips), out_shape=[jax.Sh...  96.6 us
    ppermute x16, waiting for transfers between devices, swap_y(): return lax.ppermute(values, 'fsdp', [(0, 2), (2, 0), (1, 3), (3, 1)])  94.6 us
    pallas_call x1, Pallas kernels, opening(): pl.pallas_call(functools.partial(opening_kernel, chips), out_shape=[jax.S...  85.2 us
    ppermute x16, waiting for transfers between devices, swap_x(): return lax.ppermute(values, 'fsdp', [(0, 1), (1, 0), (2, 3), (3, 2)])  31.5 us
    unnamed x175, local copies, waits for them, and re-layouts  22.2 us
    ppermute x16, starting transfers between devices, swap_x(): return lax.ppermute(values, 'fsdp', [(0, 1), (1, 0), (2, 3), (3, 2)])  19.5 us
  transfers between devices with their start and end apart: 39, of which 16 were waited for; matrix products, arithmetic and copies ran while one was open for 29% of the time, Pallas kernels for 17%

profile of v5, /device:TPU:0, one launch (start us, length us, event | category | flops | bytes accessed | tf_op | source)
XLA Modules:
  0.0 789.5 jit_solution(1094969530944868760)
XLA Ops:
  7.3 2.5 copy.78
  12.6 85.2 %opening.1 = (f32[8,2048]{1,0:T(8,128)}, f32[8,8,128]{2,1,0:T(8,128)}, bf16[4,128,2048]{2,1,0:T(8,128)(2,1)}, bf16[3,8,256,512]{3,2,1,0:T(8,128)(2,1)}, bf16[1,8...) custom-call(bf16[128,2048]{1,0:T(8,128)(2,1)} %bitcast.193, f32[8,128]{1,0:T(8,128)} %copy-done.49, ...), custom_call_target="tpu_custom_call" | custom-call | tf_op jit(solution)/shard_map/opening/pallas_call | solution.py:365
  102.4 6.7 convolution_bitcast_fusion
  124.3 7.6 collective-permute-done.2
  135.9 9.6 %collective-permute-done.3 = bf16[128,2048]{1,0:T(8,128)(2,1)S(1)} collective-permute-done((bf16[128,2048]{1,0:T(8,128)(2,1)S(1)}, bf16[128,2048]{1,0:T(8,128)(2,1)S(1)}, u32[]{:S(2)}, u32[]{:S(2)}) %collective-permute-start.3) | collective-permute-done | bytes 524320 | tf_op jit(solution)/shard_map/ppermute | solution.py:50
  147.7 48.5 %spread3.1 = (bf16[8,128,2048]{2,1,0:T(8,128)(2,1)}, bf16[4,128,2048]{2,1,0:T(8,128)(2,1)}) custom-call(bf16[128,2048]{1,0:T(8,128)(2,1)} %multiply_convert_fusion.9.block_ref.tokens_ref, bf16[128,2048]{1,0:T(8,128)(2,1)} %multiply_convert_fusion.9.block_ref.tokens_ref), custom_call_target="tpu_custom_call" | custom-call | bytes 120000000 | tf_op jit(solution)/shard_map/spread3/pallas_call | solution.py:611
  197.7 1.9 collective-permute-start.4
  208.2 8.7 %fusion.72 = f32[768,1408]{1,0:T(8,128)S(1)} fusion(bf16[768,2048]{1,0:T(8,128)(2,1)S(1)} %bitcast.201, bf16[2048,1408]{1,0:T(8,128)(2,1)} %bitcast.250), kind=kOutput, calls=%fused_computation.220 | convolution fusion | flops 4429185024 | bytes 13238272 | tf_op jit(solution)/shard_map/rd,df->rf/dot_general | solution.py:42
  219.3 13.2 %collective-permute-done.4 = bf16[512,1408]{1,0:T(8,128)(2,1)} collective-permute-done((bf16[512,1408]{1,0:T(8,128)(2,1)}, bf16[512,1408]{1,0:T(8,128)(2,1)}, u32[]{:S(2)}, u32[]{:S(2)}) %collective-permute-start.4) | collective-permute-done | bytes 1441824 | tf_op jit(solution)/shard_map/ppermute | solution.py:46
  237.7 39.0 %collective-permute-done.6 = bf16[256,1408]{1,0:T(8,128)(2,1)S(1)} collective-permute-done((bf16[256,1408]{1,0:T(8,128)(2,1)S(1)}, bf16[256,1408]{1,0:T(8,128)(2,1)S(1)}, u32[]{:S(2)}, u32[]{:S(2)}) %collective-permute-start.6) | collective-permute-done | bytes 720928 | tf_op jit(solution)/shard_map/ppermute | solution.py:50
  278.7 6.8 multiply_convert_fusion.3
  287.8 8.1 %collective-permute-done.10 = bf16[176,2048]{1,0:T(8,128)(2,1)S(1)} collective-permute-done((bf16[176,2048]{1,0:T(8,128)(2,1)S(1)}, bf16[176,2048]{1,0:T(8,128)(2,1)S(1)}, u32[]{:S(2)}, u32[]{:S(2)}) %collective-permute-start.10) | collective-permute-done | bytes 720928 | tf_op jit(solution)/shard_map/ppermute | solution.py:50
  295.9 7.1 collective-permute-done.11
  303.1 5.4 multiply_convert_fusion
  308.5 3.3 convolution_convert_fusion.7.terms_ref
  311.8 8.3 %fusion.3 = f32[512,1408]{1,0:T(8,128)} fusion(bf16[512,2048]{1,0:T(8,128)(2,1)} %bitcast.258, bf16[1,2048,1408]{2,1,0:T(8,128)(2,1)} %all-gather.9.cloned.1.call-done), kind=kOutput, calls=%fused_computation.13 | convolution fusion | flops 2952790016 | bytes 10747904 | tf_op jit(solution)/shard_map/td,df->tf/dot_general | solution.py:42
  320.2 9.1 %multiply_convert_fusion.7 = (bf16[512,1408]{1,0:T(8,128)(2,1)S(1)}, f32[512,1408]{1,0:T(8,128)}) fusion(f32[512,1408]{1,0:T(8,128)} %fusion.3, bf16[512,2048]{1,0:T(8,128)(2,1)} %bitcast.259, bf16[2048,1408]{1,0:T(8,128)(2,1)} %all-gather.5.cloned.1.call-done), kind=kOutput, calls=%fused_computation.40 | convolution fusion | flops 2957115392 | bytes 15073280 | tf_op jit(solution)/shard_map/td,df->tf/dot_general | solution.py:42
  329.3 7.8 convolution_convert_fusion.10
  337.1 44.1 %combine4.1 = (f32[128,2048]{1,0:T(8,128)}, f32[128,2048]{1,0:T(8,128)}) custom-call(bf16[8,128,2048]{2,1,0:T(8,128)(2,1)} %convolution_convert_fusion.7.terms_ref, bf16[4,128,2048]{2,1,0:T(8,128)(2,1)} %bitcast.209), custom_call_target="tpu_custom_call" | custom-call | bytes 120000000 | tf_op jit(solution)/shard_map/combine4/pallas_call | solution.py:779
  381.2 2.0 multiply_reduce_fusion.3
  384.3 48.1 %spread5.1 = (bf16[8,128,2048]{2,1,0:T(8,128)(2,1)}, bf16[4,128,2048]{2,1,0:T(8,128)(2,1)}) custom-call(bf16[128,2048]{1,0:T(8,128)(2,1)} %get-tuple-element.217.block_ref, bf16[128,2048]{1,0:T(8,128)(2,1)} %get-tuple-element.216.tokens_ref), custom_call_target="tpu_custom_call" | custom-call | bytes 120000000 | tf_op jit(solution)/shard_map/spread5/pallas_call | solution.py:611
  432.5 7.9 convolution_convert_fusion.5
  440.5 3.4 fusion.41
  444.3 5.3 convolution_convert_fusion.4
  454.3 9.5 %multiply_convert_fusion.1 = (bf16[768,1408]{1,0:T(8,128)(2,1)}, bf16[768,1408]{1,0:T(8,128)(2,1)}) fusion(f32[768,1408]{1,0:T(8,128)S(1)} %bitcast.265, f32[768,1408]{1,0:T(8,128)} %get-tuple-element.255, bf16[768,2048]{1,0:T(8,128)(2,1)S(1)} %fusion, bf16[1408,2048]{1,0:T(8,128)(2,1)S(1)} %bitcast.197), kind=kOutput, calls=%fused_computation.15 | convolution fusion | flops 4443242496 | bytes 21889024 | tf_op jit(solution)/shard_map/rd,fd->rf/dot_general | solution.py:42
  463.7 7.0 convolution_convert_fusion.1
  472.4 2.1 copy-done.7
  475.4 1.9 collective-permute-start.15
  477.4 7.9 %fusion.73 = f32[768,2048]{1,0:T(8,128)S(1)} fusion(bf16[768,1408]{1,0:T(8,128)(2,1)S(1)} %copy-done.71, bf16[2048,1408]{1,0:T(8,128)(2,1)} %bitcast.251), kind=kOutput, calls=%fused_computation.221 | convolution fusion | flops 4429185024 | bytes 14221312 | tf_op jit(solution)/shard_map/rf,df->rd/dot_general | solution.py:42
  485.4 5.2 multiply_convert_fusion.5
  490.6 9.0 %add_convert_fusion = bf16[768,2048]{1,0:T(8,128)(2,1)} fusion(f32[768,2048]{1,0:T(8,128)S(1)} %fusion.73, bf16[768,1408]{1,0:T(8,128)(2,1)} %get-tuple-element.110, bf16[2048,1408]{1,0:T(8,128)(2,1)S(1)} %bitcast.195), kind=kOutput, calls=%fused_computation.9 | convolution fusion | flops 4432330752 | bytes 17367040 | tf_op jit(solution)/shard_map/rf,df->rd/dot_general | solution.py:42
  499.6 5.2 convolution_convert_fusion.2
  504.8 7.9 %convolution_convert_fusion.3 = bf16[2048,1408]{1,0:T(8,128)(2,1)} fusion(bf16[512,2048]{1,0:T(8,128)(2,1)} %bitcast.260, bf16[512,1408]{1,0:T(8,128)(2,1)} %get-tuple-element.198), kind=kOutput, calls=%fused_computation.3 | convolution fusion | flops 2955673600 | bytes 9306112 | tf_op jit(solution)/shard_map/td,tf->df/dot_general | solution.py:42
  512.7 5.3 convolution_convert_fusion.6.terms_ref
  518.1 2.3 add_convert_fusion.6
  520.5 2.6 pad_maximum_fusion.1
  525.1 2.2 add_convert_fusion.4
  531.0 1.9 collective-permute-start.19
  532.9 3.4 fusion.74
  536.3 5.1 add_convert_fusion.1
  541.4 75.0 %combine6.1 = (f32[128,2048]{1,0:T(8,128)}, f32[128,2048]{1,0:T(8,128)}) custom-call(bf16[8,128,2048]{2,1,0:T(8,128)(2,1)} %convolution_convert_fusion.6.terms_ref, bf16[4,128,2048]{2,1,0:T(8,128)(2,1)} %bitcast.208), custom_call_target="tpu_custom_call" | custom-call | bytes 120000000 | tf_op jit(solution)/shard_map/combine6/pallas_call | solution.py:779
  617.6 2.7 multiply_reduce_fusion.1
  622.2 2.1 collective-permute-start.20
  624.3 6.9 convolution_convert_fusion
  637.5 3.2 collective-permute-done.22
  642.1 3.2 constant_dynamic-slice_fusion.6
  645.3 2.4 collective-permute-start.24
  648.4 2.9 fusion.10
  651.4 4.0 pad.8
  655.4 2.9 convolution_convert_fusion.11
  658.5 3.4 multiply_reduce_fusion
  669.0 5.5 bitcast_dynamic-update-slice_fusion
  674.6 8.9 %reduce-scatter.9.cloned.1.call-done = bf16[256,1408]{1,0:T(8,128)(2,1)} async-done(((bf16[2048,1408]{1,0:T(8,128)(2,1)}), bf16[256,1408]{1,0:T(8,128)(2,1)}) %reduce-scatter.9.cloned.1.call-update) | async-done | bytes 720912 | tf_op jit(solution)/shard_map/reduce_scatter | solution.py:982
  684.8 4.3 add_bitcast_fusion.1
  689.1 7.3 bitcast_convert_fusion
  699.5 2.2 add_convert_fusion.2
  704.9 2.4 collective-permute-done.26
  709.6 4.6 add_bitcast_fusion.2
  714.2 32.3 %collective-permute-done.29 = bf16[128,2048]{1,0:T(8,128)(2,1)S(1)} collective-permute-done((bf16[128,2048]{1,0:T(8,128)(2,1)S(1)}, bf16[128,2048]{1,0:T(8,128)(2,1)S(1)}, u32[]{:S(2)}, u32[]{:S(2)}) %collective-permute-start.29) | collective-permute-done | bytes 524320 | tf_op jit(solution)/shard_map/ppermute | solution.py:50
  748.0 11.9 %collect.1 = f32[8,128]{1,0:T(8,128)} custom-call(f32[32,8,128]{2,1,0:T(8,128)} %pad.9.terms_ref), custom_call_target="tpu_custom_call" | custom-call | tf_op jit(solution)/shard_map/collect/pallas_call | solution.py:436
  761.2 4.5 add_bitcast_fusion
  765.7 2.4 maximum_convert_fusion
  768.1 7.8 reduce-scatter.11.cloned.1.call-done
  779.8 2.7 copy.63
  (345 shorter events, 94.5 us)
Async XLA Ops:
  7.2 90.6 %copy-start.23 = (bf16[256,3,1408]{2,0,1:T(8,128)(2,1)S(1)}, bf16[256,3,1408]{2,0,1:T(8,128)(2,1)}, u32[]{:S(2)}) copy-start(bf16[256,3,1408]{2,0,1:T(8,128)(2,1)} %param.21) | copy-start | bytes 6488068
  7.2 304.7 %all-gather.9.cloned.1.call-start = ((), (), s32[]{:S(2)}) async-start(), calls=%async_computation.10 | async-start | bytes 6488064 | tf_op jit(solution)/shard_map/all_gather | solution.py:854
  99.2 221.0 %all-gather.5.cloned.1.call-start = ((), (), s32[]{:S(2)}) async-start(), calls=%async_computation.4 | async-start | bytes 6488064 | tf_op jit(solution)/shard_map/all_gather | solution.py:918
  123.1 22.6 %copy-start.4 = (bf16[1,128,2048]{2,1,0:T(8,128)(2,1)S(1)}, bf16[1,128,2048]{2,1,0:T(8,128)(2,1)}, u32[]{:S(2)}) copy-start(bf16[1,128,2048]{2,1,0:T(8,128)(2,1)} %param.13) | copy-start | bytes 1572868
  123.2 8.7 %collective-permute-start.2 = (bf16[64,2048]{1,0:T(8,128)(2,1)S(1)}, bf16[64,2048]{1,0:T(8,128)(2,1)S(1)}, u32[]{:S(2)}, u32[]{:S(2)}) collective-permute-start(bf16[64,2048]{1,0:T(8,128)(2,1)S(1)} %get-tuple-element.214), channel_id=1, source_target_pairs={{0,8},{8,0},{16,24},{24,16},{1,9},{9,1},{17,25},{25,17},{2,10},{10... | collective-permute-start | bytes 786440 | tf_op jit(solution)/shard_map/ppermute | solution.py:46
  123.7 8.3 %collective-permute-start = (bf16[64,2048]{1,0:T(8,128)(2,1)S(1)}, bf16[64,2048]{1,0:T(8,128)(2,1)S(1)}, u32[]{:S(2)}, u32[]{:S(2)}) collective-permute-start(bf16[64,2048]{1,0:T(8,128)(2,1)S(1)} %get-tuple-element.215), channel_id=1, source_target_pairs={{0,16},{16,0},{8,24},{24,8},{1,17},{17,1},{9,25},{25,9},{2,18},{18... | collective-permute-start | bytes 786440 | tf_op jit(solution)/shard_map/ppermute | solution.py:50
  132.1 13.4 %collective-permute-start.3 = (bf16[128,2048]{1,0:T(8,128)(2,1)S(1)}, bf16[128,2048]{1,0:T(8,128)(2,1)S(1)}, u32[]{:S(2)}, u32[]{:S(2)}) collective-permute-start(bf16[128,2048]{1,0:T(8,128)(2,1)S(1)} %pad_maximum_fusion.8), channel_id=1, source_target_pairs={{0,16},{16,0},{8,24},{24,8},{1,17},{17,1},{9,25},{25,9},{2,18},{18... | collective-permute-start | bytes 1572872 | tf_op jit(solution)/shard_map/ppermute | solution.py:50
  132.8 12.9 %collective-permute-start.1 = (bf16[128,2048]{1,0:T(8,128)(2,1)S(1)}, bf16[128,2048]{1,0:T(8,128)(2,1)S(1)}, u32[]{:S(2)}, u32[]{:S(2)}) collective-permute-start(bf16[128,2048]{1,0:T(8,128)(2,1)S(1)} %pad_maximum_fusion.7), channel_id=1, source_target_pairs={{0,8},{8,0},{16,24},{24,16},{1,9},{9,1},{17,25},{25,17},{2,10},{10... | collective-permute-start | bytes 1572872 | tf_op jit(solution)/shard_map/ppermute | solution.py:46
  135.9 10.8 %copy-start.37 = (f32[1,2048]{1,0:T(1,128)}, f32[1,2048]{1,0:T(1,128)S(1)}, u32[]{:S(2)}) copy-start(f32[1,2048]{1,0:T(1,128)S(1)} %get-tuple-element.240) | copy-start | bytes 24580
  135.9 81.9 %copy-start.42 = (f32[1,2048]{1,0:T(1,128)}, f32[1,2048]{1,0:T(1,128)S(1)}, u32[]{:S(2)}) copy-start(f32[1,2048]{1,0:T(1,128)S(1)} %get-tuple-element.239) | copy-start | bytes 24580
  146.7 55.5 %copy-start.50 = (f32[128]{0:T(128)}, f32[128]{0:T(128)S(1)}, u32[]{:S(2)}) copy-start(f32[128]{0:T(128)S(1)} %add_rsqrt_fusion.1) | copy-start | bytes 1540
  196.2 133.1 %all-gather.7.cloned.1.call-start = ((), (), s32[]{:S(2)}) async-start(), calls=%async_computation.5 | async-start | bytes 6488064 | tf_op jit(solution)/shard_map/all_gather | solution.py:919
  196.2 38.1 %collective-permute-start.5 = (bf16[512,1408]{1,0:T(8,128)(2,1)}, bf16[512,1408]{1,0:T(8,128)(2,1)S(1)}, u32[]{:S(2)}, u32[]{:S(2)}) collective-permute-start(bf16[512,1408]{1,0:T(8,128)(2,1)} %bitcast.218), channel_id=1, source_target_pairs={{0,16},{16,0},{8,24},{24,8},{1,17},{17,1},{9,25},{25,9},{2,18},{18... | collective-permute-start | bytes 4325384 | tf_op jit(solution)/shard_map/ppermute | solution.py:50
  197.7 34.8 %collective-permute-start.4 = (bf16[512,1408]{1,0:T(8,128)(2,1)}, bf16[512,1408]{1,0:T(8,128)(2,1)}, u32[]{:S(2)}, u32[]{:S(2)}) collective-permute-start(bf16[512,1408]{1,0:T(8,128)(2,1)} %bitcast.219), channel_id=1, source_target_pairs={{0,8},{8,0},{16,24},{24,16},{1,9},{9,1},{17,25},{25,17},{2,10},{10... | collective-permute-start | bytes 4325384 | tf_op jit(solution)/shard_map/ppermute | solution.py:46
  199.6 416.8 %reduce-scatter.5.cloned.1.call-start = ((), (), s32[]{:S(2)}) async-start(), calls=%async_computation.6 | async-start | bytes 6488064 | tf_op jit(solution)/shard_map/reduce_scatter | solution.py:982
  206.3 79.2 %collective-permute-start.9 = (bf16[352,2048]{1,0:T(8,128)(2,1)S(1)}, bf16[352,2048]{1,0:T(8,128)(2,1)S(1)}, u32[]{:S(2)}, u32[]{:S(2)}) collective-permute-start(bf16[352,2048]{1,0:T(8,128)(2,1)S(1)} %bitcast.221), channel_id=1, source_target_pairs={{0,16},{16,0},{8,24},{24,8},{1,17},{17,1},{9,25},{25,9},{2,18},{18... | collective-permute-start | bytes 4325384 | tf_op jit(solution)/shard_map/ppermute | solution.py:50
  206.8 71.3 %collective-permute-start.8 = (bf16[352,2048]{1,0:T(8,128)(2,1)S(1)}, bf16[352,2048]{1,0:T(8,128)(2,1)S(1)}, u32[]{:S(2)}, u32[]{:S(2)}) collective-permute-start(bf16[352,2048]{1,0:T(8,128)(2,1)S(1)} %bitcast.222), channel_id=1, source_target_pairs={{0,8},{8,0},{16,24},{24,16},{1,9},{9,1},{17,25},{25,17},{2,10},{10... | collective-permute-start | bytes 4325384 | tf_op jit(solution)/shard_map/ppermute | solution.py:46
  208.2 70.5 %copy-start.17 = (bf16[8,96,2048]{2,1,0:T(8,128)(2,1)}, bf16[8,96,2048]{2,1,0:T(8,128)(2,1)S(1)}, u32[]{:S(2)}) copy-start(bf16[8,96,2048]{2,1,0:T(8,128)(2,1)S(1)} %convolution_convert_fusion.8) | copy-start | bytes 9437188
  216.9 61.8 %copy-start.67 = (f32[768,1408]{1,0:T(8,128)}, f32[768,1408]{1,0:T(8,128)S(1)}, u32[]{:S(2)}) copy-start(f32[768,1408]{1,0:T(8,128)S(1)} %fusion.72) | copy-start | bytes 12976132
  219.3 18.2 %copy-start.56 = (f32[128]{0:T(128)}, f32[128]{0:T(128)S(1)}, u32[]{:S(2)}) copy-start(f32[128]{0:T(128)S(1)} %fusion.22) | copy-start | bytes 1540
  233.7 43.1 %collective-permute-start.6 = (bf16[256,1408]{1,0:T(8,128)(2,1)S(1)}, bf16[256,1408]{1,0:T(8,128)(2,1)S(1)}, u32[]{:S(2)}, u32[]{:S(2)}) collective-permute-start(bf16[256,1408]{1,0:T(8,128)(2,1)S(1)} %slice.271), channel_id=1, source_target_pairs={{0,16},{16,0},{8,24},{24,8},{1,17},{17,1},{9,25},{25,9},{2,18},{18... | collective-permute-start | bytes 2162696 | tf_op jit(solution)/shard_map/ppermute | solution.py:50
  234.4 43.6 %collective-permute-start.7 = (bf16[256,1408]{1,0:T(8,128)(2,1)S(1)}, bf16[256,1408]{1,0:T(8,128)(2,1)S(1)}, u32[]{:S(2)}, u32[]{:S(2)}) collective-permute-start(bf16[256,1408]{1,0:T(8,128)(2,1)S(1)} %slice.272), channel_id=1, source_target_pairs={{0,8},{8,0},{16,24},{24,16},{1,9},{9,1},{17,25},{25,17},{2,10},{10... | collective-permute-start | bytes 2162696 | tf_op jit(solution)/shard_map/ppermute | solution.py:46
  278.2 17.6 %collective-permute-start.10 = (bf16[176,2048]{1,0:T(8,128)(2,1)S(1)}, bf16[176,2048]{1,0:T(8,128)(2,1)S(1)}, u32[]{:S(2)}, u32[]{:S(2)}) collective-permute-start(bf16[176,2048]{1,0:T(8,128)(2,1)S(1)} %slice.273), channel_id=1, source_target_pairs={{0,16},{16,0},{8,24},{24,8},{1,17},{17,1},{9,25},{25,9},{2,18},{18... | collective-permute-start | bytes 2162696 | tf_op jit(solution)/shard_map/ppermute | solution.py:50
  285.5 17.6 %copy-start.69 = (bf16[768,1408]{1,0:T(8,128)(2,1)}, bf16[768,1408]{1,0:T(8,128)(2,1)S(1)}, u32[]{:S(2)}) copy-start(bf16[768,1408]{1,0:T(8,128)(2,1)S(1)} %get-tuple-element.254) | copy-start | bytes 6488068
  285.6 17.4 %collective-permute-start.11 = (bf16[176,2048]{1,0:T(8,128)(2,1)S(1)}, bf16[176,2048]{1,0:T(8,128)(2,1)S(1)}, u32[]{:S(2)}, u32[]{:S(2)}) collective-permute-start(bf16[176,2048]{1,0:T(8,128)(2,1)S(1)} %slice.274), channel_id=1, source_target_pairs={{0,8},{8,0},{16,24},{24,16},{1,9},{9,1},{17,25},{25,17},{2,10},{10... | collective-permute-start | bytes 2162696 | tf_op jit(solution)/shard_map/ppermute | solution.py:46
  337.1 44.1 %copy-start.10 = (bf16[1,128,2048]{2,1,0:T(8,128)(2,1)S(1)}, bf16[1,128,2048]{2,1,0:T(8,128)(2,1)}, u32[]{:S(2)}) copy-start(bf16[1,128,2048]{2,1,0:T(8,128)(2,1)} %param.14) | copy-start | bytes 1572868
  440.4 201.7 %reduce-scatter.7.cloned.1.call-start = ((), (), s32[]{:S(2)}) async-start(), calls=%async_computation.7 | async-start | bytes 6488064 | tf_op jit(solution)/shard_map/reduce_scatter | solution.py:982
  443.8 10.4 %slice-start.2 = ((s8[5767168]{0:T(1024)(128)(4,1)}), s8[4194304]{0:T(1024)(128)(4,1)S(1)}, s32[]{:S(2)}) async-start(s8[5767168]{0:T(1024)(128)(4,1)} %bitcast.196), calls=%async_computation.13 | async-start | bytes 8388608
  443.9 10.4 %slice-start.10 = ((s8[4325376]{0:T(1024)(128)(4,1)}), s8[4194304]{0:T(1024)(128)(4,1)S(1)}, s32[]{:S(2)}) async-start(s8[4325376]{0:T(1024)(128)(4,1)} %bitcast.264), calls=%async_computation.21 | async-start | bytes 8388608
  444.3 10.0 %slice-start.3 = ((s8[5767168]{0:T(1024)(128)(4,1)}), s8[1572864]{0:T(1024)(128)(4,1)S(1)}, s32[]{:S(2)}) async-start(s8[5767168]{0:T(1024)(128)(4,1)} %bitcast.196), calls=%async_computation.14 | async-start | bytes 3145728
  444.3 9.9 %slice-start.11 = ((s8[4325376]{0:T(1024)(128)(4,1)}), s8[131072]{0:T(1024)(128)(4,1)S(1)}, s32[]{:S(2)}) async-start(s8[4325376]{0:T(1024)(128)(4,1)} %bitcast.264), calls=%async_computation.22 | async-start | bytes 262144
  453.0 59.7 %collective-permute-start.12 = (bf16[176,2048]{1,0:T(8,128)(2,1)}, bf16[176,2048]{1,0:T(8,128)(2,1)}, u32[]{:S(2)}, u32[]{:S(2)}) collective-permute-start(bf16[176,2048]{1,0:T(8,128)(2,1)} %get-tuple-element.195), channel_id=1, source_target_pairs={{0,8},{8,0},{16,24},{24,16},{1,9},{9,1},{17,25},{25,17},{2,10},{10... | collective-permute-start | bytes 2162696 | tf_op jit(solution)/shard_map/ppermute | solution.py:46
  453.5 59.2 %collective-permute-start.13 = (bf16[176,2048]{1,0:T(8,128)(2,1)}, bf16[176,2048]{1,0:T(8,128)(2,1)}, u32[]{:S(2)}, u32[]{:S(2)}) collective-permute-start(bf16[176,2048]{1,0:T(8,128)(2,1)} %get-tuple-element.196), channel_id=1, source_target_pairs={{0,16},{16,0},{8,24},{24,8},{1,17},{17,1},{9,25},{25,9},{2,18},{18... | collective-permute-start | bytes 2162696 | tf_op jit(solution)/shard_map/ppermute | solution.py:50
  474.4 43.6 %collective-permute-start.14 = (bf16[256,1408]{1,0:T(8,128)(2,1)}, bf16[256,1408]{1,0:T(8,128)(2,1)}, u32[]{:S(2)}, u32[]{:S(2)}) collective-permute-start(bf16[256,1408]{1,0:T(8,128)(2,1)} %get-tuple-element.189), channel_id=1, source_target_pairs={{0,8},{8,0},{16,24},{24,16},{1,9},{9,1},{17,25},{25,17},{2,10},{10... | collective-permute-start | bytes 2162696 | tf_op jit(solution)/shard_map/ppermute | solution.py:46
  475.4 9.9 %slice-start.9 = ((s8[5767168]{0:T(1024)(128)(4,1)}), s8[1572864]{0:T(1024)(128)(4,1)S(1)}, s32[]{:S(2)}) async-start(s8[5767168]{0:T(1024)(128)(4,1)} %bitcast.254), calls=%async_computation.20 | async-start | bytes 3145728
  475.4 9.9 %copy-start.60 = (bf16[4,128,2048]{2,1,0:T(8,128)(2,1)S(1)}, bf16[4,128,2048]{2,1,0:T(8,128)(2,1)}, u32[]{:S(2)}) copy-start(bf16[4,128,2048]{2,1,0:T(8,128)(2,1)} %get-tuple-element.91) | copy-start | bytes 6291460
  475.4 9.9 %copy-start.65 = (f32[512,1408]{1,0:T(8,128)S(1)}, f32[512,1408]{1,0:T(8,128)}, u32[]{:S(2)}) copy-start(f32[512,1408]{1,0:T(8,128)} %fusion.3) | copy-start | bytes 8650756
  475.4 10.0 %copy-start.66 = (f32[512,1408]{1,0:T(8,128)S(1)}, f32[512,1408]{1,0:T(8,128)}, u32[]{:S(2)}) copy-start(f32[512,1408]{1,0:T(8,128)} %get-tuple-element.257) | copy-start | bytes 8650756
  475.4 42.6 %collective-permute-start.15 = (bf16[256,1408]{1,0:T(8,128)(2,1)}, bf16[256,1408]{1,0:T(8,128)(2,1)}, u32[]{:S(2)}, u32[]{:S(2)}) collective-permute-start(bf16[256,1408]{1,0:T(8,128)(2,1)} %get-tuple-element.190), channel_id=1, source_target_pairs={{0,16},{16,0},{8,24},{24,8},{1,17},{17,1},{9,25},{25,9},{2,18},{18... | collective-permute-start | bytes 2162696 | tf_op jit(solution)/shard_map/ppermute | solution.py:50
  477.4 13.2 %slice-start = ((s8[5767168]{0:T(1024)(128)(4,1)}), s8[4194304]{0:T(1024)(128)(4,1)S(1)}, s32[]{:S(2)}) async-start(s8[5767168]{0:T(1024)(128)(4,1)} %bitcast.194), calls=%async_computation.11 | async-start | bytes 8388608
  518.0 165.4 %reduce-scatter.9.cloned.1.call-start = ((), (), s32[]{:S(2)}) async-start(), calls=%async_computation.8 | async-start | bytes 6488064 | tf_op jit(solution)/shard_map/reduce_scatter | solution.py:982
  520.5 12.4 %slice-start.6 = ((s8[5767168]{0:T(1024)(128)(4,1)}), s8[4194304]{0:T(1024)(128)(4,1)S(1)}, s32[]{:S(2)}) async-start(s8[5767168]{0:T(1024)(128)(4,1)} %bitcast.252), calls=%async_computation.17 | async-start | bytes 8388608
  523.0 93.4 %collective-permute-start.16 = (bf16[352,2048]{1,0:T(8,128)(2,1)}, bf16[352,2048]{1,0:T(8,128)(2,1)}, u32[]{:S(2)}, u32[]{:S(2)}) collective-permute-start(bf16[352,2048]{1,0:T(8,128)(2,1)} %pad_maximum_fusion.1), channel_id=1, source_target_pairs={{0,8},{8,0},{16,24},{24,16},{1,9},{9,1},{17,25},{25,17},{2,10},{10... | collective-permute-start | bytes 4325384 | tf_op jit(solution)/shard_map/ppermute | solution.py:46
  524.6 91.8 %collective-permute-start.17 = (bf16[352,2048]{1,0:T(8,128)(2,1)}, bf16[352,2048]{1,0:T(8,128)(2,1)}, u32[]{:S(2)}, u32[]{:S(2)}) collective-permute-start(bf16[352,2048]{1,0:T(8,128)(2,1)} %pad_maximum_fusion.2), channel_id=1, source_target_pairs={{0,16},{16,0},{8,24},{24,8},{1,17},{17,1},{9,25},{25,9},{2,18},{18... | collective-permute-start | bytes 4325384 | tf_op jit(solution)/shard_map/ppermute | solution.py:50
  528.6 87.9 %collective-permute-start.18 = (bf16[512,1408]{1,0:T(8,128)(2,1)}, bf16[512,1408]{1,0:T(8,128)(2,1)}, u32[]{:S(2)}, u32[]{:S(2)}) collective-permute-start(bf16[512,1408]{1,0:T(8,128)(2,1)} %pad_maximum_fusion.3), channel_id=1, source_target_pairs={{0,8},{8,0},{16,24},{24,16},{1,9},{9,1},{17,25},{25,17},{2,10},{10... | collective-permute-start | bytes 4325384 | tf_op jit(solution)/shard_map/ppermute | solution.py:46
  531.0 85.4 %collective-permute-start.19 = (bf16[512,1408]{1,0:T(8,128)(2,1)}, bf16[512,1408]{1,0:T(8,128)(2,1)}, u32[]{:S(2)}, u32[]{:S(2)}) collective-permute-start(bf16[512,1408]{1,0:T(8,128)(2,1)} %pad_maximum_fusion.4), channel_id=1, source_target_pairs={{0,16},{16,0},{8,24},{24,8},{1,17},{17,1},{9,25},{25,9},{2,18},{18... | collective-permute-start | bytes 4325384 | tf_op jit(solution)/shard_map/ppermute | solution.py:50
  616.6 159.3 %reduce-scatter.11.cloned.1.call-start = ((), (), s32[]{:S(2)}) async-start(), calls=%async_computation.9 | async-start | bytes 9437184 | tf_op jit(solution)/shard_map/reduce_scatter | solution.py:1054
  621.8 10.2 %collective-permute-start.21 = (bf16[128,2048]{1,0:T(8,128)(2,1)S(1)}, bf16[128,2048]{1,0:T(8,128)(2,1)S(1)}, u32[]{:S(2)}, u32[]{:S(2)}) collective-permute-start(bf16[128,2048]{1,0:T(8,128)(2,1)S(1)} %get-tuple-element.108), channel_id=1, source_target_pairs={{0,16},{16,0},{8,24},{24,8},{1,17},{17,1},{9,25},{25,9},{2,18},{18... | collective-permute-start | bytes 1572872 | tf_op jit(solution)/shard_map/ppermute | solution.py:50
  622.2 12.1 %collective-permute-start.20 = (bf16[128,2048]{1,0:T(8,128)(2,1)S(1)}, bf16[128,2048]{1,0:T(8,128)(2,1)S(1)}, u32[]{:S(2)}, u32[]{:S(2)}) collective-permute-start(bf16[128,2048]{1,0:T(8,128)(2,1)S(1)} %get-tuple-element.108), channel_id=1, source_target_pairs={{0,8},{8,0},{16,24},{24,16},{1,9},{9,1},{17,25},{25,17},{2,10},{10... | collective-permute-start | bytes 1572872 | tf_op jit(solution)/shard_map/ppermute | solution.py:46
  632.0 9.4 %collective-permute-start.23 = (bf16[64,2048]{1,0:T(8,128)(2,1)S(1)}, bf16[64,2048]{1,0:T(8,128)(2,1)S(1)}, u32[]{:S(2)}, u32[]{:S(2)}) collective-permute-start(bf16[64,2048]{1,0:T(8,128)(2,1)S(1)} %slice.277), channel_id=1, source_target_pairs={{0,8},{8,0},{16,24},{24,16},{1,9},{9,1},{17,25},{25,17},{2,10},{10... | collective-permute-start | bytes 786440 | tf_op jit(solution)/shard_map/ppermute | solution.py:46
  634.3 6.4 collective-permute-start.22
  645.3 22.2 %collective-permute-start.24 = (bf16[256,1408]{1,0:T(8,128)(2,1)}, bf16[256,1408]{1,0:T(8,128)(2,1)}, u32[]{:S(2)}, u32[]{:S(2)}) collective-permute-start(bf16[256,1408]{1,0:T(8,128)(2,1)} %get-tuple-element.183), channel_id=1, source_target_pairs={{0,8},{8,0},{16,24},{24,16},{1,9},{9,1},{17,25},{25,17},{2,10},{10... | collective-permute-start | bytes 2162696 | tf_op jit(solution)/shard_map/ppermute | solution.py:46
  647.8 19.8 %collective-permute-start.25 = (bf16[256,1408]{1,0:T(8,128)(2,1)}, bf16[256,1408]{1,0:T(8,128)(2,1)}, u32[]{:S(2)}, u32[]{:S(2)}) collective-permute-start(bf16[256,1408]{1,0:T(8,128)(2,1)} %get-tuple-element.184), channel_id=1, source_target_pairs={{0,16},{16,0},{8,24},{24,8},{1,17},{17,1},{9,25},{25,9},{2,18},{18... | collective-permute-start | bytes 2162696 | tf_op jit(solution)/shard_map/ppermute | solution.py:50
  696.5 8.4 %collective-permute-start.28 = (bf16[64,2048]{1,0:T(8,128)(2,1)S(1)}, bf16[64,2048]{1,0:T(8,128)(2,1)S(1)}, u32[]{:S(2)}, u32[]{:S(2)}) collective-permute-start(bf16[64,2048]{1,0:T(8,128)(2,1)S(1)} %get-tuple-element.208), channel_id=1, source_target_pairs={{0,8},{8,0},{16,24},{24,16},{1,9},{9,1},{17,25},{25,17},{2,10},{10... | collective-permute-start | bytes 786440 | tf_op jit(solution)/shard_map/ppermute | solution.py:46
  698.0 9.2 %collective-permute-start.26 = (bf16[64,2048]{1,0:T(8,128)(2,1)S(1)}, bf16[64,2048]{1,0:T(8,128)(2,1)S(1)}, u32[]{:S(2)}, u32[]{:S(2)}) collective-permute-start(bf16[64,2048]{1,0:T(8,128)(2,1)S(1)} %get-tuple-element.209), channel_id=1, source_target_pairs={{0,16},{16,0},{8,24},{24,8},{1,17},{17,1},{9,25},{25,9},{2,18},{18... | collective-permute-start | bytes 786440 | tf_op jit(solution)/shard_map/ppermute | solution.py:50
  701.8 44.9 %collective-permute-start.30 = (bf16[512,1408]{1,0:T(8,128)(2,1)S(1)}, bf16[512,1408]{1,0:T(8,128)(2,1)}, u32[]{:S(2)}, u32[]{:S(2)}) collective-permute-start(bf16[512,1408]{1,0:T(8,128)(2,1)S(1)} %pad_maximum_fusion.5), channel_id=1, source_target_pairs={{0,8},{8,0},{16,24},{24,16},{1,9},{9,1},{17,25},{25,17},{2,10},{10... | collective-permute-start | bytes 4325384 | tf_op jit(solution)/shard_map/ppermute | solution.py:46
  702.5 44.2 %collective-permute-start.31 = (bf16[512,1408]{1,0:T(8,128)(2,1)S(1)}, bf16[512,1408]{1,0:T(8,128)(2,1)}, u32[]{:S(2)}, u32[]{:S(2)}) collective-permute-start(bf16[512,1408]{1,0:T(8,128)(2,1)S(1)} %pad_maximum_fusion.6), channel_id=1, source_target_pairs={{0,16},{16,0},{8,24},{24,8},{1,17},{17,1},{9,25},{25,9},{2,18},{18... | collective-permute-start | bytes 4325384 | tf_op jit(solution)/shard_map/ppermute | solution.py:50
  707.4 39.1 %collective-permute-start.29 = (bf16[128,2048]{1,0:T(8,128)(2,1)S(1)}, bf16[128,2048]{1,0:T(8,128)(2,1)S(1)}, u32[]{:S(2)}, u32[]{:S(2)}) collective-permute-start(bf16[128,2048]{1,0:T(8,128)(2,1)S(1)} %pad_maximum_fusion.10), channel_id=1, source_target_pairs={{0,16},{16,0},{8,24},{24,8},{1,17},{17,1},{9,25},{25,9},{2,18},{18... | collective-permute-start | bytes 1572872 | tf_op jit(solution)/shard_map/ppermute | solution.py:50
  709.0 37.7 %copy-start.41 = (f32[1,2048]{1,0:T(1,128)S(1)}, f32[1,2048]{1,0:T(1,128)}, u32[]{:S(2)}) copy-start(f32[1,2048]{1,0:T(1,128)} %get-tuple-element.238) | copy-start | bytes 24580
  709.0 37.7 %copy-start.52 = (f32[128]{0:T(128)S(1)}, f32[128]{0:T(128)}, u32[]{:S(2)}) copy-start(f32[128]{0:T(128)} %add_rsqrt_fusion) | copy-start | bytes 1540
  709.0 37.5 %collective-permute-start.27 = (bf16[128,2048]{1,0:T(8,128)(2,1)S(1)}, bf16[128,2048]{1,0:T(8,128)(2,1)S(1)}, u32[]{:S(2)}, u32[]{:S(2)}) collective-permute-start(bf16[128,2048]{1,0:T(8,128)(2,1)S(1)} %pad_maximum_fusion.9), channel_id=1, source_target_pairs={{0,8},{8,0},{16,24},{24,16},{1,9},{9,1},{17,25},{25,17},{2,10},{10... | collective-permute-start | bytes 1572872 | tf_op jit(solution)/shard_map/ppermute | solution.py:46
  714.2 32.5 %copy-start.5 = (bf16[1,128,2048]{2,1,0:T(8,128)(2,1)S(1)}, bf16[1,128,2048]{2,1,0:T(8,128)(2,1)}, u32[]{:S(2)}) copy-start(bf16[1,128,2048]{2,1,0:T(8,128)(2,1)} %param.13) | copy-start | bytes 1572868
  714.2 33.0 %copy-start.44 = (f32[1,32,64]{2,0,1:T(1,128)S(1)}, f32[1,32,64]{2,0,1:T(1,128)}, u32[]{:S(2)}) copy-start(f32[1,32,64]{2,0,1:T(1,128)} %stack.31) | copy-start | bytes 24580
  714.2 45.7 %copy-start.16 = (f32[128,2048]{1,0:T(8,128)S(1)}, f32[128,2048]{1,0:T(8,128)}, u32[]{:S(2)}) copy-start(f32[128,2048]{1,0:T(8,128)} %get-tuple-element.169) | copy-start | bytes 3145732
  (59 other events, 239.0 us)
Sparse Core Ops, SparseCore 0:
  99.3 60.8 all-gather.8
  196.3 58.9 all-gather.4
  257.5 59.0 all-gather.6
  440.5 62.9 reduce-scatter.4
  518.2 74.1 reduce-scatter.6
  616.7 66.7 reduce-scatter.8
  685.8 90.0 reduce-scatter.10
